TPU v7x, 32 devices: a whole 2x2x4 slice. The times are simulated.
32 devices in a mesh: seq: 16 (over z, y, x), head: 2 (over core).
Axes of the slice: x: 2, y: 2, z: 4, core: 2. Of those that a mesh axis runs over, the one named last changes fastest.
Arguments:
- win_query: bfloat16 [4096, 4096], P('seq', 'head'), may hold values from -24 to 24
- win_key: bfloat16 [4096, 4096], P('seq', 'head'), may hold values from -24 to 24
- win_value: bfloat16 [4096, 4096], P('seq', 'head'), may hold values from -24 to 24
- clu_query: bfloat16 [4096, 4096], P('seq', 'head'), may hold values from -24 to 24
- clu_key: bfloat16 [4096, 4096], P('seq', 'head'), may hold values from -24 to 24
- clu_value: bfloat16 [4096, 4096], P('seq', 'head'), may hold values from -24 to 24
- cluster_ids: int32 [32, 4096], P('head', 'seq'), may hold values from 0 to 63, as said below
- win_gain: float32 [4096], P('head'), may hold values from 0.5 to 1.5
- clu_gain: float32 [4096], P('head'), may hold values from 0.5 to 1.5
- win_out_grad: bfloat16 [4096, 4096], P('seq', 'head'), may hold values from -9 to 9
- clu_out_grad: bfloat16 [4096, 4096], P('seq', 'head'), may hold values from -9 to 9
Outputs:
- win_normed: bfloat16 [4096, 4096], P('seq', 'head')
- clu_normed: bfloat16 [4096, 4096], P('seq', 'head')
- win_dq: bfloat16 [4096, 4096], P('seq', 'head')
- win_dk: bfloat16 [4096, 4096], P('seq', 'head')
- win_dv: bfloat16 [4096, 4096], P('seq', 'head')
- clu_dq: bfloat16 [4096, 4096], P('seq', 'head')
- clu_dk: bfloat16 [4096, 4096], P('seq', 'head')
- clu_dv: bfloat16 [4096, 4096], P('seq', 'head')
Inputs may be any that keep to these rules, and one draw needn't show every extreme that they name: `cluster_ids`: in every cluster head each cluster holds at most 8 of the tokens of each aligned block of 256 positions, hence at most 128 tokens in all; in every head one cluster holds exactly 8 tokens of every block.
All inputs are finite; a program needn't handle non-finite values.
Results may differ from a plain program's by a relative error of at most 0.035.
Values may be sent and summed in bfloat16 or wider, within the bound.
A program may use at most 192 MiB of HBM per device.

v0:
```python
import jax
import jax.numpy as jnp
from jax import lax
from jax.sharding import PartitionSpec as P

HW = 32
HC = 32
DH = 128
WINDOW = 256
SLOTS = 128


EPSILON = 1e-06


def from_behind(block, axis, distance):
    devices = range(lax.axis_size(axis))
    route = [(i - distance, i) for i in devices if i - distance in devices]
    return lax.ppermute(block, axis, route)


def split_heads(values):
    return values.reshape(values.shape[0], values.shape[1] // DH, DH)


def five_dims(values):
    return values.reshape(
        values.shape[0], values.shape[1], values.shape[2], values.shape[3] // DH, DH
    )


def softmax_rows(scores, allowed):
    masked = jnp.where(allowed, scores, -jnp.inf)
    top_row = jnp.max(masked, axis=-1, keepdims=True)
    summed = jnp.sum(jnp.exp(masked - top_row), axis=-1, keepdims=True)
    return jnp.exp(masked - (top_row + jnp.log(summed)))


def owner_attend(queries, key_rows, val_rows, filled, factor):
    layout = queries.shape
    sources, n_items, n_cap, n_heads = (layout[0], layout[1], layout[2], layout[3])
    member_count = sources * n_cap
    scores = jnp.einsum(
        "scahd,tcbhd->hcsatb", queries, key_rows, preferred_element_type=jnp.float32
    )
    scores = scores.reshape(n_heads, n_items, member_count, member_count) * factor
    live_cols = filled.transpose(3, 1, 0, 2).reshape(n_heads, n_items, 1, member_count) > 0
    row_pos = lax.broadcasted_iota(jnp.int32, (member_count, member_count), 0)
    col_pos = lax.broadcasted_iota(jnp.int32, (member_count, member_count), 1)
    allowed = live_cols & (col_pos <= row_pos) | (col_pos == row_pos)
    attn_prob = softmax_rows(scores, allowed)
    weights = attn_prob.astype(jnp.bfloat16)
    six_dims = (n_heads, n_items, sources, n_cap, sources, n_cap)
    outputs = jnp.einsum(
        "hcsatb,tcbhd->scahd",
        weights.reshape(six_dims),
        val_rows,
        preferred_element_type=jnp.float32,
    ).astype(jnp.bfloat16)
    return (attn_prob, weights, outputs)


def owner_gradients(queries, key_rows, val_rows, attn_prob, weights, outputs, grad_rows, factor):
    layout = queries.shape
    sources, n_items, n_cap, n_heads = (layout[0], layout[1], layout[2], layout[3])
    member_count = sources * n_cap
    six_dims = (n_heads, n_items, sources, n_cap, sources, n_cap)
    flat_dims = (sources, n_items, n_cap, n_heads * DH)
    row_dot = jnp.sum(grad_rows.astype(jnp.float32) * outputs.astype(jnp.float32), axis=-1)
    row_dot = row_dot.transpose(3, 1, 0, 2).reshape(n_heads, n_items, member_count, 1)
    slope_rows = jnp.einsum(
        "scahd,tcbhd->hcsatb", grad_rows, val_rows, preferred_element_type=jnp.float32
    )
    slope_rows = slope_rows.reshape(n_heads, n_items, member_count, member_count)
    change = (attn_prob * (slope_rows - row_dot)).astype(jnp.bfloat16).reshape(six_dims)
    grad_q = jnp.einsum("hcsatb,tcbhd->scahd", change, key_rows, preferred_element_type=jnp.float32)
    grad_k = jnp.einsum("hcsatb,scahd->tcbhd", change, queries, preferred_element_type=jnp.float32)
    grad_v = jnp.einsum(
        "hcsatb,scahd->tcbhd",
        weights.reshape(six_dims),
        grad_rows,
        preferred_element_type=jnp.float32,
    )
    grad_q = (grad_q * factor).astype(jnp.bfloat16).reshape(flat_dims)
    grad_k = (grad_k * factor).astype(jnp.bfloat16).reshape(flat_dims)
    grad_v = grad_v.astype(jnp.bfloat16).reshape(flat_dims)
    return (grad_q, grad_k, grad_v)


def body(
    win_query,
    win_key,
    win_value,
    clu_query,
    clu_key,
    clu_value,
    cluster_ids,
    win_gain,
    clu_gain,
    win_out_grad,
    clu_out_grad,
):
    n_rows = win_query.shape[0]
    factor = DH ** (-0.5)
    feat_width = (HW + HC) * DH
    sources = lax.axis_size("seq")
    position = lax.axis_index("seq")
    n_cap = SLOTS // sources
    owned_count = 2 * n_rows // SLOTS
    pool_size = 2 * n_rows
    clu_heads = clu_query.shape[1] // DH
    rim_rows = jnp.stack([win_key, win_value])
    before = from_behind(rim_rows, "seq", 1)
    key_local = split_heads(jnp.concatenate([before[0], win_key], axis=0))
    val_local = split_heads(jnp.concatenate([before[1], win_value], axis=0))
    query_win = split_heads(win_query)
    row_pos = lax.broadcasted_iota(jnp.int32, (n_rows, n_rows + WINDOW), 0)
    col_pos = lax.broadcasted_iota(jnp.int32, (n_rows, n_rows + WINDOW), 1)
    gap_pos = row_pos + WINDOW - col_pos
    allowed = (gap_pos >= 0) & (gap_pos < WINDOW) & ((col_pos >= WINDOW) | (position > 0))
    scores = (
        jnp.einsum("ihd,jhd->hij", query_win, key_local, preferred_element_type=jnp.float32)
        * factor
    )
    prob_win = softmax_rows(scores, allowed)
    weight_win = prob_win.astype(jnp.bfloat16)
    attn_win = jnp.einsum(
        "hij,jhd->ihd", weight_win, val_local, preferred_element_type=jnp.float32
    ).astype(jnp.bfloat16)
    row_ids = lax.broadcasted_iota(jnp.int32, (n_rows, n_rows), 0)
    col_ids = lax.broadcasted_iota(jnp.int32, (n_rows, n_rows), 1)
    same_cluster = (cluster_ids[:, :, None] == cluster_ids[:, None, :]) & (col_ids < row_ids)
    rank_in = jnp.sum(same_cluster.astype(jnp.int32), axis=-1)
    slot_at = cluster_ids * n_cap + rank_in
    picker = (
        lax.broadcasted_iota(jnp.int32, (clu_heads, pool_size, n_rows), 1) == slot_at[:, None, :]
    ).astype(jnp.bfloat16)

    def dispatch(values):
        spread = jnp.einsum(
            "hpt,thd->phd", picker, split_heads(values), preferred_element_type=jnp.float32
        )
        return spread.astype(jnp.bfloat16).reshape(sources, owned_count, n_cap, clu_heads * DH)

    def collect(values):
        merged = jnp.einsum(
            "hpt,phd->thd",
            picker,
            values.reshape(pool_size, clu_heads, DH),
            preferred_element_type=jnp.float32,
        )
        return merged.astype(jnp.bfloat16).reshape(n_rows, clu_heads * DH)

    filled = jnp.sum(picker, axis=2).transpose(1, 0).reshape(sources, owned_count, n_cap, clu_heads)
    sent_query = dispatch(clu_query)
    sent_key = dispatch(clu_key)
    sent_value = dispatch(clu_value)
    queries = lax.all_to_all(sent_query, "seq", split_axis=0, concat_axis=0, tiled=True)
    key_rows = lax.all_to_all(sent_key, "seq", split_axis=0, concat_axis=0, tiled=True)
    val_rows = lax.all_to_all(sent_value, "seq", split_axis=0, concat_axis=0, tiled=True)
    live_rows = lax.all_to_all(filled, "seq", split_axis=0, concat_axis=0, tiled=True)
    q_five = five_dims(queries)
    k_five = five_dims(key_rows)
    v_five = five_dims(val_rows)
    attn_prob, weights, outputs = owner_attend(q_five, k_five, v_five, live_rows, factor)
    returned = lax.all_to_all(
        outputs.reshape(queries.shape), "seq", split_axis=0, concat_axis=0, tiled=True
    )
    result = (returned, q_five, k_five, v_five, attn_prob, weights, outputs)
    returned = result[0]
    attn_clu = collect(returned)
    flat_win = attn_win.reshape(n_rows, -1).astype(jnp.float32)
    flat_clu = attn_clu.astype(jnp.float32)
    sq_total = lax.psum(
        jnp.sum(flat_win * flat_win, axis=1) + jnp.sum(flat_clu * flat_clu, axis=1), "head"
    )
    inv_rms = 1.0 / jnp.sqrt(sq_total / feat_width + EPSILON)
    win_normed = (flat_win * inv_rms[:, None] * win_gain).astype(jnp.bfloat16)
    clu_normed = (flat_clu * inv_rms[:, None] * clu_gain).astype(jnp.bfloat16)
    grad_win = win_out_grad.astype(jnp.float32) * win_gain
    grad_clu = clu_out_grad.astype(jnp.float32) * clu_gain
    dot_total = lax.psum(
        jnp.sum(grad_win * flat_win, axis=1) + jnp.sum(grad_clu * flat_clu, axis=1), "head"
    )
    coef_rows = inv_rms**3 * dot_total / feat_width
    dout_win = (inv_rms[:, None] * grad_win - coef_rows[:, None] * flat_win).astype(jnp.bfloat16)
    dout_clu = (inv_rms[:, None] * grad_clu - coef_rows[:, None] * flat_clu).astype(jnp.bfloat16)
    dout_heads = split_heads(dout_win)
    row_dot_win = jnp.sum(dout_heads.astype(jnp.float32) * attn_win.astype(jnp.float32), axis=-1)
    slope_win = jnp.einsum(
        "ihd,jhd->hij", dout_heads, val_local, preferred_element_type=jnp.float32
    )
    change_win = (prob_win * (slope_win - row_dot_win.T[:, :, None])).astype(jnp.bfloat16)
    win_dq = jnp.einsum("hij,jhd->ihd", change_win, key_local, preferred_element_type=jnp.float32)
    win_dq = (win_dq * factor).astype(jnp.bfloat16).reshape(n_rows, -1)
    key_terms = jnp.einsum(
        "hij,ihd->jhd", change_win, query_win, preferred_element_type=jnp.float32
    )
    val_terms = jnp.einsum(
        "hij,ihd->jhd", weight_win, dout_heads, preferred_element_type=jnp.float32
    )
    rim_terms = jnp.stack([key_terms[:WINDOW], val_terms[:WINDOW]]).reshape(2, WINDOW, -1)
    after_rim = from_behind(rim_terms.astype(jnp.bfloat16), "seq", -1).astype(rim_terms.dtype)
    win_dk = key_terms[WINDOW:].reshape(n_rows, -1).at[n_rows - WINDOW :].add(after_rim[0])
    win_dk = (win_dk * factor).astype(jnp.bfloat16)
    win_dv = (
        val_terms[WINDOW:]
        .reshape(n_rows, -1)
        .at[n_rows - WINDOW :]
        .add(after_rim[1])
        .astype(jnp.bfloat16)
    )
    grad_sent = dispatch(dout_clu)
    grad_owned = lax.all_to_all(grad_sent, "seq", split_axis=0, concat_axis=0, tiled=True)
    grad_q, grad_k, grad_v = owner_gradients(
        result[1],
        result[2],
        result[3],
        result[4],
        result[5],
        result[6],
        five_dims(grad_owned),
        factor,
    )
    home_rows = (
        lax.all_to_all(grad_q, "seq", split_axis=0, concat_axis=0, tiled=True),
        lax.all_to_all(grad_k, "seq", split_axis=0, concat_axis=0, tiled=True),
        lax.all_to_all(grad_v, "seq", split_axis=0, concat_axis=0, tiled=True),
    )
    clu_dq = collect(home_rows[0])
    clu_dk = collect(home_rows[1])
    clu_dv = collect(home_rows[2])
    return (win_normed, clu_normed, win_dq, win_dk, win_dv, clu_dq, clu_dk, clu_dv)


def solution(mesh):
    return jax.shard_map(
        body,
        mesh=mesh,
        in_specs=(
            P("seq", "head"),
            P("seq", "head"),
            P("seq", "head"),
            P("seq", "head"),
            P("seq", "head"),
            P("seq", "head"),
            P("head", "seq"),
            P("head"),
            P("head"),
            P("seq", "head"),
            P("seq", "head"),
        ),
        out_specs=(
            P("seq", "head"),
            P("seq", "head"),
            P("seq", "head"),
            P("seq", "head"),
            P("seq", "head"),
            P("seq", "head"),
            P("seq", "head"),
            P("seq", "head"),
        ),
        check_vma=False,
    )
```

profile of v0, /device:TPU:14, one launch (start us, length us, event | category | flops | bytes accessed | tf_op | source)
XLA Modules:
  0.0 635.6 jit_solution(10428212256974955099)
XLA Ops:
  0.7 2.1 convert_reduce_fusion
  5.6 7.1 %all-to-all-start.1 = ((bf16[16,2,256]{2,1,0:T(2,128)(2,1)}), bf16[16,2,256]{2,1,0:T(2,128)(2,1)S(1)}, u32[]{:S(2)}, u32[]{:S(2)}) async-start(bf16[16,2,256]{2,1,0:T(2,128)(2,1)} %reshape.323), calls=%async_computation.1 | async-start | bytes 32768 | tf_op jit(solution)/shard_map/all_to_all | solution.py:161
  15.7 2.3 reshape.287
  18.0 7.0 %all-to-all-start.3 = ((bf16[16,4,8,2048]{3,2,1,0:T(8,128)(2,1)}), bf16[16,4,8,2048]{3,2,1,0:T(8,128)(2,1)S(1)}, u32[]{:S(2)}, u32[]{:S(2)}) async-start(bf16[16,4,8,2048]{3,2,1,0:T(8,128)(2,1)} %reshape.287), calls=%async_computation.3 | async-start | bytes 4194304 | tf_op jit(solution)/shard_map/all_to_all | solution.py:159
  26.6 2.7 copy.199
  29.3 4.2 reshape.284
  33.5 39.0 %all-to-all-done.3 = bf16[16,4,8,2048]{3,2,1,0:T(8,128)(2,1)S(1)} async-done(((bf16[16,4,8,2048]{3,2,1,0:T(8,128)(2,1)}), bf16[16,4,8,2048]{3,2,1,0:T(8,128)(2,1)S(1)}, u32[]{:S(2)}, u32[]{:S(2)}) %all-to-all-start.3) | async-done | bytes 2097184 | tf_op jit(solution)/shard_map/all_to_all | solution.py:159
  72.5 5.4 all-to-all-start.2
  79.5 2.7 copy.194
  82.2 4.2 reshape.280
  86.4 38.7 %all-to-all-done.2 = bf16[16,4,8,2048]{3,2,1,0:T(8,128)(2,1)} async-done(((bf16[16,4,8,2048]{3,2,1,0:T(8,128)(2,1)}), bf16[16,4,8,2048]{3,2,1,0:T(8,128)(2,1)}, u32[]{:S(2)}, u32[]{:S(2)}) %all-to-all-start.2) | async-done | bytes 2097184 | tf_op jit(solution)/shard_map/all_to_all | solution.py:158
  125.1 5.1 all-to-all-start
  131.7 2.3 copy.186
  134.0 2.7 pad_maximum_fusion
  136.7 3.4 collective-permute-start
  143.5 3.5 copy.291
  147.0 30.7 %all-to-all-done = bf16[16,4,8,2048]{3,2,1,0:T(8,128)(2,1)} async-done(((bf16[16,4,8,2048]{3,2,1,0:T(8,128)(2,1)}), bf16[16,4,8,2048]{3,2,1,0:T(8,128)(2,1)}, u32[]{:S(2)}, u32[]{:S(2)}) %all-to-all-start) | async-done | bytes 2097184 | tf_op jit(solution)/shard_map/all_to_all | solution.py:160
  177.7 2.2 copy.290
  180.0 21.8 %fusion.119 = (f32[16,4,16,8]{3,2,1,0:T(8,128)}, f32[16,4,16,8,16,8]{4,3,5,2,1,0:T(8,128)}) fusion(bf16[16,4,8,16,128,1]{4,3,2,1,0,5:T(8,128)(2,1)} %bitcast.229, bf16[16,4,8,16,128,1]{4,3,2,1,0,5:T(8,128)(2,1)} %bitcast.215, pred[16,8,16,8]{2,1,3,0:T(8,128)(4,1)S(1)} %copy-done.28, pred[16,8,16,8]{2,1,3,0:T(8,128)(4,1)S(1)} %get-tuple-element.92, ...), kind=kOutput, calls=%fused_computation.139 | convolution fusion | flops 273670144 | bytes 8462336 | tf_op jit(solution)/shard_map/scahd,tcbhd->hcsatb/dot_general | solution.py:43
  201.8 16.3 %exponential_reduce_fusion = f32[16,4,16,8]{3,2,1,0:T(8,128)S(1)} fusion(f32[16,4,16,8,16,8]{4,3,5,2,1,0:T(8,128)} %get-tuple-element.99, f32[16,4,16,8]{3,2,1,0:T(8,128)} %get-tuple-element.98), kind=kLoop, calls=%fused_computation.2 | loop fusion | flops 2088960 | bytes 4259840 | tf_op jit(solution)/shard_map/reduce_sum | solution.py:35
  218.2 4.2 copy-done.2
  222.3 8.6 %fusion = bf16[16,4,16,8,16,8]{4,3,5,2,1,0:T(8,128)(2,1)} fusion(f32[16,4,16,8,16,8]{4,3,5,2,1,0:T(8,128)S(1)} %copy-done.2, f32[16,4,16,8]{3,2,1,0:T(8,128)S(1)} %log_add_fusion), kind=kLoop, calls=%fused_computation.4 | loop fusion | flops 2097152 | bytes 6324224 | tf_op jit(solution)/shard_map/convert_element_type | solution.py:52
  230.9 20.6 %fusion.63 = bf16[16,4,8,16,128]{4,0,2,3,1:T(8,128)(2,1)S(1)} fusion(bf16[16,4,16,8,16,8]{4,3,5,2,1,0:T(8,128)(2,1)} %fusion, bf16[16,4,8,16,128,1]{4,3,2,1,0,5:T(8,128)(2,1)S(1)} %bitcast.209), kind=kOutput, calls=%fused_computation.92 | convolution fusion | flops 269484032 | bytes 6291456 | tf_op jit(solution)/shard_map/hcsatb,tcbhd->scahd/dot_general | solution.py:54
  254.2 2.3 reshape.289
  256.5 10.3 %all-to-all-start.4 = ((bf16[16,4,8,2048]{3,2,1,0:T(8,128)(2,1)}), bf16[16,4,8,2048]{3,2,1,0:T(8,128)(2,1)}, u32[]{:S(2)}, u32[]{:S(2)}) async-start(bf16[16,4,8,2048]{3,2,1,0:T(8,128)(2,1)} %reshape.289), calls=%async_computation.4 | async-start | bytes 4194304 | tf_op jit(solution)/shard_map/all_to_all | solution.py:166
  268.8 2.8 fusion.118
  272.9 2.5 fusion.19
  279.0 3.5 fusion.53
  284.4 27.7 %all-to-all-done.4 = bf16[16,4,8,2048]{3,2,1,0:T(8,128)(2,1)} async-done(((bf16[16,4,8,2048]{3,2,1,0:T(8,128)(2,1)}), bf16[16,4,8,2048]{3,2,1,0:T(8,128)(2,1)}, u32[]{:S(2)}, u32[]{:S(2)}) %all-to-all-start.4) | async-done | bytes 2097184 | tf_op jit(solution)/shard_map/all_to_all | solution.py:166
  312.1 2.2 copy.293
  314.3 3.4 multiply_reduce_fusion.3
  317.7 3.0 copy.209
  320.8 2.5 multiply_reduce_fusion.1
  323.3 2.5 all-reduce
  325.8 5.1 subtract_convert_fusion
  331.5 3.3 convert_bitcast_fusion
  334.8 3.4 copy.228
  338.2 2.3 reshape.298
  340.5 52.9 %all_to_all.45 = bf16[16,4,8,2048]{3,2,1,0:T(8,128)(2,1)S(1)} all-to-all(bf16[16,4,8,2048]{3,2,1,0:T(8,128)(2,1)} %reshape.298), channel_id=1, replica_groups=mesh['seq'=16,'head'=2] {'seq'}, dimensions={0} | all-to-all | bytes 4194304 | tf_op jit(solution)/shard_map/all_to_all | solution.py:214
  396.3 8.1 %fusion.73 = bf16[16,4,8,16,128]{4,0,2,3,1:T(8,128)(2,1)S(1)} fusion(bf16[16,4,16,8,16,8]{4,3,5,2,1,0:T(8,128)(2,1)} %fusion, bf16[16,4,8,16,128,1]{4,3,2,1,0,5:T(8,128)(2,1)S(1)} %bitcast.204), kind=kOutput, calls=%fused_computation.94 | convolution fusion | flops 269484032 | bytes 6291456 | tf_op jit(solution)/shard_map/hcsatb,scahd->tcbhd/dot_general | solution.py:78
  404.4 2.7 copy.243
  407.2 4.2 reshape.306
  411.3 6.8 %all-to-all-start.8 = ((bf16[16,4,8,2048]{3,2,1,0:T(8,128)(2,1)}), bf16[16,4,8,2048]{3,2,1,0:T(8,128)(2,1)}, u32[]{:S(2)}, u32[]{:S(2)}) async-start(bf16[16,4,8,2048]{3,2,1,0:T(8,128)(2,1)} %reshape.306), calls=%async_computation.8 | async-start | bytes 4194304 | tf_op jit(solution)/shard_map/all_to_all | solution.py:228
  418.4 29.2 %multiply_convert_fusion = bf16[16,4,16,8,16,8]{4,3,5,2,1,0:T(8,128)(2,1)} fusion(f32[16,4,16,8,16,8]{4,3,5,2,1,0:T(8,128)} %get-tuple-element.99, f32[16,4,16,8]{3,2,1,0:T(8,128)S(1)} %copy.232, f32[16,4,16,8]{3,2,1,0:T(8,128)S(1)} %copy-done.13, bf16[16,4,8,16,128,1]{4,3,2,1,0,5:T(8,128)(2,1)} %bitcast.210, bf16[16,4,8,16,128,1]{4,3,2,1,0,5:T(8,128)(2,1)S(1)} %bitcast.205), kind=kOutput, calls=%fused_computation | convolution fusion | flops 272629760 | bytes 10551296 | tf_op jit(solution)/shard_map/scahd,tcbhd->hcsatb/dot_general | solution.py:71
  447.6 8.1 %fusion.68 = bf16[16,4,8,16,128]{4,0,2,3,1:T(8,128)(2,1)S(1)} fusion(bf16[16,4,16,8,16,8]{4,3,5,2,1,0:T(8,128)(2,1)} %multiply_convert_fusion, bf16[16,4,8,16,128,1]{4,3,2,1,0,5:T(8,128)(2,1)S(1)} %bitcast.216), kind=kOutput, calls=%fused_computation.93 | convolution fusion | flops 270532608 | bytes 6291456 | tf_op jit(solution)/shard_map/hcsatb,scahd->tcbhd/dot_general | solution.py:77
  457.1 2.3 reshape.303
  459.4 5.6 all-to-all-done.8
  465.0 5.1 all-to-all-start.7
  472.3 7.8 %convolution_bitcast_fusion = f32[512,16,128]{0,2,1:T(8,128)} fusion(bf16[256,16,128]{0,2,1:T(8,128)(2,1)S(1)} %bitcast.213, f32[16,512,256]{2,1,0:T(8,128)} %copy-done.3, f32[16,256]{1,0:T(8,128)S(1)} %log_add_fusion.1, pred[256,512]{0,1:T(8,128)(4,1)S(1)} %fusion.104), kind=kOutput, calls=%fused_computation.46 | convolution fusion | flops 545259520 | bytes 13778944 | tf_op jit(solution)/shard_map/hij,ihd->jhd/dot_general | solution.py:199
  480.1 4.3 multiply_convert_fusion.1
  484.5 20.9 %fusion.58 = bf16[16,4,8,16,128]{4,0,2,3,1:T(8,128)(2,1)S(1)} fusion(bf16[16,4,16,8,16,8]{4,3,5,2,1,0:T(8,128)(2,1)} %multiply_convert_fusion, bf16[16,4,8,16,128,1]{4,3,2,1,0,5:T(8,128)(2,1)S(1)} %bitcast.230), kind=kOutput, calls=%fused_computation.91 | convolution fusion | flops 270532608 | bytes 6291456 | tf_op jit(solution)/shard_map/hcsatb,tcbhd->scahd/dot_general | solution.py:76
  506.8 2.4 reshape.300
  509.1 8.3 %all-to-all-done.7 = bf16[16,4,8,2048]{3,2,1,0:T(8,128)(2,1)} async-done(((bf16[16,4,8,2048]{3,2,1,0:T(8,128)(2,1)}), bf16[16,4,8,2048]{3,2,1,0:T(8,128)(2,1)}, u32[]{:S(2)}, u32[]{:S(2)}) %all-to-all-start.7) | async-done | bytes 2097184 | tf_op jit(solution)/shard_map/all_to_all | solution.py:227
  517.5 5.4 all-to-all-start.6
  522.9 3.7 convolution_bitcast_fusion.1
  533.3 2.7 collective-permute-start.1
  540.8 2.4 copy.245
  547.0 66.9 %collective-permute-done.1 = bf16[2,256,2048]{2,1,0:T(8,128)(2,1)} collective-permute-done((bf16[2,256,2048]{2,1,0:T(8,128)(2,1)}, bf16[2,256,2048]{2,1,0:T(8,128)(2,1)}, u32[]{:S(2)}, u32[]{:S(2)}) %collective-permute-start.1) | collective-permute-done | bytes 2097184 | tf_op jit(solution)/shard_map/ppermute | solution.py:19
  613.9 2.1 convert_element_type.197
  616.1 2.2 fusion.40
  618.3 2.2 copy.297
  624.0 2.2 copy.296
  626.2 2.1 fusion.87
  629.7 2.2 copy.295
  (132 shorter events, 57.6 us)
Async XLA Ops:
  0.6 12.1 %copy-start = (bf16[256,2048]{1,0:T(8,128)(2,1)S(1)}, bf16[256,2048]{1,0:T(8,128)(2,1)}, u32[]{:S(2)}) copy-start(bf16[256,2048]{1,0:T(8,128)(2,1)} %param.23) | copy-start | bytes 3145732
  3.6 328.0 %copy-start.29 = (s32[16,256]{1,0:T(8,128)}, s32[16,256]{1,0:T(8,128)S(1)}, u32[]{:S(2)}) copy-start(s32[16,256]{1,0:T(8,128)S(1)} %multiply_add_fusion) | copy-start | bytes 49156
  5.6 12.4 %all-to-all-start.1 = ((bf16[16,2,256]{2,1,0:T(2,128)(2,1)}), bf16[16,2,256]{2,1,0:T(2,128)(2,1)S(1)}, u32[]{:S(2)}, u32[]{:S(2)}) async-start(bf16[16,2,256]{2,1,0:T(2,128)(2,1)} %reshape.323), calls=%async_computation.1 | async-start | bytes 32768 | tf_op jit(solution)/shard_map/all_to_all | solution.py:161
  18.0 7.1 %copy-start.33 = (bf16[256,2048]{1,0:T(8,128)(2,1)S(1)}, bf16[256,2048]{1,0:T(8,128)(2,1)}, u32[]{:S(2)}) copy-start(bf16[256,2048]{1,0:T(8,128)(2,1)} %param.22) | copy-start | bytes 3145732
  18.0 54.5 %all-to-all-start.3 = ((bf16[16,4,8,2048]{3,2,1,0:T(8,128)(2,1)}), bf16[16,4,8,2048]{3,2,1,0:T(8,128)(2,1)S(1)}, u32[]{:S(2)}, u32[]{:S(2)}) async-start(bf16[16,4,8,2048]{3,2,1,0:T(8,128)(2,1)} %reshape.287), calls=%async_computation.3 | async-start | bytes 4194304 | tf_op jit(solution)/shard_map/all_to_all | solution.py:159
  33.5 44.4 %copy-start.34 = (bf16[256,2048]{1,0:T(8,128)(2,1)S(1)}, bf16[256,2048]{1,0:T(8,128)(2,1)}, u32[]{:S(2)}) copy-start(bf16[256,2048]{1,0:T(8,128)(2,1)} %param.24) | copy-start | bytes 3145732
  72.5 52.6 %all-to-all-start.2 = ((bf16[16,4,8,2048]{3,2,1,0:T(8,128)(2,1)}), bf16[16,4,8,2048]{3,2,1,0:T(8,128)(2,1)}, u32[]{:S(2)}, u32[]{:S(2)}) async-start(bf16[16,4,8,2048]{3,2,1,0:T(8,128)(2,1)} %reshape.284), calls=%async_computation.2 | async-start | bytes 4194304 | tf_op jit(solution)/shard_map/all_to_all | solution.py:158
  125.1 52.6 %all-to-all-start = ((bf16[16,4,8,2048]{3,2,1,0:T(8,128)(2,1)}), bf16[16,4,8,2048]{3,2,1,0:T(8,128)(2,1)}, u32[]{:S(2)}, u32[]{:S(2)}) async-start(bf16[16,4,8,2048]{3,2,1,0:T(8,128)(2,1)} %reshape.280), calls=%async_computation | async-start | bytes 4194304 | tf_op jit(solution)/shard_map/all_to_all | solution.py:160
  136.7 132.1 %collective-permute-start = (bf16[2,256,2048]{1,2,0:T(8,128)(2,1)}, bf16[2,256,2048]{1,2,0:T(8,128)(2,1)}, u32[]{:S(2)}, u32[]{:S(2)}) collective-permute-start(bf16[2,256,2048]{1,2,0:T(8,128)(2,1)} %pad_maximum_fusion), channel_id=1, source_target_pairs={{0,2},{2,4},{4,6},{6,8},{8,10},{10,12},{12,14},{14,16},{16,18},{18... | collective-permute-start | bytes 6291464 | tf_op jit(solution)/shard_map/ppermute | solution.py:19
  177.7 2.3 copy-start.28
  179.9 51.0 %copy-start.6 = (bf16[64,8,16,128]{3,2,1,0:T(8,128)(2,1)}, bf16[64,8,16,128]{3,2,1,0:T(8,128)(2,1)S(1)}, u32[]{:S(2)}) copy-start(bf16[64,8,16,128]{3,2,1,0:T(8,128)(2,1)S(1)} %copy.290) | copy-start | bytes 6291460
  201.8 16.3 %copy-start.20 = (f32[16,4,16,8]{3,2,1,0:T(8,128)S(1)}, f32[16,4,16,8]{3,2,1,0:T(8,128)}, u32[]{:S(2)}) copy-start(f32[16,4,16,8]{3,2,1,0:T(8,128)} %get-tuple-element.98) | copy-start | bytes 98308
  201.8 20.6 %copy-start.2 = (f32[16,4,16,8,16,8]{4,3,5,2,1,0:T(8,128)S(1)}, f32[16,4,16,8,16,8]{4,3,5,2,1,0:T(8,128)}, u32[]{:S(2)}) copy-start(f32[16,4,16,8,16,8]{4,3,5,2,1,0:T(8,128)} %get-tuple-element.99) | copy-start | bytes 12582916
  222.3 8.6 %copy-start.12 = (f32[16,4,16,8]{3,2,1,0:T(8,128)}, f32[16,4,16,8]{3,2,1,0:T(8,128)S(1)}, u32[]{:S(2)}) copy-start(f32[16,4,16,8]{3,2,1,0:T(8,128)S(1)} %log_add_fusion) | copy-start | bytes 98308
  251.5 1.4 copy-start.9
  256.5 55.6 %all-to-all-start.4 = ((bf16[16,4,8,2048]{3,2,1,0:T(8,128)(2,1)}), bf16[16,4,8,2048]{3,2,1,0:T(8,128)(2,1)}, u32[]{:S(2)}, u32[]{:S(2)}) async-start(bf16[16,4,8,2048]{3,2,1,0:T(8,128)(2,1)} %reshape.289), calls=%async_computation.4 | async-start | bytes 4194304 | tf_op jit(solution)/shard_map/all_to_all | solution.py:166
  266.8 1.2 copy-start.22
  268.1 4.9 copy-start.23
  268.6 4.3 copy-start.14
  275.4 3.5 copy-start.3
  275.4 3.5 copy-start.18
  275.5 3.5 copy-start.26
  317.7 3.0 copy-start.17
  317.7 3.0 copy-start.31
  317.7 3.0 copy-start.32
  393.4 1.6 copy-start.10
  411.3 7.1 %copy-start.13 = (f32[16,4,16,8]{3,2,1,0:T(8,128)S(1)}, f32[16,4,16,8]{3,2,1,0:T(8,128)}, u32[]{:S(2)}) copy-start(f32[16,4,16,8]{3,2,1,0:T(8,128)} %copy-done.12) | copy-start | bytes 98308
  411.3 53.7 %all-to-all-start.8 = ((bf16[16,4,8,2048]{3,2,1,0:T(8,128)(2,1)}), bf16[16,4,8,2048]{3,2,1,0:T(8,128)(2,1)}, u32[]{:S(2)}, u32[]{:S(2)}) async-start(bf16[16,4,8,2048]{3,2,1,0:T(8,128)(2,1)} %reshape.306), calls=%async_computation.8 | async-start | bytes 4194304 | tf_op jit(solution)/shard_map/all_to_all | solution.py:228
  418.4 29.2 %copy-start.7 = (bf16[64,8,16,128]{3,2,1,0:T(8,128)(2,1)S(1)}, bf16[64,8,16,128]{3,2,1,0:T(8,128)(2,1)}, u32[]{:S(2)}) copy-start(bf16[64,8,16,128]{3,2,1,0:T(8,128)(2,1)} %copy.291) | copy-start | bytes 6291460
  465.0 52.5 %all-to-all-start.7 = ((bf16[16,4,8,2048]{3,2,1,0:T(8,128)(2,1)}), bf16[16,4,8,2048]{3,2,1,0:T(8,128)(2,1)}, u32[]{:S(2)}, u32[]{:S(2)}) async-start(bf16[16,4,8,2048]{3,2,1,0:T(8,128)(2,1)} %reshape.303), calls=%async_computation.7 | async-start | bytes 4194304 | tf_op jit(solution)/shard_map/all_to_all | solution.py:227
  470.1 1.9 copy-start.11
  472.0 8.1 %slice-start = ((s8[8388608]{0:T(1024)(128)(4,1)}), s8[4194304]{0:T(1024)(128)(4,1)S(1)}, s32[]{:S(2)}) async-start(s8[8388608]{0:T(1024)(128)(4,1)} %bitcast.206), calls=%async_computation.9 | async-start | bytes 8388608
  472.3 7.8 %slice-start.1 = ((s8[8388608]{0:T(1024)(128)(4,1)}), s8[4194304]{0:T(1024)(128)(4,1)S(1)}, s32[]{:S(2)}) async-start(s8[8388608]{0:T(1024)(128)(4,1)} %bitcast.206), calls=%async_computation.10 | async-start | bytes 8388608
  472.3 7.8 %copy-start.19 = (bf16[256,2048]{0,1:T(8,128)(2,1)S(1)}, bf16[256,2048]{0,1:T(8,128)(2,1)}, u32[]{:S(2)}) copy-start(bf16[256,2048]{0,1:T(8,128)(2,1)} %copy.186) | copy-start | bytes 3145732
  472.3 7.8 %copy-start.27 = (bf16[1,256,2048]{1,2,0:T(8,128)(2,1)S(1)}, bf16[1,256,2048]{1,2,0:T(8,128)(2,1)}, u32[]{:S(2)}) copy-start(bf16[1,256,2048]{1,2,0:T(8,128)(2,1)} %get-tuple-element.91) | copy-start | bytes 3145732
  480.1 4.3 copy-start.21
  509.1 13.8 %copy-start.15 = (bf16[256,2048]{0,1:T(8,128)(2,1)S(1)}, bf16[256,2048]{0,1:T(8,128)(2,1)}, u32[]{:S(2)}) copy-start(bf16[256,2048]{0,1:T(8,128)(2,1)} %copy-done.14) | copy-start | bytes 3145732
  517.5 112.3 %all-to-all-start.6 = ((bf16[16,4,8,2048]{3,2,1,0:T(8,128)(2,1)}), bf16[16,4,8,2048]{3,2,1,0:T(8,128)(2,1)}, u32[]{:S(2)}, u32[]{:S(2)}) async-start(bf16[16,4,8,2048]{3,2,1,0:T(8,128)(2,1)} %reshape.300), calls=%async_computation.6 | async-start | bytes 4194304 | tf_op jit(solution)/shard_map/all_to_all | solution.py:226
  526.6 2.0 copy-start.4
  531.8 5.9 copy-start.24
  531.8 5.9 copy-start.25
  533.3 2.7 copy-start.5
  533.3 80.6 %collective-permute-start.1 = (bf16[2,256,2048]{2,1,0:T(8,128)(2,1)}, bf16[2,256,2048]{2,1,0:T(8,128)(2,1)}, u32[]{:S(2)}, u32[]{:S(2)}) collective-permute-start(bf16[2,256,2048]{2,1,0:T(8,128)(2,1)} %pad_maximum_fusion.3), channel_id=1, source_target_pairs={{2,0},{4,2},{6,4},{8,6},{10,8},{12,10},{14,12},{16,14},{18,16},{20... | collective-permute-start | bytes 6291464 | tf_op jit(solution)/shard_map/ppermute | solution.py:19
  536.1 2.9 copy-start.16
  540.8 2.4 slice-start.2
  547.0 69.0 %copy-start.8 = (f32[256,2048]{1,0:T(8,128)S(1)}, f32[256,2048]{1,0:T(8,128)}, u32[]{:S(2)}) copy-start(f32[256,2048]{1,0:T(8,128)} %copy.224) | copy-start | bytes 6291460
  618.3 2.2 copy-start.30
  631.9 3.5 copy-start.1
where the time goes:
time: 644 us; the launch traced here: 636 us
  waiting for transfers between devices  217 us (34%)
  matrix products  150 us (23%)
  local copies, waits for them, and re-layouts  104 us (16%)
  starting transfers between devices  58.5 us (9%)
  blocking collectives  55.3 us (9%)
  other arithmetic  49.6 us (8%)
    ppermute x2, waiting for transfers between devices, from_behind(): return lax.ppermute(block, axis, route)  66.9 us
    all_to_all x1, blocking collectives, body(): lax.all_to_all(grad_sent, 'seq', split_axis=0, concat_axis=0, tiled=True)  52.9 us
    unnamed x89, local copies, waits for them, and re-layouts  40.4 us
    all_to_all x1, waiting for transfers between devices, body(): lax.all_to_all(sent_key, 'seq', split_axis=0, concat_axis=0, tiled=True)  39 us
    all_to_all x1, waiting for transfers between devices, body(): lax.all_to_all(sent_query, 'seq', split_axis=0, concat_axis=0, tiled=True)  38.7 us
    all_to_all x1, waiting for transfers between devices, body(): lax.all_to_all(sent_value, 'seq', split_axis=0, concat_axis=0, tiled=True)  30.7 us
    dot_general x1, matrix products, owner_gradients(): jnp.einsum('scahd,tcbhd->hcsatb', grad_rows, val_rows, preferred_element_...  29.2 us
    all_to_all x1, waiting for transfers between devices, body(): lax.all_to_all(outputs.reshape(queries.shape), 'seq', split_axis=0, conca...  27.7 us
  transfers between devices with their start and end apart: 10, of which 7 were waited for; matrix products, arithmetic and copies ran while one was open for 37% of the time, Pallas kernels for 0%

commit v1 on v0

v1 whole, which is shorter than its diff:
```python
import functools

import jax
import jax.numpy as jnp
from jax import lax
from jax.experimental import pallas as pl
from jax.experimental.pallas import tpu as pltpu
from jax.sharding import PartitionSpec as P

HW = 32
HC = 32
DH = 128
WINDOW = 256
SLOTS = 128
CHUNKS = 2

EPSILON = 1e-06
F32 = jnp.float32
BF16 = jnp.bfloat16


def from_behind(block, axis, distance):
    devices = range(lax.axis_size(axis))
    route = [(i - distance, i) for i in devices if i - distance in devices]
    return lax.ppermute(block, axis, route)


def nt(a, b):
    return lax.dot_general(a, b, (((1,), (1,)), ((), ())), preferred_element_type=F32)


def tn(a, b):
    return lax.dot_general(a, b, (((0,), (0,)), ((), ())), preferred_element_type=F32)


def nn(a, b):
    return jnp.dot(a, b, preferred_element_type=F32)


def one_hot(slot_ref, pool):
    n = slot_ref.shape[-1]
    hit = lax.broadcasted_iota(jnp.int32, (pool, n), 0) == slot_ref[0]
    return jnp.where(hit, 1.0, 0.0).astype(BF16)


def normalized(scores, allowed):
    masked = jnp.where(allowed, scores, -jnp.inf)
    grown = jnp.exp(masked - jnp.max(masked, axis=-1, keepdims=True))
    return grown * (1.0 / jnp.sum(grown, axis=-1, keepdims=True))


def call(kernel, grid, in_specs, out_specs, out_shape, flops, size, **more):
    return pl.pallas_call(
        kernel,
        grid=grid,
        in_specs=in_specs,
        out_specs=out_specs,
        out_shape=out_shape,
        cost_estimate=pl.CostEstimate(flops=flops, bytes_accessed=size, transcendentals=0),
        compiler_params=pltpu.CompilerParams(vmem_limit_bytes=48 << 20),
        **more,
    )


def dispatch_kernel(*refs):
    slot_ref, value_refs, out_ref = refs[0], refs[1:-1], refs[-1]
    picked = one_hot(slot_ref, out_ref.shape[0])
    for i, ref in enumerate(value_refs):
        out_ref[:, i * DH : (i + 1) * DH] = nn(picked, ref[...]).astype(BF16)


def dispatch(slot_at, values, first, count, pool):
    n = slot_at.shape[-1]
    wide = len(values) * DH
    return call(
        dispatch_kernel,
        (count,),
        [pl.BlockSpec((1, 1, n), lambda h: (h + first, 0, 0))]
        + [pl.BlockSpec((n, DH), lambda h: (0, h + first)) for _ in values],
        pl.BlockSpec((pool, wide), lambda h: (0, h)),
        jax.ShapeDtypeStruct((pool, count * wide), BF16),
        2 * count * pool * n * wide,
        2 * count * (pool + n) * wide,
    )(slot_at, *values)


def collect_kernel(n_out, *refs):
    slot_ref, rows_ref, out_refs = refs[0], refs[1], refs[-n_out:]
    picked = one_hot(slot_ref, rows_ref.shape[0])
    merged = tn(picked, rows_ref[...]).astype(BF16)
    for i, ref in enumerate(out_refs):
        ref[...] = merged[:, i * DH : (i + 1) * DH]


def collect(slot_at, rows, first, count, n_out, earlier):
    n = slot_at.shape[-1]
    pool = rows.shape[0]
    heads = slot_at.shape[0]
    wide = n_out * DH
    return call(
        functools.partial(collect_kernel, n_out),
        (count,),
        [
            pl.BlockSpec((1, 1, n), lambda h: (h + first, 0, 0)),
            pl.BlockSpec((pool, wide), lambda h: (0, h)),
        ]
        + [pl.BlockSpec(memory_space=pl.ANY) for _ in earlier],
        [pl.BlockSpec((n, DH), lambda h: (0, h + first))] * n_out,
        [jax.ShapeDtypeStruct((n, heads * DH), BF16)] * n_out,
        2 * count * pool * n * wide,
        2 * count * (pool + n) * wide,
        input_output_aliases={2 + i: i for i in range(len(earlier))},
    )(slot_at, rows, *earlier)


class Rows:
    def __init__(self, sources, owned, cap):
        self.sources, self.owned, self.cap = sources, owned, cap
        self.aligned = cap % 8 == 0

    def selector(self, c):
        members = self.sources * self.cap
        layout = (members, members * self.owned)
        member = lax.broadcasted_iota(jnp.int32, layout, 0)
        row = lax.broadcasted_iota(jnp.int32, layout, 1)
        want = member // self.cap * (self.cap * self.owned) + c * self.cap + member % self.cap
        return jnp.where(row == want, 1.0, 0.0).astype(BF16)

    def split(self, rows):
        members = self.sources * self.cap
        if not self.aligned:
            return [nn(self.selector(c), rows).astype(BF16) for c in range(self.owned)]
        wide = rows.shape[1]
        four = rows.astype(F32).reshape(self.sources, self.owned, self.cap, wide)
        return [four[:, c].reshape(members, wide).astype(BF16) for c in range(self.owned)]

    def join(self, parts):
        wide = parts[0].shape[1]
        pool = self.sources * self.cap * self.owned
        if not self.aligned:
            total = jnp.zeros((pool, wide), F32)
            for c, part in enumerate(parts):
                total = total + tn(self.selector(c), part.astype(BF16))
            return total.astype(BF16)
        shaped = [p.reshape(self.sources, 1, self.cap, wide) for p in parts]
        return jnp.concatenate(shaped, axis=1).reshape(pool, wide).astype(BF16)


def cluster_allowed(live_ref, c, members):
    row = lax.broadcasted_iota(jnp.int32, (members, members), 0)
    col = lax.broadcasted_iota(jnp.int32, (members, members), 1)
    live = jnp.broadcast_to(live_ref[0, c : c + 1, :], (members, members)) > 0.5
    return (live & (col <= row)) | (col == row)


def owner_fwd_kernel(rows, factor, live_ref, qkv_ref, out_ref):
    members = rows.sources * rows.cap
    parts = []
    for c, qkv in enumerate(rows.split(qkv_ref[...])):
        q, k, v = qkv[:, :DH], qkv[:, DH : 2 * DH], qkv[:, 2 * DH :]
        prob = normalized(nt(q, k) * factor, cluster_allowed(live_ref, c, members))
        parts.append(nn(prob.astype(BF16), v))
    out_ref[...] = rows.join(parts)


def owner_bwd_kernel(rows, factor, live_ref, qkv_ref, attn_ref, grad_ref, out_ref):
    members = rows.sources * rows.cap
    attn_parts = rows.split(attn_ref[...])
    grad_parts = rows.split(grad_ref[...])
    parts = []
    for c, qkv in enumerate(rows.split(qkv_ref[...])):
        q, k, v = qkv[:, :DH], qkv[:, DH : 2 * DH], qkv[:, 2 * DH :]
        grad = grad_parts[c]
        row_dot = jnp.sum(grad.astype(F32) * attn_parts[c].astype(F32), axis=-1, keepdims=True)
        prob = normalized(nt(q, k) * factor, cluster_allowed(live_ref, c, members))
        change = (prob * (nt(grad, v) - row_dot)).astype(BF16)
        dq = nn(change, k) * factor
        dk = tn(change, q) * factor
        dv = tn(prob.astype(BF16), grad)
        parts.append(jnp.concatenate([dq, dk, dv], axis=1))
    out_ref[...] = rows.join(parts)


def owner_call(kernel, rows, factor, live, first, arrays, n_out):
    pool = arrays[0].shape[0]
    count = arrays[0].shape[1] // (3 * DH)
    members = rows.sources * rows.cap
    wides = [a.shape[1] // count for a in arrays]
    return call(
        functools.partial(kernel, rows, factor),
        (count,),
        [pl.BlockSpec((1, rows.owned, members), lambda h: (h + first, 0, 0))]
        + [pl.BlockSpec((pool, w), lambda h: (0, h)) for w in wides],
        pl.BlockSpec((pool, n_out * DH), lambda h: (0, h)),
        jax.ShapeDtypeStruct((pool, count * n_out * DH), BF16),
        12 * count * pool * members * DH,
        2 * count * pool * (sum(wides) + n_out * DH),
    )(live, *arrays)


def window_prob(factor, q, keys):
    n = q.shape[0]
    row = lax.broadcasted_iota(jnp.int32, (n, n + WINDOW), 0)
    col = lax.broadcasted_iota(jnp.int32, (n, n + WINDOW), 1)
    gap = row + WINDOW - col
    lowest = jnp.where(lax.axis_index("seq") > 0, 0, WINDOW)
    allowed = (gap >= 0) & (gap < WINDOW) & (col >= lowest)
    return normalized(nt(q, keys) * factor, allowed)


def window_fwd_kernel(factor, q_ref, kp_ref, k_ref, vp_ref, v_ref, out_ref):
    keys = jnp.concatenate([kp_ref[0], k_ref[...]], axis=0)
    vals = jnp.concatenate([vp_ref[0], v_ref[...]], axis=0)
    prob = window_prob(factor, q_ref[...], keys)
    out_ref[...] = nn(prob.astype(BF16), vals).astype(BF16)


def window_bwd_kernel(
    factor, q_ref, kp_ref, k_ref, vp_ref, v_ref, attn_ref, grad_ref, dq_ref, dk_ref, dv_ref, rim_ref
):
    q, grad = q_ref[...], grad_ref[...]
    keys = jnp.concatenate([kp_ref[0], k_ref[...]], axis=0)
    vals = jnp.concatenate([vp_ref[0], v_ref[...]], axis=0)
    prob = window_prob(factor, q, keys)
    row_dot = jnp.sum(grad.astype(F32) * attn_ref[...].astype(F32), axis=-1, keepdims=True)
    change = (prob * (nt(grad, vals) - row_dot)).astype(BF16)
    dq_ref[...] = (nn(change, keys) * factor).astype(BF16)
    dk = tn(change, q)
    dv = tn(prob.astype(BF16), grad)
    rim_ref[0] = dk[:WINDOW].astype(BF16)
    rim_ref[1] = dv[:WINDOW].astype(BF16)
    dk_ref[...] = dk[WINDOW:]
    dv_ref[...] = dv[WINDOW:]


def window_specs(n):
    here = pl.BlockSpec((n, DH), lambda h: (0, h))
    key = pl.BlockSpec((1, n, DH), lambda h: (0, 0, h))
    val = pl.BlockSpec((1, n, DH), lambda h: (1, 0, h))
    return here, key, val


def window_fwd(factor, query, key, value, before):
    n, wide = query.shape
    here, rim_key, rim_val = window_specs(n)
    return call(
        functools.partial(window_fwd_kernel, factor),
        (wide // DH,),
        [here, rim_key, here, rim_val, here],
        here,
        jax.ShapeDtypeStruct((n, wide), BF16),
        4 * n * 2 * n * wide,
        12 * n * wide,
    )(query, before, key, before, value)


def window_bwd(factor, query, key, value, before, attn, grad):
    n, wide = query.shape
    here, rim_key, rim_val = window_specs(n)
    return call(
        functools.partial(window_bwd_kernel, factor),
        (wide // DH,),
        [here, rim_key, here, rim_val, here, here, here],
        [here, here, here, pl.BlockSpec((2, n, DH), lambda h: (0, 0, h))],
        [
            jax.ShapeDtypeStruct((n, wide), BF16),
            jax.ShapeDtypeStruct((n, wide), F32),
            jax.ShapeDtypeStruct((n, wide), F32),
            jax.ShapeDtypeStruct((2, n, wide), BF16),
        ],
        10 * n * 2 * n * wide,
        28 * n * wide,
    )(query, before, key, before, value, attn, grad)


def body(
    win_query,
    win_key,
    win_value,
    clu_query,
    clu_key,
    clu_value,
    cluster_ids,
    win_gain,
    clu_gain,
    win_out_grad,
    clu_out_grad,
):
    n_rows = win_query.shape[0]
    factor = DH ** (-0.5)
    feat_width = (HW + HC) * DH
    sources = lax.axis_size("seq")
    n_cap = SLOTS // sources
    owned_count = 2 * n_rows // SLOTS
    pool_size = 2 * n_rows
    clu_heads = clu_query.shape[1] // DH
    rows = Rows(sources, owned_count, n_cap)

    def exchange(values):
        shaped = values.reshape(sources, pool_size // sources, values.shape[1])
        moved = lax.all_to_all(shaped, "seq", split_axis=0, concat_axis=0, tiled=True)
        return moved.reshape(values.shape)

    row_ids = lax.broadcasted_iota(jnp.int32, (n_rows, n_rows), 0)
    col_ids = lax.broadcasted_iota(jnp.int32, (n_rows, n_rows), 1)
    same_cluster = (cluster_ids[:, :, None] == cluster_ids[:, None, :]) & (col_ids < row_ids)
    rank_in = jnp.sum(same_cluster.astype(jnp.int32), axis=-1)
    slot_at = (cluster_ids * n_cap + rank_in)[:, None, :]

    n_clusters = sources * owned_count
    every = lax.broadcasted_iota(jnp.int32, (n_clusters, clu_heads, n_rows), 0)
    counts = jnp.sum((cluster_ids[None] == every).astype(F32), axis=-1)
    counts = counts.reshape(sources, owned_count, clu_heads)
    counts = lax.all_to_all(counts, "seq", split_axis=0, concat_axis=0, tiled=True)
    slot_pos = lax.broadcasted_iota(F32, (clu_heads, owned_count, sources, n_cap), 3)
    live = (slot_pos < counts.transpose(2, 1, 0)[..., None]).astype(F32)
    live = live.reshape(clu_heads, owned_count, sources * n_cap)

    chunks = CHUNKS if clu_heads % CHUNKS == 0 else 1
    per = clu_heads // chunks
    starts = [i * per for i in range(chunks)]

    held = [
        exchange(dispatch(slot_at, [clu_query, clu_key, clu_value], first, per, pool_size))
        for first in starts
    ]
    before = from_behind(jnp.stack([win_key, win_value]), "seq", 1)
    attn_win = window_fwd(factor, win_query, win_key, win_value, before)

    attn_held = [
        owner_call(owner_fwd_kernel, rows, factor, live, first, [qkv], 1)
        for first, qkv in zip(starts, held)
    ]
    attn_back = [exchange(part) for part in attn_held]
    attn_clu = ()
    for first, part in zip(starts, attn_back):
        attn_clu = collect(slot_at, part, first, per, 1, attn_clu)
    attn_clu = attn_clu[0]

    flat_win = attn_win.astype(F32)
    flat_clu = attn_clu.astype(F32)
    grad_win = win_out_grad.astype(F32) * win_gain
    grad_clu = clu_out_grad.astype(F32) * clu_gain
    totals = jnp.stack(
        [
            jnp.sum(flat_win * flat_win, axis=1) + jnp.sum(flat_clu * flat_clu, axis=1),
            jnp.sum(grad_win * flat_win, axis=1) + jnp.sum(grad_clu * flat_clu, axis=1),
        ]
    )
    totals = lax.psum(totals, "head")
    sq_total, dot_total = totals[0], totals[1]
    inv_rms = 1.0 / jnp.sqrt(sq_total / feat_width + EPSILON)
    coef_rows = inv_rms**3 * dot_total / feat_width
    dout_clu = (inv_rms[:, None] * grad_clu - coef_rows[:, None] * flat_clu).astype(BF16)
    dout_win = (inv_rms[:, None] * grad_win - coef_rows[:, None] * flat_win).astype(BF16)
    win_normed = (flat_win * inv_rms[:, None] * win_gain).astype(BF16)
    clu_normed = (flat_clu * inv_rms[:, None] * clu_gain).astype(BF16)

    grad_held = [
        exchange(dispatch(slot_at, [dout_clu], first, per, pool_size)) for first in starts
    ]
    win_dq, key_own, val_own, rim = window_bwd(
        factor, win_query, win_key, win_value, before, attn_win, dout_win
    )
    after_rim = from_behind(rim, "seq", -1)

    clu_grads = ()
    sent = [
        owner_call(owner_bwd_kernel, rows, factor, live, first, [qkv, part, grad], 3)
        for first, qkv, part, grad in zip(starts, held, attn_held, grad_held)
    ]
    home = [exchange(part) for part in sent]
    win_dk = ((key_own + after_rim[0]) * factor).astype(BF16)
    win_dv = (val_own + after_rim[1]).astype(BF16)
    for first, part in zip(starts, home):
        clu_grads = collect(slot_at, part, first, per, 3, clu_grads)
    return (win_normed, clu_normed, win_dq, win_dk, win_dv, *clu_grads)


def solution(mesh):
    return jax.shard_map(
        body,
        mesh=mesh,
        in_specs=(P("seq", "head"),) * 6
        + (P("head", "seq"), P("head"), P("head"))
        + (P("seq", "head"),) * 2,
        out_specs=(P("seq", "head"),) * 8,
        check_vma=False,
    )
```

time: 644 us -> 568 us (0.88)
  matrix products: 150 us -> 0 us
  Pallas kernels: 0 us -> 121 us
  waiting for transfers between devices: 217 us -> 333 us
  local copies, waits for them, and re-layouts: 104 us -> 28.4 us
  blocking collectives: 55.3 us -> 2.47 us
  other arithmetic: 49.6 us -> 17.6 us
    dot_general x20 -> x0, matrix products: 150 us -> none  [the longest x1 29.2 us: owner_gradients(): jnp.einsum('scahd,tcbhd->hcsatb', grad_rows, val_rows, preferred_element_...]
    pallas_call x0 -> x14, Pallas kernels: none -> 121 us  [the longest x4 54.5 us: owner_call(): call(functools.partial(kernel, rows, factor), (count,), [pl.BlockSpec((1,...]
    ppermute x2, waiting for transfers between devices: 66.9 us -> 136 us  [from_behind(): return lax.ppermute(block, axis, route)]
    all_to_all x1 -> x0, blocking collectives: 52.9 us -> none  [body(): lax.all_to_all(grad_sent, 'seq', split_axis=0, concat_axis=0, tiled=True)]
    all_to_all x8 -> x9, waiting for transfers between devices: 150 us -> 197 us  [the longest x8 197 us: exchange(): lax.all_to_all(shaped, 'seq', split_axis=0, concat_axis=0, tiled=True)]
    reshape x13 -> x0, local copies, waits for them, and re-layouts: 29.7 us -> none  [the longest x4 13 us: dispatch(): spread.astype(jnp.bfloat16)]
    convert_element_type x11 -> x0, local copies, waits for them, and re-layouts: 23.5 us -> none  [the longest x4 10.2 us: dispatch(): spread.astype(jnp.bfloat16)]
    reduce_sum x6 -> x3, other arithmetic: 23.3 us -> 2.68 us  [the longest x1 1.55 us: body(): counts = jnp.sum((cluster_ids[None] == every).astype(F32), axis=-1)]
  transfers between devices with their start and end apart: 10 -> 11, of which waited for: 7 -> 8; matrix products, arithmetic and copies ran while one was open for 37% -> 2% of each run, Pallas kernels for 0% -> 19%
where the time goes in v1:
time: 568 us; the launch traced here: 565 us
  waiting for transfers between devices  333 us (59%)
  Pallas kernels  121 us (21%)
  starting transfers between devices  61.8 us (11%)
  local copies, waits for them, and re-layouts  28.4 us (5%)
  other arithmetic  17.6 us (3%)
    all_to_all x8, waiting for transfers between devices, exchange(): lax.all_to_all(shaped, 'seq', split_axis=0, concat_axis=0, tiled=True)  197 us
    ppermute x2, waiting for transfers between devices, from_behind(): return lax.ppermute(block, axis, route)  136 us
    pallas_call x4, Pallas kernels, owner_call(): call(functools.partial(kernel, rows, factor), (count,), [pl.BlockSpec((1,...  54.5 us
    all_to_all x8, starting transfers between devices, exchange(): lax.all_to_all(shaped, 'seq', split_axis=0, concat_axis=0, tiled=True)  48.9 us
    unnamed x60, local copies, waits for them, and re-layouts  28.2 us
    pallas_call x4, Pallas kernels, collect(): call(functools.partial(collect_kernel, n_out), (count,), [pl.BlockSpec((1...  19.2 us
    pallas_call x4, Pallas kernels, dispatch(): call(dispatch_kernel, (count,), [pl.BlockSpec((1, 1, n), lambda h: (h + f...  18.9 us
    pallas_call x1, Pallas kernels, window_bwd(): call(functools.partial(window_bwd_kernel, factor), (wide // DH,), [here,...  15.7 us
  transfers between devices with their start and end apart: 11, of which 8 were waited for; matrix products, arithmetic and copies ran while one was open for 2% of the time, Pallas kernels for 19%

profile of v1, /device:TPU:14, one launch (start us, length us, event | category | flops | bytes accessed | tf_op | source)
XLA Modules:
  0.0 565.1 jit_solution(16823704255417097045)
XLA Ops:
  0.6 1.5 convert_reduce_fusion.1
  2.2 7.1 %all-to-all-start = ((f32[16,4,16]{2,1,0:T(4,128)}), f32[16,4,16]{2,1,0:T(4,128)S(1)}, u32[]{:S(2)}, u32[]{:S(2)}) async-start(f32[16,4,16]{2,1,0:T(4,128)} %bitcast.2), calls=%async_computation | async-start | bytes 65536 | tf_op jit(solution)/shard_map/all_to_all | solution.py:314
  9.3 2.1 convert_reduce_fusion
  11.5 0.7 multiply_add_fusion
  12.2 1.2 copy-done.11
  13.5 1.2 copy-done.13
  14.7 1.2 copy-done.15
  15.9 5.5 shard_map.173
  21.4 6.9 %all-to-all-start.3 = ((bf16[16,32,3072]{2,1,0:T(8,128)(2,1)}), bf16[16,32,3072]{2,1,0:T(8,128)(2,1)S(1)}, u32[]{:S(2)}, u32[]{:S(2)}) async-start(bf16[16,32,3072]{2,1,0:T(8,128)(2,1)} %bitcast.50), calls=%async_computation.3 | async-start | bytes 6291456 | tf_op jit(solution)/shard_map/all_to_all | solution.py:301
  28.3 1.2 copy-done.12
  29.6 1.2 copy-done.14
  30.8 1.2 copy-done.16
  32.0 5.5 shard_map.171
  37.5 60.7 %all-to-all-done.3 = bf16[16,32,3072]{2,1,0:T(8,128)(2,1)S(1)} async-done(((bf16[16,32,3072]{2,1,0:T(8,128)(2,1)}), bf16[16,32,3072]{2,1,0:T(8,128)(2,1)S(1)}, u32[]{:S(2)}, u32[]{:S(2)}) %all-to-all-start.3) | async-done | bytes 3145760 | tf_op jit(solution)/shard_map/all_to_all | solution.py:301
  98.2 1.7 copy-done.1
  99.9 5.1 all-to-all-start.1
  105.2 1.9 copy-done.2
  107.1 11.8 %shard_map.174.attn_ref = bf16[512,1024]{1,0:T(8,128)(2,1)S(1)} custom-call(f32[16,4,128]{2,1,0:T(4,128)S(1)} %compare_convert_fusion.live_ref, bf16[512,3072]{1,0:T(8,128)(2,1)S(1)} %bitcast.39), custom_call_target="tpu_custom_call" | custom-call | flops 805306368 | bytes 4194304 | tf_op jit(solution)/shard_map/pallas_call | solution.py:189
  118.9 1.0 copy-done.7
  119.9 54.7 %all-to-all-done.1 = bf16[16,32,3072]{2,1,0:T(8,128)(2,1)S(1)} async-done(((bf16[16,32,3072]{2,1,0:T(8,128)(2,1)}), bf16[16,32,3072]{2,1,0:T(8,128)(2,1)S(1)}, u32[]{:S(2)}, u32[]{:S(2)}) %all-to-all-start.1) | async-done | bytes 3145760 | tf_op jit(solution)/shard_map/all_to_all | solution.py:301
  174.6 5.1 all-to-all-start.4
  179.7 3.1 pad_maximum_fusion
  182.8 3.4 collective-permute-start
  186.2 11.8 %shard_map.172.attn_ref = bf16[512,1024]{1,0:T(8,128)(2,1)S(1)} custom-call(f32[16,4,128]{2,1,0:T(4,128)S(1)} %compare_convert_fusion.live_ref, bf16[512,3072]{1,0:T(8,128)(2,1)S(1)} %bitcast.36), custom_call_target="tpu_custom_call" | custom-call | flops 805306368 | bytes 4194304 | tf_op jit(solution)/shard_map/pallas_call | solution.py:189
  198.0 1.0 copy-done.9
  199.0 4.7 all-to-all-done.4
  203.6 7.5 %all-to-all-start.2 = ((bf16[16,32,1024]{2,1,0:T(8,128)(2,1)}), bf16[16,32,1024]{2,1,0:T(8,128)(2,1)S(1)}, u32[]{:S(2)}, u32[]{:S(2)}) async-start(bf16[16,32,1024]{2,1,0:T(8,128)(2,1)} %bitcast.44), calls=%async_computation.2 | async-start | bytes 2097152 | tf_op jit(solution)/shard_map/all_to_all | solution.py:301
  211.1 46.6 %collective-permute-done.kp_ref.vp_ref = bf16[2,256,2048]{2,1,0:T(8,128)(2,1)} collective-permute-done((bf16[2,256,2048]{2,1,0:T(8,128)(2,1)}, bf16[2,256,2048]{2,1,0:T(8,128)(2,1)}, u32[]{:S(2)}, u32[]{:S(2)}) %collective-permute-start) | collective-permute-done | bytes 2097184 | tf_op jit(solution)/shard_map/ppermute | solution.py:25
  257.7 1.2 copy-done.21
  258.9 1.2 copy-done.24
  260.1 12.6 %shard_map.170.attn_ref = bf16[256,2048]{1,0:T(8,128)(2,1)S(1)} custom-call(bf16[256,2048]{1,0:T(8,128)(2,1)S(1)} %copy-done.24, bf16[2,256,2048]{2,1,0:T(8,128)(2,1)} %collective-permute-done.kp_ref.vp_ref, bf16[256,2048]{1,0:T(8,128)(2,1)S(1)} %copy-done.21, bf16[2,256,2048]{2,1,0:T(8,128)(2,1)} %collective-permute-done.kp_ref.vp_ref, ...), custom_call_target="tpu_custom_call" | custom-call | flops 1073741824 | bytes 6291456 | tf_op jit(solution)/shard_map/pallas_call | solution.py:246
  272.8 0.6 fusion
  273.4 5.1 shard_map.175.refs_2_
  278.6 2.7 shard_map.176
  281.2 0.6 fusion.6
  281.8 2.5 psum.7
  284.3 4.6 fusion.11
  289.0 4.0 shard_map.180
  293.0 7.5 %all-to-all-start.7 = ((bf16[16,32,1024]{2,1,0:T(8,128)(2,1)}), bf16[16,32,1024]{2,1,0:T(8,128)(2,1)}, u32[]{:S(2)}, u32[]{:S(2)}) async-start(bf16[16,32,1024]{2,1,0:T(8,128)(2,1)} %bitcast.23), calls=%async_computation.7 | async-start | bytes 2097152 | tf_op jit(solution)/shard_map/all_to_all | solution.py:301
  300.5 4.0 shard_map.178
  304.5 21.2 %all-to-all-done.7 = bf16[16,32,1024]{2,1,0:T(8,128)(2,1)} async-done(((bf16[16,32,1024]{2,1,0:T(8,128)(2,1)}), bf16[16,32,1024]{2,1,0:T(8,128)(2,1)}, u32[]{:S(2)}, u32[]{:S(2)}) %all-to-all-start.7) | async-done | bytes 1048608 | tf_op jit(solution)/shard_map/all_to_all | solution.py:301
  325.7 5.8 %all-to-all-start.5 = ((bf16[16,32,1024]{2,1,0:T(8,128)(2,1)}), bf16[16,32,1024]{2,1,0:T(8,128)(2,1)S(1)}, u32[]{:S(2)}, u32[]{:S(2)}) async-start(bf16[16,32,1024]{2,1,0:T(8,128)(2,1)} %bitcast.19), calls=%async_computation.5 | async-start | bytes 2097152 | tf_op jit(solution)/shard_map/all_to_all | solution.py:301
  331.4 15.4 %shard_map.181 = bf16[512,3072]{1,0:T(8,128)(2,1)S(1)} custom-call(f32[16,4,128]{2,1,0:T(4,128)S(1)} %compare_convert_fusion.live_ref, bf16[512,3072]{1,0:T(8,128)(2,1)} %bitcast.38, bf16[512,1024]{1,0:T(8,128)(2,1)S(1)} %copy-done.8, bf16[512,1024]{1,0:T(8,128)(2,1)} %bitcast.24.grad_ref), custom_call_target="tpu_custom_call" | custom-call | flops 805306368 | bytes 8388608 | tf_op jit(solution)/shard_map/pallas_call | solution.py:189
  346.9 1.7 copy-done.4
  348.5 6.4 %all-to-all-done.5 = bf16[16,32,1024]{2,1,0:T(8,128)(2,1)S(1)} async-done(((bf16[16,32,1024]{2,1,0:T(8,128)(2,1)}), bf16[16,32,1024]{2,1,0:T(8,128)(2,1)S(1)}, u32[]{:S(2)}, u32[]{:S(2)}) %all-to-all-start.5) | async-done | bytes 1048608 | tf_op jit(solution)/shard_map/all_to_all | solution.py:301
  354.9 1.0 copy-done.17
  355.9 5.8 %all-to-all-start.8 = ((bf16[16,32,3072]{2,1,0:T(8,128)(2,1)}), bf16[16,32,3072]{2,1,0:T(8,128)(2,1)S(1)}, u32[]{:S(2)}, u32[]{:S(2)}) async-start(bf16[16,32,3072]{2,1,0:T(8,128)(2,1)} %bitcast.42), calls=%async_computation.8 | async-start | bytes 6291456 | tf_op jit(solution)/shard_map/all_to_all | solution.py:301
  361.8 1.2 copy-done.10
  363.0 1.2 copy-done.18
  364.2 15.6 %shard_map.179 = bf16[512,3072]{1,0:T(8,128)(2,1)S(1)} custom-call(f32[16,4,128]{2,1,0:T(4,128)S(1)} %compare_convert_fusion.live_ref, bf16[512,3072]{1,0:T(8,128)(2,1)} %bitcast.37, bf16[512,1024]{1,0:T(8,128)(2,1)S(1)} %copy-done.10, bf16[512,1024]{1,0:T(8,128)(2,1)S(1)} %bitcast.46), custom_call_target="tpu_custom_call" | custom-call | flops 805306368 | bytes 8388608 | tf_op jit(solution)/shard_map/pallas_call | solution.py:189
  379.8 1.6 copy-done.3
  381.4 49.3 %all-to-all-done.8 = bf16[16,32,3072]{2,1,0:T(8,128)(2,1)S(1)} async-done(((bf16[16,32,3072]{2,1,0:T(8,128)(2,1)}), bf16[16,32,3072]{2,1,0:T(8,128)(2,1)S(1)}, u32[]{:S(2)}, u32[]{:S(2)}) %all-to-all-start.8) | async-done | bytes 3145760 | tf_op jit(solution)/shard_map/all_to_all | solution.py:301
  430.7 5.1 all-to-all-start.6
  435.8 1.2 copy-done.6
  437.0 1.2 copy-done.20
  438.2 1.2 copy-done.22
  439.5 1.2 copy-done.23
  440.7 1.2 copy-done.25
  441.9 15.7 %shard_map.177 = (bf16[256,2048]{1,0:T(8,128)(2,1)}, f32[256,2048]{1,0:T(8,128)}, f32[256,2048]{1,0:T(8,128)}, bf16[2,256,2048]{2,1,0:T(8,128)(2,1)}) custom-call(bf16[256,2048]{1,0:T(8,128)(2,1)S(1)} %copy-done.25, bf16[2,256,2048]{2,1,0:T(8,128)(2,1)} %collective-permute-done.kp_ref.vp_ref, bf16[256,2048]{1,0:T(8,128)(2,1)S(1)} %copy-done.22, ...), custom_call_target="tpu_custom_call" | custom-call | flops 2684354560 | bytes 14680064 | tf_op jit(solution)/shard_map/pallas_call | solution.py:260
  457.6 2.5 collective-permute-start.1
  460.1 89.3 %collective-permute-done.1 = bf16[2,256,2048]{2,1,0:T(8,128)(2,1)S(1)} collective-permute-done((bf16[2,256,2048]{2,1,0:T(8,128)(2,1)}, bf16[2,256,2048]{2,1,0:T(8,128)(2,1)S(1)}, u32[]{:S(2)}, u32[]{:S(2)}) %collective-permute-start.1) | collective-permute-done | bytes 2097184 | tf_op jit(solution)/shard_map/ppermute | solution.py:25
  549.3 4.3 fusion.12
  553.6 4.6 shard_map.182
  558.2 6.9 %shard_map.183 = (bf16[256,2048]{1,0:T(8,128)(2,1)}, bf16[256,2048]{1,0:T(8,128)(2,1)}, bf16[256,2048]{1,0:T(8,128)(2,1)}) custom-call(s32[16,1,256]{2,1,0:T(1,128)S(1)} %broadcast_in_dim.2.refs_0_, bf16[512,3072]{1,0:T(8,128)(2,1)} %bitcast.22.refs_1_, ...), custom_call_target="tpu_custom_call", output_to_operand_aliasing={{0}: (2, {}), {1}: (3, {}), {2}: (4, {})} | custom-call | flops 805306368 | bytes 4718592 | tf_op jit(solution)/shard_map/pallas_call | solution.py:100
  (54 shorter events, 0.4 us)
Async XLA Ops:
  2.2 19.2 %all-to-all-start = ((f32[16,4,16]{2,1,0:T(4,128)}), f32[16,4,16]{2,1,0:T(4,128)S(1)}, u32[]{:S(2)}, u32[]{:S(2)}) async-start(f32[16,4,16]{2,1,0:T(4,128)} %bitcast.2), calls=%async_computation | async-start | bytes 65536 | tf_op jit(solution)/shard_map/all_to_all | solution.py:314
  12.2 1.2 copy-start.11
  13.4 1.2 copy-start.13
  14.7 1.2 copy-start.15
  21.4 76.8 %all-to-all-start.3 = ((bf16[16,32,3072]{2,1,0:T(8,128)(2,1)}), bf16[16,32,3072]{2,1,0:T(8,128)(2,1)S(1)}, u32[]{:S(2)}, u32[]{:S(2)}) async-start(bf16[16,32,3072]{2,1,0:T(8,128)(2,1)} %bitcast.50), calls=%async_computation.3 | async-start | bytes 6291456 | tf_op jit(solution)/shard_map/all_to_all | solution.py:301
  28.3 1.2 copy-start.12
  29.6 1.2 copy-start.14
  30.8 1.2 copy-start.16
  98.2 1.7 copy-start.1
  99.9 74.7 %all-to-all-start.1 = ((bf16[16,32,3072]{2,1,0:T(8,128)(2,1)}), bf16[16,32,3072]{2,1,0:T(8,128)(2,1)S(1)}, u32[]{:S(2)}, u32[]{:S(2)}) async-start(bf16[16,32,3072]{2,1,0:T(8,128)(2,1)} %bitcast.49), calls=%async_computation.1 | async-start | bytes 6291456 | tf_op jit(solution)/shard_map/all_to_all | solution.py:301
  105.2 1.9 copy-start.2
  118.9 1.0 copy-start.7
  174.6 11.6 %copy-start = (bf16[16,32,3072]{2,1,0:T(8,128)(2,1)}, bf16[16,32,3072]{2,1,0:T(8,128)(2,1)S(1)}, u32[]{:S(2)}) copy-start(bf16[16,32,3072]{2,1,0:T(8,128)(2,1)S(1)} %all-to-all-done.1) | copy-start | bytes 9437188
  174.6 29.0 %all-to-all-start.4 = ((bf16[16,32,1024]{2,1,0:T(8,128)(2,1)}), bf16[16,32,1024]{2,1,0:T(8,128)(2,1)}, u32[]{:S(2)}, u32[]{:S(2)}) async-start(bf16[16,32,1024]{2,1,0:T(8,128)(2,1)} %bitcast.43), calls=%async_computation.4 | async-start | bytes 2097152 | tf_op jit(solution)/shard_map/all_to_all | solution.py:301
  182.8 74.8 %collective-permute-start = (bf16[2,256,2048]{2,1,0:T(8,128)(2,1)}, bf16[2,256,2048]{2,1,0:T(8,128)(2,1)}, u32[]{:S(2)}, u32[]{:S(2)}) collective-permute-start(bf16[2,256,2048]{2,1,0:T(8,128)(2,1)} %pad_maximum_fusion), channel_id=1, source_target_pairs={{0,2},{2,4},{4,6},{6,8},{8,10},{10,12},{12,14},{14,16},{16,18},{18... | collective-permute-start | bytes 6291464 | tf_op jit(solution)/shard_map/ppermute | solution.py:25
  198.0 1.0 copy-start.9
  199.0 58.7 %copy-start.19 = (bf16[256,2048]{1,0:T(8,128)(2,1)S(1)}, bf16[256,2048]{1,0:T(8,128)(2,1)}, u32[]{:S(2)}) copy-start(bf16[256,2048]{1,0:T(8,128)(2,1)} %v_ref.3) | copy-start | bytes 3145732
  203.6 74.9 %all-to-all-start.2 = ((bf16[16,32,1024]{2,1,0:T(8,128)(2,1)}), bf16[16,32,1024]{2,1,0:T(8,128)(2,1)S(1)}, u32[]{:S(2)}, u32[]{:S(2)}) async-start(bf16[16,32,1024]{2,1,0:T(8,128)(2,1)} %bitcast.44), calls=%async_computation.2 | async-start | bytes 2097152 | tf_op jit(solution)/shard_map/all_to_all | solution.py:301
  257.7 1.2 copy-start.21
  258.9 1.2 copy-start.24
  260.1 12.7 %copy-start.27 = (bf16[256,2048]{1,0:T(8,128)(2,1)S(1)}, bf16[256,2048]{1,0:T(8,128)(2,1)}, u32[]{:S(2)}) copy-start(bf16[256,2048]{1,0:T(8,128)(2,1)} %param.20) | copy-start | bytes 3145732
  260.1 12.7 %copy-start.28 = (f32[2048]{0:T(1024)S(1)}, f32[2048]{0:T(1024)}, u32[]{:S(2)}) copy-start(f32[2048]{0:T(1024)} %param.18) | copy-start | bytes 24580
  272.8 11.5 %copy-start.5 = (bf16[256,2048]{1,0:T(8,128)(2,1)}, bf16[256,2048]{1,0:T(8,128)(2,1)S(1)}, u32[]{:S(2)}) copy-start(bf16[256,2048]{1,0:T(8,128)(2,1)S(1)} %shard_map.170.attn_ref) | copy-start | bytes 3145732
  278.5 2.7 copy-start.29
  278.5 2.7 copy-start.26
  293.0 32.7 %all-to-all-start.7 = ((bf16[16,32,1024]{2,1,0:T(8,128)(2,1)}), bf16[16,32,1024]{2,1,0:T(8,128)(2,1)}, u32[]{:S(2)}, u32[]{:S(2)}) async-start(bf16[16,32,1024]{2,1,0:T(8,128)(2,1)} %bitcast.23), calls=%async_computation.7 | async-start | bytes 2097152 | tf_op jit(solution)/shard_map/all_to_all | solution.py:301
  300.5 30.9 %copy-start.8 = (bf16[512,1024]{1,0:T(8,128)(2,1)S(1)}, bf16[512,1024]{1,0:T(8,128)(2,1)}, u32[]{:S(2)}) copy-start(bf16[512,1024]{1,0:T(8,128)(2,1)} %copy-done.7) | copy-start | bytes 3145732
  325.7 29.3 %all-to-all-start.5 = ((bf16[16,32,1024]{2,1,0:T(8,128)(2,1)}), bf16[16,32,1024]{2,1,0:T(8,128)(2,1)S(1)}, u32[]{:S(2)}, u32[]{:S(2)}) async-start(bf16[16,32,1024]{2,1,0:T(8,128)(2,1)} %bitcast.19), calls=%async_computation.5 | async-start | bytes 2097152 | tf_op jit(solution)/shard_map/all_to_all | solution.py:301
  346.9 1.7 copy-start.4
  354.9 1.0 copy-start.17
  355.9 74.7 %all-to-all-start.8 = ((bf16[16,32,3072]{2,1,0:T(8,128)(2,1)}), bf16[16,32,3072]{2,1,0:T(8,128)(2,1)S(1)}, u32[]{:S(2)}, u32[]{:S(2)}) async-start(bf16[16,32,3072]{2,1,0:T(8,128)(2,1)} %bitcast.42), calls=%async_computation.8 | async-start | bytes 6291456 | tf_op jit(solution)/shard_map/all_to_all | solution.py:301
  361.7 1.2 copy-start.10
  363.0 1.2 copy-start.18
  379.8 1.6 copy-start.3
  430.7 127.5 %all-to-all-start.6 = ((bf16[16,32,3072]{2,1,0:T(8,128)(2,1)}), bf16[16,32,3072]{2,1,0:T(8,128)(2,1)}, u32[]{:S(2)}, u32[]{:S(2)}) async-start(bf16[16,32,3072]{2,1,0:T(8,128)(2,1)} %bitcast.41), calls=%async_computation.6 | async-start | bytes 6291456 | tf_op jit(solution)/shard_map/all_to_all | solution.py:301
  435.8 1.2 copy-start.6
  437.0 1.2 copy-start.20
  438.2 1.2 copy-start.22
  439.5 1.2 copy-start.23
  440.7 1.2 copy-start.25
  457.6 91.7 %collective-permute-start.1 = (bf16[2,256,2048]{2,1,0:T(8,128)(2,1)}, bf16[2,256,2048]{2,1,0:T(8,128)(2,1)S(1)}, u32[]{:S(2)}, u32[]{:S(2)}) collective-permute-start(bf16[2,256,2048]{2,1,0:T(8,128)(2,1)} %get-tuple-element.20), channel_id=1, source_target_pairs={{2,0},{4,2},{6,4},{8,6},{10,8},{12,10},{14,12},{16,14},{18,16},{20... | collective-permute-start | bytes 6291464 | tf_op jit(solution)/shard_map/ppermute | solution.py:25

commit v2 on v1

--- a/solution.py
+++ b/solution.py
@@ -13,6 +13,7 @@
 WINDOW = 256
 SLOTS = 128
 CHUNKS = 2
+EMPTY = 1000.0
 
 EPSILON = 1e-06
 F32 = jnp.float32
@@ -57,23 +58,27 @@
         out_specs=out_specs,
         out_shape=out_shape,
         cost_estimate=pl.CostEstimate(flops=flops, bytes_accessed=size, transcendentals=0),
-        compiler_params=pltpu.CompilerParams(vmem_limit_bytes=48 << 20),
+        compiler_params=pltpu.CompilerParams(vmem_limit_bytes=60 << 20),
         **more,
     )
 
 
-def dispatch_kernel(*refs):
+def dispatch_kernel(mark, *refs):
     slot_ref, value_refs, out_ref = refs[0], refs[1:-1], refs[-1]
     picked = one_hot(slot_ref, out_ref.shape[0])
     for i, ref in enumerate(value_refs):
-        out_ref[:, i * DH : (i + 1) * DH] = nn(picked, ref[...]).astype(BF16)
-
-
-def dispatch(slot_at, values, first, count, pool):
+        moved = nn(picked, ref[...])
+        if mark and i == len(value_refs) - 1:
+            filled = nn(picked, jnp.ones(ref.shape, BF16))
+            moved = jnp.where(filled > 0.5, moved, EMPTY)
+        out_ref[:, i * DH : (i + 1) * DH] = moved.astype(BF16)
+
+
+def dispatch(slot_at, values, first, count, pool, mark):
     n = slot_at.shape[-1]
     wide = len(values) * DH
     return call(
-        dispatch_kernel,
+        functools.partial(dispatch_kernel, mark),
         (count,),
         [pl.BlockSpec((1, 1, n), lambda h: (h + first, 0, 0))]
         + [pl.BlockSpec((n, DH), lambda h: (0, h + first)) for _ in values],
@@ -146,25 +151,26 @@
         return jnp.concatenate(shaped, axis=1).reshape(pool, wide).astype(BF16)
 
 
-def cluster_allowed(live_ref, c, members):
+def cluster_allowed(v):
+    members = v.shape[0]
+    lane = lax.broadcasted_iota(jnp.int32, (8, DH), 1)
+    first = nt(jnp.where(lane == 0, 1.0, 0.0).astype(BF16), v)[:1]
     row = lax.broadcasted_iota(jnp.int32, (members, members), 0)
     col = lax.broadcasted_iota(jnp.int32, (members, members), 1)
-    live = jnp.broadcast_to(live_ref[0, c : c + 1, :], (members, members)) > 0.5
+    live = jnp.broadcast_to(first, (members, members)) < EMPTY / 2
     return (live & (col <= row)) | (col == row)
 
 
-def owner_fwd_kernel(rows, factor, live_ref, qkv_ref, out_ref):
-    members = rows.sources * rows.cap
+def owner_fwd_kernel(rows, factor, qkv_ref, out_ref):
     parts = []
-    for c, qkv in enumerate(rows.split(qkv_ref[...])):
+    for qkv in rows.split(qkv_ref[...]):
         q, k, v = qkv[:, :DH], qkv[:, DH : 2 * DH], qkv[:, 2 * DH :]
-        prob = normalized(nt(q, k) * factor, cluster_allowed(live_ref, c, members))
+        prob = normalized(nt(q, k) * factor, cluster_allowed(v))
         parts.append(nn(prob.astype(BF16), v))
     out_ref[...] = rows.join(parts)
 
 
-def owner_bwd_kernel(rows, factor, live_ref, qkv_ref, attn_ref, grad_ref, out_ref):
-    members = rows.sources * rows.cap
+def owner_bwd_kernel(rows, factor, qkv_ref, attn_ref, grad_ref, out_ref):
     attn_parts = rows.split(attn_ref[...])
     grad_parts = rows.split(grad_ref[...])
     parts = []
@@ -172,7 +178,7 @@
         q, k, v = qkv[:, :DH], qkv[:, DH : 2 * DH], qkv[:, 2 * DH :]
         grad = grad_parts[c]
         row_dot = jnp.sum(grad.astype(F32) * attn_parts[c].astype(F32), axis=-1, keepdims=True)
-        prob = normalized(nt(q, k) * factor, cluster_allowed(live_ref, c, members))
+        prob = normalized(nt(q, k) * factor, cluster_allowed(v))
         change = (prob * (nt(grad, v) - row_dot)).astype(BF16)
         dq = nn(change, k) * factor
         dk = tn(change, q) * factor
@@ -181,7 +187,7 @@
     out_ref[...] = rows.join(parts)
 
 
-def owner_call(kernel, rows, factor, live, first, arrays, n_out):
+def owner_call(kernel, rows, factor, arrays, n_out):
     pool = arrays[0].shape[0]
     count = arrays[0].shape[1] // (3 * DH)
     members = rows.sources * rows.cap
@@ -189,13 +195,12 @@
     return call(
         functools.partial(kernel, rows, factor),
         (count,),
-        [pl.BlockSpec((1, rows.owned, members), lambda h: (h + first, 0, 0))]
-        + [pl.BlockSpec((pool, w), lambda h: (0, h)) for w in wides],
+        [pl.BlockSpec((pool, w), lambda h: (0, h)) for w in wides],
         pl.BlockSpec((pool, n_out * DH), lambda h: (0, h)),
         jax.ShapeDtypeStruct((pool, count * n_out * DH), BF16),
         12 * count * pool * members * DH,
         2 * count * pool * (sum(wides) + n_out * DH),
-    )(live, *arrays)
+    )(*arrays)
 
 
 def window_prob(factor, q, keys):
@@ -209,68 +214,62 @@
 
 
 def window_fwd_kernel(factor, q_ref, kp_ref, k_ref, vp_ref, v_ref, out_ref):
-    keys = jnp.concatenate([kp_ref[0], k_ref[...]], axis=0)
-    vals = jnp.concatenate([vp_ref[0], v_ref[...]], axis=0)
+    keys = jnp.concatenate([kp_ref[...], k_ref[...]], axis=0)
+    vals = jnp.concatenate([vp_ref[...], v_ref[...]], axis=0)
     prob = window_prob(factor, q_ref[...], keys)
     out_ref[...] = nn(prob.astype(BF16), vals).astype(BF16)
 
 
 def window_bwd_kernel(
-    factor, q_ref, kp_ref, k_ref, vp_ref, v_ref, attn_ref, grad_ref, dq_ref, dk_ref, dv_ref, rim_ref
+    factor, q_ref, kp_ref, k_ref, vp_ref, v_ref, attn_ref, grad_ref, dq_ref, dk_ref, dv_ref, rim_key_ref, rim_val_ref
 ):
     q, grad = q_ref[...], grad_ref[...]
-    keys = jnp.concatenate([kp_ref[0], k_ref[...]], axis=0)
-    vals = jnp.concatenate([vp_ref[0], v_ref[...]], axis=0)
+    keys = jnp.concatenate([kp_ref[...], k_ref[...]], axis=0)
+    vals = jnp.concatenate([vp_ref[...], v_ref[...]], axis=0)
     prob = window_prob(factor, q, keys)
     row_dot = jnp.sum(grad.astype(F32) * attn_ref[...].astype(F32), axis=-1, keepdims=True)
     change = (prob * (nt(grad, vals) - row_dot)).astype(BF16)
     dq_ref[...] = (nn(change, keys) * factor).astype(BF16)
     dk = tn(change, q)
     dv = tn(prob.astype(BF16), grad)
-    rim_ref[0] = dk[:WINDOW].astype(BF16)
-    rim_ref[1] = dv[:WINDOW].astype(BF16)
+    rim_key_ref[...] = dk[:WINDOW].astype(BF16)
+    rim_val_ref[...] = dv[:WINDOW].astype(BF16)
     dk_ref[...] = dk[WINDOW:]
     dv_ref[...] = dv[WINDOW:]
 
 
-def window_specs(n):
-    here = pl.BlockSpec((n, DH), lambda h: (0, h))
-    key = pl.BlockSpec((1, n, DH), lambda h: (0, 0, h))
-    val = pl.BlockSpec((1, n, DH), lambda h: (1, 0, h))
-    return here, key, val
-
-
 def window_fwd(factor, query, key, value, before):
     n, wide = query.shape
-    here, rim_key, rim_val = window_specs(n)
+    here = pl.BlockSpec((n, DH), lambda h: (0, h))
     return call(
         functools.partial(window_fwd_kernel, factor),
         (wide // DH,),
-        [here, rim_key, here, rim_val, here],
+        [here] * 5,
         here,
         jax.ShapeDtypeStruct((n, wide), BF16),
         4 * n * 2 * n * wide,
         12 * n * wide,
-    )(query, before, key, before, value)
+    )(query, before[0], key, before[1], value)
 
 
 def window_bwd(factor, query, key, value, before, attn, grad):
     n, wide = query.shape
-    here, rim_key, rim_val = window_specs(n)
+    here = pl.BlockSpec((n, DH), lambda h: (0, h))
     return call(
         functools.partial(window_bwd_kernel, factor),
         (wide // DH,),
-        [here, rim_key, here, rim_val, here, here, here],
-        [here, here, here, pl.BlockSpec((2, n, DH), lambda h: (0, 0, h))],
+        [here] * 7,
+        [here] * 5,
         [
             jax.ShapeDtypeStruct((n, wide), BF16),
             jax.ShapeDtypeStruct((n, wide), F32),
             jax.ShapeDtypeStruct((n, wide), F32),
-            jax.ShapeDtypeStruct((2, n, wide), BF16),
+            jax.ShapeDtypeStruct((n, wide), BF16),
+            jax.ShapeDtypeStruct((n, wide), BF16),
         ],
         10 * n * 2 * n * wide,
         28 * n * wide,
-    )(query, before, key, before, value, attn, grad)
+    )(query, before[0], key, before[1], value, attn, grad)
 
 
 def body(
@@ -307,30 +306,20 @@
     rank_in = jnp.sum(same_cluster.astype(jnp.int32), axis=-1)
     slot_at = (cluster_ids * n_cap + rank_in)[:, None, :]
 
-    n_clusters = sources * owned_count
-    every = lax.broadcasted_iota(jnp.int32, (n_clusters, clu_heads, n_rows), 0)
-    counts = jnp.sum((cluster_ids[None] == every).astype(F32), axis=-1)
-    counts = counts.reshape(sources, owned_count, clu_heads)
-    counts = lax.all_to_all(counts, "seq", split_axis=0, concat_axis=0, tiled=True)
-    slot_pos = lax.broadcasted_iota(F32, (clu_heads, owned_count, sources, n_cap), 3)
-    live = (slot_pos < counts.transpose(2, 1, 0)[..., None]).astype(F32)
-    live = live.reshape(clu_heads, owned_count, sources * n_cap)
-
     chunks = CHUNKS if clu_heads % CHUNKS == 0 else 1
     per = clu_heads // chunks
     starts = [i * per for i in range(chunks)]
 
-    held = [
-        exchange(dispatch(slot_at, [clu_query, clu_key, clu_value], first, per, pool_size))
+    sent_first = [
+        dispatch(slot_at, [clu_query, clu_key, clu_value], first, per, pool_size, True)
         for first in starts
     ]
-    before = from_behind(jnp.stack([win_key, win_value]), "seq", 1)
+    before = (from_behind(win_key, "seq", 1), from_behind(win_value, "seq", 1))
+    held = [exchange(part) for part in sent_first]
     attn_win = window_fwd(factor, win_query, win_key, win_value, before)
-
-    attn_held = [
-        owner_call(owner_fwd_kernel, rows, factor, live, first, [qkv], 1)
-        for first, qkv in zip(starts, held)
-    ]
+    held[0], attn_win = lax.optimization_barrier((held[0], attn_win))
+
+    attn_held = [owner_call(owner_fwd_kernel, rows, factor, [qkv], 1) for qkv in held]
     attn_back = [exchange(part) for part in attn_held]
     attn_clu = ()
     for first, part in zip(starts, attn_back):
@@ -357,21 +346,26 @@
     clu_normed = (flat_clu * inv_rms[:, None] * clu_gain).astype(BF16)
 
     grad_held = [
-        exchange(dispatch(slot_at, [dout_clu], first, per, pool_size)) for first in starts
+        exchange(dispatch(slot_at, [dout_clu], first, per, pool_size, False)) for first in starts
     ]
-    win_dq, key_own, val_own, rim = window_bwd(
+    win_dq, key_own, val_own, rim_key, rim_val = window_bwd(
         factor, win_query, win_key, win_value, before, attn_win, dout_win
     )
-    after_rim = from_behind(rim, "seq", -1)
+    grad_held[0], rim_key, rim_val = lax.optimization_barrier((grad_held[0], rim_key, rim_val))
+    after_key = from_behind(rim_key, "seq", -1)
+    after_val = from_behind(rim_val, "seq", -1)
+    grad_held[-1], after_key, after_val = lax.optimization_barrier(
+        (grad_held[-1], after_key, after_val)
+    )
 
     clu_grads = ()
     sent = [
-        owner_call(owner_bwd_kernel, rows, factor, live, first, [qkv, part, grad], 3)
-        for first, qkv, part, grad in zip(starts, held, attn_held, grad_held)
+        owner_call(owner_bwd_kernel, rows, factor, [qkv, part, grad], 3)
+        for qkv, part, grad in zip(held, attn_held, grad_held)
     ]
     home = [exchange(part) for part in sent]
-    win_dk = ((key_own + after_rim[0]) * factor).astype(BF16)
-    win_dv = (val_own + after_rim[1]).astype(BF16)
+    win_dk = ((key_own + after_key) * factor).astype(BF16)
+    win_dv = (val_own + after_val).astype(BF16)
     for first, part in zip(starts, home):
         clu_grads = collect(slot_at, part, first, per, 3, clu_grads)
     return (win_normed, clu_normed, win_dq, win_dk, win_dv, *clu_grads)

time: 568 us -> 610 us (1.074)
  waiting for transfers between devices: 333 us -> 380 us
  local copies, waits for them, and re-layouts: 28.4 us -> 5.02 us
  Pallas kernels: 121 us -> 140 us
    ppermute x2 -> x4, waiting for transfers between devices: 136 us -> 212 us  [from_behind(): return lax.ppermute(block, axis, route)]
    all_to_all x8, waiting for transfers between devices: 197 us -> 167 us  [exchange(): lax.all_to_all(shaped, 'seq', split_axis=0, concat_axis=0, tiled=True)]
    unnamed x60 -> x22, local copies, waits for them, and re-layouts: 28.2 us -> 4.4 us
    pallas_call x10, Pallas kernels: 102 us -> 114 us  [the longest x4 57.1 us: owner_call(): call(functools.partial(kernel, rows, factor), (count,), [pl.BlockSpec((po...]
    all_to_all x1 -> x0, starting transfers between devices: 7.14 us -> none  [body(): lax.all_to_all(counts, 'seq', split_axis=0, concat_axis=0, tiled=True)]
    pallas_call x4, Pallas kernels: 19.2 us -> 26.1 us  [collect(): call(functools.partial(collect_kernel, n_out), (count,), [pl.BlockSpec((1...]
    ppermute x2 -> x4, starting transfers between devices: 5.82 us -> 12.6 us  [from_behind(): return lax.ppermute(block, axis, route)]
  transfers between devices with their start and end apart: 11 -> 12, of which waited for: 8 -> 9; matrix products, arithmetic and copies ran while one was open for 2% -> 1% of each run, Pallas kernels for 19% -> 19%
where the time goes in v2:
time: 610 us; the launch traced here: 605 us
  waiting for transfers between devices  380 us (62%)
  Pallas kernels  140 us (23%)
  starting transfers between devices  61.4 us (10%)
  other arithmetic  14.9 us (2%)
    ppermute x4, waiting for transfers between devices, from_behind(): return lax.ppermute(block, axis, route)  212 us
    all_to_all x8, waiting for transfers between devices, exchange(): lax.all_to_all(shaped, 'seq', split_axis=0, concat_axis=0, tiled=True)  167 us
    pallas_call x4, Pallas kernels, owner_call(): call(functools.partial(kernel, rows, factor), (count,), [pl.BlockSpec((po...  57.1 us
    all_to_all x8, starting transfers between devices, exchange(): lax.all_to_all(shaped, 'seq', split_axis=0, concat_axis=0, tiled=True)  48.8 us
    pallas_call x4, Pallas kernels, dispatch(): call(functools.partial(dispatch_kernel, mark), (count,), [pl.BlockSpec((1...  26.4 us
    pallas_call x4, Pallas kernels, collect(): call(functools.partial(collect_kernel, n_out), (count,), [pl.BlockSpec((1...  26.1 us
    pallas_call x1, Pallas kernels, window_bwd(): call(functools.partial(window_bwd_kernel, factor), (wide // DH,), [here]...  16.6 us
    pallas_call x1, Pallas kernels, window_fwd(): call(functools.partial(window_fwd_kernel, factor), (wide // DH,), [here]...  14.1 us
  transfers between devices with their start and end apart: 12, of which 9 were waited for; matrix products, arithmetic and copies ran while one was open for 1% of the time, Pallas kernels for 19%

profile of v2, /device:TPU:14, one launch (start us, length us, event | category | flops | bytes accessed | tf_op | source)
XLA Modules:
  0.0 604.5 jit_solution(5044466675365012815)
XLA Ops:
  0.7 2.1 convert_reduce_fusion
  2.8 0.7 multiply_add_fusion
  3.5 0.6 broadcast_in_dim.2.refs_0_
  4.1 7.4 %shard_map.170 = bf16[512,3072]{1,0:T(8,128)(2,1)} custom-call(s32[16,1,256]{2,1,0:T(1,128)} %broadcast_in_dim.2.refs_0_, bf16[256,2048]{1,0:T(8,128)(2,1)} %refs_1_.3, bf16[256,2048]{1,0:T(8,128)(2,1)} %refs_2_.3, bf16[256,2048]{1,0:T(8,128)(2,1)} %refs_3_.3), custom_call_target="tpu_custom_call" | custom-call | flops 805306368 | bytes 4718592 | tf_op jit(solution)/shard_map/pallas_call | solution.py:80
  11.5 7.1 %all-to-all-start = ((bf16[16,32,3072]{2,1,0:T(8,128)(2,1)}), bf16[16,32,3072]{2,1,0:T(8,128)(2,1)S(1)}, u32[]{:S(2)}, u32[]{:S(2)}) async-start(bf16[16,32,3072]{2,1,0:T(8,128)(2,1)} %bitcast.26), calls=%async_computation | async-start | bytes 6291456 | tf_op jit(solution)/shard_map/all_to_all | solution.py:300
  18.7 7.4 %shard_map.172 = bf16[512,3072]{1,0:T(8,128)(2,1)} custom-call(s32[16,1,256]{2,1,0:T(1,128)} %broadcast_in_dim.2.refs_0_, bf16[256,2048]{1,0:T(8,128)(2,1)} %refs_1_.3, bf16[256,2048]{1,0:T(8,128)(2,1)} %refs_2_.3, bf16[256,2048]{1,0:T(8,128)(2,1)} %refs_3_.3), custom_call_target="tpu_custom_call" | custom-call | flops 805306368 | bytes 4718592 | tf_op jit(solution)/shard_map/pallas_call | solution.py:80
  26.0 63.5 %all-to-all-done = bf16[16,32,3072]{2,1,0:T(8,128)(2,1)S(1)} async-done(((bf16[16,32,3072]{2,1,0:T(8,128)(2,1)}), bf16[16,32,3072]{2,1,0:T(8,128)(2,1)S(1)}, u32[]{:S(2)}, u32[]{:S(2)}) %all-to-all-start) | async-done | bytes 3145760 | tf_op jit(solution)/shard_map/all_to_all | solution.py:300
  89.5 0.0 copy-start.1
  89.5 1.7 copy-done.1
  91.2 5.1 all-to-all-start.1
  96.3 3.4 collective-permute-start
  99.7 3.4 collective-permute-start.1
  103.1 85.0 %collective-permute-done.kp_ref = bf16[256,2048]{1,0:T(8,128)(2,1)} collective-permute-done((bf16[256,2048]{1,0:T(8,128)(2,1)}, bf16[256,2048]{1,0:T(8,128)(2,1)}, u32[]{:S(2)}, u32[]{:S(2)}) %collective-permute-start) | collective-permute-done | bytes 1048608 | tf_op jit(solution)/shard_map/ppermute | solution.py:26
  188.1 20.3 %collective-permute-done.1.vp_ref = bf16[256,2048]{1,0:T(8,128)(2,1)} collective-permute-done((bf16[256,2048]{1,0:T(8,128)(2,1)}, bf16[256,2048]{1,0:T(8,128)(2,1)}, u32[]{:S(2)}, u32[]{:S(2)}) %collective-permute-start.1) | collective-permute-done | bytes 1048608 | tf_op jit(solution)/shard_map/ppermute | solution.py:26
  208.4 14.1 %shard_map.171.attn_ref = bf16[256,2048]{1,0:T(8,128)(2,1)} custom-call(bf16[256,2048]{1,0:T(8,128)(2,1)} %q_ref.3, bf16[256,2048]{1,0:T(8,128)(2,1)} %collective-permute-done.kp_ref, bf16[256,2048]{1,0:T(8,128)(2,1)} %k_ref.3, bf16[256,2048]{1,0:T(8,128)(2,1)} %collective-permute-done.1.vp_ref, bf16[256,2048]{1,0:T(8,128)(2,1)} %v_ref.3), custom_call_target="tpu_custom_call" | custom-call | flops 1073741824 | bytes 6291456 | tf_op jit(solution)/shard_map/pallas_call | solution.py:244
  222.5 13.1 %shard_map.174.attn_ref = bf16[512,1024]{1,0:T(8,128)(2,1)} custom-call(bf16[512,3072]{1,0:T(8,128)(2,1)} %bitcast.22), custom_call_target="tpu_custom_call" | custom-call | flops 805306368 | bytes 4194304 | tf_op jit(solution)/shard_map/pallas_call | solution.py:195
  235.5 0.0 all-to-all-done.1
  235.5 0.0 copy-start
  235.5 7.0 %all-to-all-start.3 = ((bf16[16,32,1024]{2,1,0:T(8,128)(2,1)}), bf16[16,32,1024]{2,1,0:T(8,128)(2,1)}, u32[]{:S(2)}, u32[]{:S(2)}) async-start(bf16[16,32,1024]{2,1,0:T(8,128)(2,1)} %bitcast.30), calls=%async_computation.3 | async-start | bytes 2097152 | tf_op jit(solution)/shard_map/all_to_all | solution.py:300
  242.6 0.0 copy-done
  242.6 0.0 copy-start.9
  242.6 13.1 %shard_map.173.attn_ref = bf16[512,1024]{1,0:T(8,128)(2,1)} custom-call(bf16[512,3072]{1,0:T(8,128)(2,1)} %bitcast.20), custom_call_target="tpu_custom_call" | custom-call | flops 805306368 | bytes 4194304 | tf_op jit(solution)/shard_map/pallas_call | solution.py:195
  255.7 0.0 copy-start.4
  255.7 0.0 copy-start.6
  255.7 10.0 %all-to-all-done.3 = bf16[16,32,1024]{2,1,0:T(8,128)(2,1)} async-done(((bf16[16,32,1024]{2,1,0:T(8,128)(2,1)}), bf16[16,32,1024]{2,1,0:T(8,128)(2,1)}, u32[]{:S(2)}, u32[]{:S(2)}) %all-to-all-start.3) | async-done | bytes 1048608 | tf_op jit(solution)/shard_map/all_to_all | solution.py:300
  265.6 5.6 all-to-all-start.2
  271.3 0.0 copy-done.9
  271.3 0.0 copy-done.4
  271.3 0.0 copy-done.6
  271.3 0.6 fusion
  271.9 6.1 %shard_map.175.refs_2_ = bf16[256,2048]{1,0:T(8,128)(2,1)} custom-call(s32[16,1,256]{2,1,0:T(1,128)} %broadcast_in_dim.2.refs_0_, bf16[512,1024]{1,0:T(8,128)(2,1)} %bitcast.7.refs_1_), custom_call_target="tpu_custom_call" | custom-call | flops 268435456 | bytes 1572864 | tf_op jit(solution)/shard_map/pallas_call | solution.py:105
  278.0 0.0 copy-start.5
  278.0 0.0 copy-start.10
  278.0 17.0 %all-to-all-done.2 = bf16[16,32,1024]{2,1,0:T(8,128)(2,1)} async-done(((bf16[16,32,1024]{2,1,0:T(8,128)(2,1)}), bf16[16,32,1024]{2,1,0:T(8,128)(2,1)}, u32[]{:S(2)}, u32[]{:S(2)}) %all-to-all-start.2) | async-done | bytes 1048608 | tf_op jit(solution)/shard_map/all_to_all | solution.py:300
  295.0 6.1 %shard_map.176 = bf16[256,2048]{1,0:T(8,128)(2,1)} custom-call(s32[16,1,256]{2,1,0:T(1,128)} %broadcast_in_dim.2.refs_0_, bf16[512,1024]{1,0:T(8,128)(2,1)} %bitcast.5.refs_1_, bf16[256,2048]{1,0:T(8,128)(2,1)} %shard_map.175.refs_2_), custom_call_target="tpu_custom_call", output_to_operand_aliasing={{}: (2, {})} | custom-call | flops 268435456 | bytes 1572864 | tf_op jit(solution)/shard_map/pallas_call | solution.py:105
  301.1 0.0 copy-done.5
  301.1 0.0 copy-done.10
  301.1 1.9 fusion.6
  303.1 2.5 psum.7
  305.6 0.0 copy-done.2
  305.6 4.7 fusion.11
  310.2 5.8 shard_map.179
  316.0 5.8 all-to-all-start.5
  321.9 5.9 shard_map.178
  327.8 18.9 %all-to-all-done.5 = bf16[16,32,1024]{2,1,0:T(8,128)(2,1)S(1)} async-done(((bf16[16,32,1024]{2,1,0:T(8,128)(2,1)}), bf16[16,32,1024]{2,1,0:T(8,128)(2,1)S(1)}, u32[]{:S(2)}, u32[]{:S(2)}) %all-to-all-start.5) | async-done | bytes 1048608 | tf_op jit(solution)/shard_map/all_to_all | solution.py:300
  346.7 6.0 %all-to-all-start.4 = ((bf16[16,32,1024]{2,1,0:T(8,128)(2,1)}), bf16[16,32,1024]{2,1,0:T(8,128)(2,1)S(1)}, u32[]{:S(2)}, u32[]{:S(2)}) async-start(bf16[16,32,1024]{2,1,0:T(8,128)(2,1)} %bitcast.31), calls=%async_computation.4 | async-start | bytes 2097152 | tf_op jit(solution)/shard_map/all_to_all | solution.py:300
  352.7 16.6 %shard_map.177 = (bf16[256,2048]{1,0:T(8,128)(2,1)}, f32[256,2048]{1,0:T(8,128)}, f32[256,2048]{1,0:T(8,128)}, bf16[256,2048]{1,0:T(8,128)(2,1)}, bf16[256,2048]{1,0:T(8,128)(2,1)}) custom-call(bf16[256,2048]{1,0:T(8,128)(2,1)} %q_ref.3, bf16[256,2048]{1,0:T(8,128)(2,1)} %collective-permute-done.kp_ref, bf16[256,2048]{1,0:T(8,128)(2,1)} %k_ref.3, ...), custom_call_target="tpu_custom_call" | custom-call | flops 2684354560 | bytes 14680064 | tf_op jit(solution)/shard_map/pallas_call | solution.py:258
  369.4 0.0 copy-done.8
  369.4 15.5 %shard_map.181 = bf16[512,3072]{1,0:T(8,128)(2,1)} custom-call(bf16[512,3072]{1,0:T(8,128)(2,1)} %bitcast.23, bf16[512,1024]{1,0:T(8,128)(2,1)} %shard_map.174.attn_ref, bf16[512,1024]{1,0:T(8,128)(2,1)} %bitcast.34), custom_call_target="tpu_custom_call" | custom-call | flops 805306368 | bytes 8388608 | tf_op jit(solution)/shard_map/pallas_call | solution.py:195
  384.9 0.0 all-to-all-done.4
  384.9 1.0 copy-done.7
  385.9 6.9 %all-to-all-start.7 = ((bf16[16,32,3072]{2,1,0:T(8,128)(2,1)}), bf16[16,32,3072]{2,1,0:T(8,128)(2,1)S(1)}, u32[]{:S(2)}, u32[]{:S(2)}) async-start(bf16[16,32,3072]{2,1,0:T(8,128)(2,1)} %bitcast.27), calls=%async_computation.7 | async-start | bytes 6291456 | tf_op jit(solution)/shard_map/all_to_all | solution.py:300
  392.8 2.5 collective-permute-start.2
  395.3 3.4 collective-permute-start.3
  398.7 85.4 %collective-permute-done.2 = bf16[256,2048]{1,0:T(8,128)(2,1)} collective-permute-done((bf16[256,2048]{1,0:T(8,128)(2,1)}, bf16[256,2048]{1,0:T(8,128)(2,1)}, u32[]{:S(2)}, u32[]{:S(2)}) %collective-permute-start.2) | collective-permute-done | bytes 1048608 | tf_op jit(solution)/shard_map/ppermute | solution.py:26
  484.1 21.5 %collective-permute-done.3 = bf16[256,2048]{1,0:T(8,128)(2,1)} collective-permute-done((bf16[256,2048]{1,0:T(8,128)(2,1)}, bf16[256,2048]{1,0:T(8,128)(2,1)}, u32[]{:S(2)}, u32[]{:S(2)}) %collective-permute-start.3) | collective-permute-done | bytes 1048608 | tf_op jit(solution)/shard_map/ppermute | solution.py:26
  505.5 15.5 %shard_map.180 = bf16[512,3072]{1,0:T(8,128)(2,1)} custom-call(bf16[512,3072]{1,0:T(8,128)(2,1)} %bitcast.21, bf16[512,1024]{1,0:T(8,128)(2,1)} %shard_map.173.attn_ref, bf16[512,1024]{1,0:T(8,128)(2,1)} %bitcast.33), custom_call_target="tpu_custom_call" | custom-call | flops 805306368 | bytes 8388608 | tf_op jit(solution)/shard_map/pallas_call | solution.py:195
  521.0 0.0 all-to-all-done.7
  521.0 1.7 copy-done.3
  522.8 5.1 all-to-all-start.6
  527.9 4.8 add_convert_fusion
  532.7 6.9 %shard_map.182 = (bf16[256,2048]{1,0:T(8,128)(2,1)}, bf16[256,2048]{1,0:T(8,128)(2,1)}, bf16[256,2048]{1,0:T(8,128)(2,1)}) custom-call(s32[16,1,256]{2,1,0:T(1,128)} %broadcast_in_dim.2.refs_0_, bf16[512,3072]{1,0:T(8,128)(2,1)} %bitcast.24), custom_call_target="tpu_custom_call" | custom-call | flops 805306368 | bytes 4718592 | tf_op jit(solution)/shard_map/pallas_call | solution.py:105
  539.6 58.0 %all-to-all-done.6 = bf16[16,32,3072]{2,1,0:T(8,128)(2,1)} async-done(((bf16[16,32,3072]{2,1,0:T(8,128)(2,1)}), bf16[16,32,3072]{2,1,0:T(8,128)(2,1)}, u32[]{:S(2)}, u32[]{:S(2)}) %all-to-all-start.6) | async-done | bytes 3145760 | tf_op jit(solution)/shard_map/all_to_all | solution.py:300
  597.6 6.9 %shard_map.183 = (bf16[256,2048]{1,0:T(8,128)(2,1)}, bf16[256,2048]{1,0:T(8,128)(2,1)}, bf16[256,2048]{1,0:T(8,128)(2,1)}) custom-call(s32[16,1,256]{2,1,0:T(1,128)} %broadcast_in_dim.2.refs_0_, bf16[512,3072]{1,0:T(8,128)(2,1)} %bitcast.17.refs_1_, ...), custom_call_target="tpu_custom_call", output_to_operand_aliasing={{0}: (2, {}), {1}: (3, {}), {2}: (4, {})} | custom-call | flops 805306368 | bytes 4718592 | tf_op jit(solution)/shard_map/pallas_call | solution.py:105
  (10 shorter events, 0.1 us)
Async XLA Ops:
  11.5 78.0 %all-to-all-start = ((bf16[16,32,3072]{2,1,0:T(8,128)(2,1)}), bf16[16,32,3072]{2,1,0:T(8,128)(2,1)S(1)}, u32[]{:S(2)}, u32[]{:S(2)}) async-start(bf16[16,32,3072]{2,1,0:T(8,128)(2,1)} %bitcast.26), calls=%async_computation | async-start | bytes 6291456 | tf_op jit(solution)/shard_map/all_to_all | solution.py:300
  89.5 1.7 copy-start.1
  91.2 144.3 %all-to-all-start.1 = ((bf16[16,32,3072]{2,1,0:T(8,128)(2,1)}), bf16[16,32,3072]{2,1,0:T(8,128)(2,1)S(1)}, u32[]{:S(2)}, u32[]{:S(2)}) async-start(bf16[16,32,3072]{2,1,0:T(8,128)(2,1)} %bitcast.25), calls=%async_computation.1 | async-start | bytes 6291456 | tf_op jit(solution)/shard_map/all_to_all | solution.py:300
  96.3 91.8 %collective-permute-start = (bf16[256,2048]{1,0:T(8,128)(2,1)}, bf16[256,2048]{1,0:T(8,128)(2,1)}, u32[]{:S(2)}, u32[]{:S(2)}) collective-permute-start(bf16[256,2048]{1,0:T(8,128)(2,1)} %k_ref.3), channel_id=1, source_target_pairs={{0,2},{2,4},{4,6},{6,8},{8,10},{10,12},{12,14},{14,16},{16,18},{18... | collective-permute-start | bytes 3145736 | tf_op jit(solution)/shard_map/ppermute | solution.py:26
  99.7 108.7 %collective-permute-start.1 = (bf16[256,2048]{1,0:T(8,128)(2,1)}, bf16[256,2048]{1,0:T(8,128)(2,1)}, u32[]{:S(2)}, u32[]{:S(2)}) collective-permute-start(bf16[256,2048]{1,0:T(8,128)(2,1)} %v_ref.3), channel_id=1, source_target_pairs={{0,2},{2,4},{4,6},{6,8},{8,10},{10,12},{12,14},{14,16},{16,18},{18... | collective-permute-start | bytes 3145736 | tf_op jit(solution)/shard_map/ppermute | solution.py:26
  235.5 7.0 %copy-start = (bf16[16,32,3072]{2,1,0:T(8,128)(2,1)}, bf16[16,32,3072]{2,1,0:T(8,128)(2,1)S(1)}, u32[]{:S(2)}) copy-start(bf16[16,32,3072]{2,1,0:T(8,128)(2,1)S(1)} %all-to-all-done.1) | copy-start | bytes 9437188
  235.5 30.1 %all-to-all-start.3 = ((bf16[16,32,1024]{2,1,0:T(8,128)(2,1)}), bf16[16,32,1024]{2,1,0:T(8,128)(2,1)}, u32[]{:S(2)}, u32[]{:S(2)}) async-start(bf16[16,32,1024]{2,1,0:T(8,128)(2,1)} %bitcast.30), calls=%async_computation.3 | async-start | bytes 2097152 | tf_op jit(solution)/shard_map/all_to_all | solution.py:300
  242.6 28.7 %copy-start.9 = (f32[2048]{0:T(1024)S(1)}, f32[2048]{0:T(1024)}, u32[]{:S(2)}) copy-start(f32[2048]{0:T(1024)} %param.18) | copy-start | bytes 24580
  255.7 15.6 %copy-start.4 = (bf16[256,2048]{1,0:T(8,128)(2,1)S(1)}, bf16[256,2048]{1,0:T(8,128)(2,1)}, u32[]{:S(2)}) copy-start(bf16[256,2048]{1,0:T(8,128)(2,1)} %shard_map.171.attn_ref) | copy-start | bytes 3145732
  255.7 15.6 %copy-start.6 = (bf16[256,2048]{1,0:T(8,128)(2,1)S(1)}, bf16[256,2048]{1,0:T(8,128)(2,1)}, u32[]{:S(2)}) copy-start(bf16[256,2048]{1,0:T(8,128)(2,1)} %param.20) | copy-start | bytes 3145732
  265.6 29.4 %all-to-all-start.2 = ((bf16[16,32,1024]{2,1,0:T(8,128)(2,1)}), bf16[16,32,1024]{2,1,0:T(8,128)(2,1)}, u32[]{:S(2)}, u32[]{:S(2)}) async-start(bf16[16,32,1024]{2,1,0:T(8,128)(2,1)} %bitcast.29), calls=%async_computation.2 | async-start | bytes 2097152 | tf_op jit(solution)/shard_map/all_to_all | solution.py:300
  278.0 23.2 %copy-start.5 = (bf16[256,2048]{1,0:T(8,128)(2,1)S(1)}, bf16[256,2048]{1,0:T(8,128)(2,1)}, u32[]{:S(2)}) copy-start(bf16[256,2048]{1,0:T(8,128)(2,1)} %param.21) | copy-start | bytes 3145732
  278.0 23.2 %copy-start.10 = (f32[2048]{0:T(1024)S(1)}, f32[2048]{0:T(1024)}, u32[]{:S(2)}) copy-start(f32[2048]{0:T(1024)} %param.19) | copy-start | bytes 24580
  301.1 4.4 copy-start.2
  316.0 30.6 %all-to-all-start.5 = ((bf16[16,32,1024]{2,1,0:T(8,128)(2,1)}), bf16[16,32,1024]{2,1,0:T(8,128)(2,1)S(1)}, u32[]{:S(2)}, u32[]{:S(2)}) async-start(bf16[16,32,1024]{2,1,0:T(8,128)(2,1)} %bitcast.32), calls=%async_computation.5 | async-start | bytes 2097152 | tf_op jit(solution)/shard_map/all_to_all | solution.py:300
  346.7 22.7 %copy-start.8 = (bf16[16,32,1024]{2,1,0:T(8,128)(2,1)}, bf16[16,32,1024]{2,1,0:T(8,128)(2,1)S(1)}, u32[]{:S(2)}) copy-start(bf16[16,32,1024]{2,1,0:T(8,128)(2,1)S(1)} %all-to-all-done.5) | copy-start | bytes 3145732
  346.7 38.2 %all-to-all-start.4 = ((bf16[16,32,1024]{2,1,0:T(8,128)(2,1)}), bf16[16,32,1024]{2,1,0:T(8,128)(2,1)S(1)}, u32[]{:S(2)}, u32[]{:S(2)}) async-start(bf16[16,32,1024]{2,1,0:T(8,128)(2,1)} %bitcast.31), calls=%async_computation.4 | async-start | bytes 2097152 | tf_op jit(solution)/shard_map/all_to_all | solution.py:300
  384.9 1.0 copy-start.7
  385.9 135.2 %all-to-all-start.7 = ((bf16[16,32,3072]{2,1,0:T(8,128)(2,1)}), bf16[16,32,3072]{2,1,0:T(8,128)(2,1)S(1)}, u32[]{:S(2)}, u32[]{:S(2)}) async-start(bf16[16,32,3072]{2,1,0:T(8,128)(2,1)} %bitcast.27), calls=%async_computation.7 | async-start | bytes 6291456 | tf_op jit(solution)/shard_map/all_to_all | solution.py:300
  392.8 91.3 %collective-permute-start.2 = (bf16[256,2048]{1,0:T(8,128)(2,1)}, bf16[256,2048]{1,0:T(8,128)(2,1)}, u32[]{:S(2)}, u32[]{:S(2)}) collective-permute-start(bf16[256,2048]{1,0:T(8,128)(2,1)} %get-tuple-element.33), channel_id=1, source_target_pairs={{2,0},{4,2},{6,4},{8,6},{10,8},{12,10},{14,12},{16,14},{18,16},{20... | collective-permute-start | bytes 3145736 | tf_op jit(solution)/shard_map/ppermute | solution.py:26
  395.3 110.3 %collective-permute-start.3 = (bf16[256,2048]{1,0:T(8,128)(2,1)}, bf16[256,2048]{1,0:T(8,128)(2,1)}, u32[]{:S(2)}, u32[]{:S(2)}) collective-permute-start(bf16[256,2048]{1,0:T(8,128)(2,1)} %get-tuple-element.34), channel_id=1, source_target_pairs={{2,0},{4,2},{6,4},{8,6},{10,8},{12,10},{14,12},{16,14},{18,16},{20... | collective-permute-start | bytes 3145736 | tf_op jit(solution)/shard_map/ppermute | solution.py:26
  521.0 1.7 copy-start.3
  522.8 74.8 %all-to-all-start.6 = ((bf16[16,32,3072]{2,1,0:T(8,128)(2,1)}), bf16[16,32,3072]{2,1,0:T(8,128)(2,1)}, u32[]{:S(2)}, u32[]{:S(2)}) async-start(bf16[16,32,3072]{2,1,0:T(8,128)(2,1)} %bitcast.28), calls=%async_computation.6 | async-start | bytes 6291456 | tf_op jit(solution)/shard_map/all_to_all | solution.py:300

commit v3 on v2

--- a/solution.py
+++ b/solution.py
@@ -13,6 +13,7 @@
 WINDOW = 256
 SLOTS = 128
 CHUNKS = 2
+GROUP = 4
 EMPTY = 1000.0
 
 EPSILON = 1e-06
@@ -20,10 +21,34 @@
 BF16 = jnp.bfloat16
 
 
-def from_behind(block, axis, distance):
-    devices = range(lax.axis_size(axis))
-    route = [(i - distance, i) for i in devices if i - distance in devices]
-    return lax.ppermute(block, axis, route)
+def permuted(block, routes):
+    size = lax.axis_size("seq")
+    return lax.ppermute(block, "seq", [(a, b) for a, b in routes if 0 <= min(a, b) and max(a, b) < size])
+
+
+def next_door(pair, step):
+    size = lax.axis_size("seq")
+    if size % GROUP or size == GROUP:
+        return tuple(permuted(x, [(i, i + step) for i in range(size)]) for x in pair)
+    bases = range(0, size, GROUP)
+    leave, enter = (GROUP - 1, 0) if step > 0 else (0, GROUP - 1)
+    place = lax.rem(lax.axis_index("seq"), GROUP)
+    straight = [(i, i + step) for i in range(size) if i // GROUP == (i + step) // GROUP]
+    near = [permuted(x, straight) for x in pair]
+    parts = GROUP // 2
+    rows = pair[0].shape[0] // parts
+    pieces = [x[i * rows : (i + 1) * rows] for x in pair for i in range(parts)]
+    spread = jnp.where(place == leave, pieces[leave], jnp.zeros_like(pieces[leave]))
+    for p in range(GROUP):
+        if p != leave:
+            spread = spread + permuted(pieces[p], [(b + leave, b + p) for b in bases])
+    crossed = permuted(spread, [(i, i + step * GROUP) for i in range(size)])
+    landed = [
+        crossed if p == enter else permuted(crossed, [(b + p, b + enter) for b in bases])
+        for p in range(GROUP)
+    ]
+    far = [jnp.concatenate(landed[i * parts : (i + 1) * parts], axis=0) for i in range(2)]
+    return tuple(jnp.where(place == enter, f, x) for f, x in zip(far, near))
 
 
 def nt(a, b):
@@ -314,7 +339,8 @@
         dispatch(slot_at, [clu_query, clu_key, clu_value], first, per, pool_size, True)
         for first in starts
     ]
-    before = (from_behind(win_key, "seq", 1), from_behind(win_value, "seq", 1))
+    before = next_door((win_key, win_value), 1)
+    sent_first[-1], before = lax.optimization_barrier((sent_first[-1], before))
     held = [exchange(part) for part in sent_first]
     attn_win = window_fwd(factor, win_query, win_key, win_value, before)
     held[0], attn_win = lax.optimization_barrier((held[0], attn_win))
@@ -352,17 +378,13 @@
         factor, win_query, win_key, win_value, before, attn_win, dout_win
     )
     grad_held[0], rim_key, rim_val = lax.optimization_barrier((grad_held[0], rim_key, rim_val))
-    after_key = from_behind(rim_key, "seq", -1)
-    after_val = from_behind(rim_val, "seq", -1)
-    grad_held[-1], after_key, after_val = lax.optimization_barrier(
-        (grad_held[-1], after_key, after_val)
-    )
-
+    after_key, after_val = next_door((rim_key, rim_val), -1)
     clu_grads = ()
     sent = [
         owner_call(owner_bwd_kernel, rows, factor, [qkv, part, grad], 3)
         for qkv, part, grad in zip(held, attn_held, grad_held)
     ]
+    sent[-1], after_key, after_val = lax.optimization_barrier((sent[-1], after_key, after_val))
     home = [exchange(part) for part in sent]
     win_dk = ((key_own + after_key) * factor).astype(BF16)
     win_dv = (val_own + after_val).astype(BF16)

time: 610 us -> 578 us (0.948)
  waiting for transfers between devices: 380 us -> 287 us
  starting transfers between devices: 61.4 us -> 101 us
  other arithmetic: 14.9 us -> 28.5 us
  local copies, waits for them, and re-layouts: 5.02 us -> 11.6 us
    ppermute x4 -> x18, waiting for transfers between devices: 212 us -> 137 us  [permuted(): lax.ppermute(block, 'seq', [(a, b) for a, b in routes if 0 <= min(a, b) a...]
    ppermute x4 -> x18, starting transfers between devices: 12.6 us -> 36.5 us  [permuted(): lax.ppermute(block, 'seq', [(a, b) for a, b in routes if 0 <= min(a, b) a...]
    all_to_all x8, waiting for transfers between devices: 167 us -> 150 us  [exchange(): lax.all_to_all(shaped, 'seq', split_axis=0, concat_axis=0, tiled=True)]
    all_to_all x8, starting transfers between devices: 48.8 us -> 64.9 us  [exchange(): lax.all_to_all(shaped, 'seq', split_axis=0, concat_axis=0, tiled=True)]
    select_n x0 -> x4, other arithmetic: none -> 10.9 us  [next_door(): return tuple((jnp.where(place == enter, f, x) for f, x in zip(far, near)))]
    slice x0 -> x4, local copies, waits for them, and re-layouts: none -> 6.5 us  [next_door(): pieces = [x[i * rows:(i + 1) * rows] for x in pair for i in range(parts)]]
  transfers between devices with their start and end apart: 12 -> 26, of which waited for: 9 -> 11; matrix products, arithmetic and copies ran while one was open for 1% -> 4% of each run, Pallas kernels for 19% -> 20%
where the time goes in v3:
time: 578 us; the launch traced here: 572 us
  waiting for transfers between devices  287 us (50%)
  Pallas kernels  140 us (24%)
  starting transfers between devices  101 us (17%)
  other arithmetic  28.5 us (5%)
  local copies, waits for them, and re-layouts  11.6 us (2%)
    all_to_all x8, waiting for transfers between devices, exchange(): lax.all_to_all(shaped, 'seq', split_axis=0, concat_axis=0, tiled=True)  150 us
    ppermute x18, waiting for transfers between devices, permuted(): lax.ppermute(block, 'seq', [(a, b) for a, b in routes if 0 <= min(a, b) a...  137 us
    all_to_all x8, starting transfers between devices, exchange(): lax.all_to_all(shaped, 'seq', split_axis=0, concat_axis=0, tiled=True)  64.9 us
    pallas_call x4, Pallas kernels, owner_call(): call(functools.partial(kernel, rows, factor), (count,), [pl.BlockSpec((po...  57.1 us
    ppermute x18, starting transfers between devices, permuted(): lax.ppermute(block, 'seq', [(a, b) for a, b in routes if 0 <= min(a, b) a...  36.5 us
    pallas_call x4, Pallas kernels, dispatch(): call(functools.partial(dispatch_kernel, mark), (count,), [pl.BlockSpec((1...  26.5 us
    pallas_call x4, Pallas kernels, collect(): call(functools.partial(collect_kernel, n_out), (count,), [pl.BlockSpec((1...  26.1 us
    pallas_call x1, Pallas kernels, window_bwd(): call(functools.partial(window_bwd_kernel, factor), (wide // DH,), [here]...  16.7 us
  transfers between devices with their start and end apart: 26, of which 11 were waited for; matrix products, arithmetic and copies ran while one was open for 4% of the time, Pallas kernels for 20%

profile of v3, /device:TPU:14, one launch (start us, length us, event | category | flops | bytes accessed | tf_op | source)
XLA Modules:
  0.0 572.1 jit_solution(3380158910200811778)
XLA Ops:
  0.7 2.1 convert_reduce_fusion
  4.1 7.4 %shard_map.170 = bf16[512,3072]{1,0:T(8,128)(2,1)} custom-call(s32[16,1,256]{2,1,0:T(1,128)} %broadcast_in_dim.2.refs_0_, bf16[256,2048]{1,0:T(8,128)(2,1)} %refs_1_.3, bf16[256,2048]{1,0:T(8,128)(2,1)} %refs_2_.3, bf16[256,2048]{1,0:T(8,128)(2,1)} %refs_3_.3), custom_call_target="tpu_custom_call" | custom-call | flops 805306368 | bytes 4718592 | tf_op jit(solution)/shard_map/pallas_call | solution.py:105
  11.5 7.1 %all-to-all-start = ((bf16[16,32,3072]{2,1,0:T(8,128)(2,1)}), bf16[16,32,3072]{2,1,0:T(8,128)(2,1)S(1)}, u32[]{:S(2)}, u32[]{:S(2)}) async-start(bf16[16,32,3072]{2,1,0:T(8,128)(2,1)} %bitcast.23), calls=%async_computation | async-start | bytes 6291456 | tf_op jit(solution)/shard_map/all_to_all | solution.py:325
  18.7 1.9 slice.33
  20.6 3.3 collective-permute-start.2
  23.8 2.3 fusion.17
  26.1 2.1 collective-permute-start
  28.2 2.1 collective-permute-start.1
  30.3 1.3 collective-permute-start.5
  31.6 8.2 %collective-permute-done.2 = bf16[128,2048]{1,0:T(8,128)(2,1)} collective-permute-done((bf16[128,2048]{1,0:T(8,128)(2,1)}, bf16[128,2048]{1,0:T(8,128)(2,1)}, u32[]{:S(2)}, u32[]{:S(2)}) %collective-permute-start.2) | collective-permute-done | bytes 524320 | tf_op jit(solution)/shard_map/ppermute | solution.py:26
  39.7 32.7 %collective-permute-done = bf16[128,2048]{1,0:T(8,128)(2,1)} collective-permute-done((bf16[128,2048]{1,0:T(8,128)(2,1)}, bf16[128,2048]{1,0:T(8,128)(2,1)}, u32[]{:S(2)}, u32[]{:S(2)}) %collective-permute-start) | collective-permute-done | bytes 524320 | tf_op jit(solution)/shard_map/ppermute | solution.py:26
  72.4 1.6 add_add_fusion.1
  74.0 4.6 collective-permute-start.3
  78.7 1.3 collective-permute-start.8
  80.0 18.4 %collective-permute-done.3 = bf16[128,2048]{1,0:T(8,128)(2,1)} collective-permute-done((bf16[128,2048]{1,0:T(8,128)(2,1)S(1)}, bf16[128,2048]{1,0:T(8,128)(2,1)}, u32[]{:S(2)}, u32[]{:S(2)}) %collective-permute-start.3) | collective-permute-done | bytes 524320 | tf_op jit(solution)/shard_map/ppermute | solution.py:26
  98.4 1.4 collective-permute-start.4
  99.8 5.8 %collective-permute-start.7 = (bf16[128,2048]{1,0:T(8,128)(2,1)}, bf16[128,2048]{1,0:T(8,128)(2,1)}, u32[]{:S(2)}, u32[]{:S(2)}) collective-permute-start(bf16[128,2048]{1,0:T(8,128)(2,1)} %collective-permute-done.3), channel_id=1, source_target_pairs={{6,0},{14,8},{22,16},{30,24},{7,1},{15,9},{23,17},{31,25}} | collective-permute-start | bytes 1572872 | tf_op jit(solution)/shard_map/ppermute | solution.py:26
  105.6 1.5 collective-permute-start.6
  107.1 7.4 %shard_map.171 = bf16[512,3072]{1,0:T(8,128)(2,1)} custom-call(s32[16,1,256]{2,1,0:T(1,128)} %broadcast_in_dim.2.refs_0_, bf16[256,2048]{1,0:T(8,128)(2,1)} %refs_1_.3, bf16[256,2048]{1,0:T(8,128)(2,1)} %refs_2_.3, bf16[256,2048]{1,0:T(8,128)(2,1)} %refs_3_.3), custom_call_target="tpu_custom_call" | custom-call | flops 805306368 | bytes 4718592 | tf_op jit(solution)/shard_map/pallas_call | solution.py:105
  114.5 2.9 maximum_select_fusion.kp_ref
  117.4 3.0 maximum_select_fusion.1.vp_ref
  120.4 1.7 copy-done
  122.1 16.8 %all-to-all-start.1 = ((bf16[16,32,3072]{2,1,0:T(8,128)(2,1)}), bf16[16,32,3072]{2,1,0:T(8,128)(2,1)}, u32[]{:S(2)}, u32[]{:S(2)}) async-start(bf16[16,32,3072]{2,1,0:T(8,128)(2,1)} %bitcast.24), calls=%async_computation.1 | async-start | bytes 6291456 | tf_op jit(solution)/shard_map/all_to_all | solution.py:325
  138.9 14.1 %shard_map.172.attn_ref = bf16[256,2048]{1,0:T(8,128)(2,1)} custom-call(bf16[256,2048]{1,0:T(8,128)(2,1)} %q_ref.3, bf16[256,2048]{1,0:T(8,128)(2,1)} %maximum_select_fusion.kp_ref, bf16[256,2048]{1,0:T(8,128)(2,1)} %k_ref.3, bf16[256,2048]{1,0:T(8,128)(2,1)} %maximum_select_fusion.1.vp_ref, bf16[256,2048]{1,0:T(8,128)(2,1)} %v_ref.3), custom_call_target="tpu_custom_call" | custom-call | flops 1073741824 | bytes 6291456 | tf_op jit(solution)/shard_map/pallas_call | solution.py:269
  153.0 13.1 %shard_map.174.attn_ref = bf16[512,1024]{1,0:T(8,128)(2,1)} custom-call(bf16[512,3072]{1,0:T(8,128)(2,1)} %bitcast.20), custom_call_target="tpu_custom_call" | custom-call | flops 805306368 | bytes 4194304 | tf_op jit(solution)/shard_map/pallas_call | solution.py:220
  166.0 44.3 %all-to-all-done.1 = bf16[16,32,3072]{2,1,0:T(8,128)(2,1)} async-done(((bf16[16,32,3072]{2,1,0:T(8,128)(2,1)}), bf16[16,32,3072]{2,1,0:T(8,128)(2,1)}, u32[]{:S(2)}, u32[]{:S(2)}) %all-to-all-start.1) | async-done | bytes 3145760 | tf_op jit(solution)/shard_map/all_to_all | solution.py:325
  210.3 5.1 all-to-all-start.3
  215.5 13.1 %shard_map.173.attn_ref = bf16[512,1024]{1,0:T(8,128)(2,1)} custom-call(bf16[512,3072]{1,0:T(8,128)(2,1)} %bitcast.3.qkv_ref), custom_call_target="tpu_custom_call" | custom-call | flops 805306368 | bytes 4194304 | tf_op jit(solution)/shard_map/pallas_call | solution.py:220
  228.5 10.6 %all-to-all-done.3 = bf16[16,32,1024]{2,1,0:T(8,128)(2,1)S(1)} async-done(((bf16[16,32,1024]{2,1,0:T(8,128)(2,1)}), bf16[16,32,1024]{2,1,0:T(8,128)(2,1)S(1)}, u32[]{:S(2)}, u32[]{:S(2)}) %all-to-all-start.3) | async-done | bytes 1048608 | tf_op jit(solution)/shard_map/all_to_all | solution.py:325
  239.2 5.8 %all-to-all-start.2 = ((bf16[16,32,1024]{2,1,0:T(8,128)(2,1)}), bf16[16,32,1024]{2,1,0:T(8,128)(2,1)}, u32[]{:S(2)}, u32[]{:S(2)}) async-start(bf16[16,32,1024]{2,1,0:T(8,128)(2,1)} %bitcast.27), calls=%async_computation.2 | async-start | bytes 2097152 | tf_op jit(solution)/shard_map/all_to_all | solution.py:325
  245.6 6.1 %shard_map.175.refs_2_ = bf16[256,2048]{1,0:T(8,128)(2,1)} custom-call(s32[16,1,256]{2,1,0:T(1,128)} %broadcast_in_dim.2.refs_0_, bf16[512,1024]{1,0:T(8,128)(2,1)} %bitcast.30), custom_call_target="tpu_custom_call" | custom-call | flops 268435456 | bytes 1572864 | tf_op jit(solution)/shard_map/pallas_call | solution.py:130
  251.7 16.5 %all-to-all-done.2 = bf16[16,32,1024]{2,1,0:T(8,128)(2,1)} async-done(((bf16[16,32,1024]{2,1,0:T(8,128)(2,1)}), bf16[16,32,1024]{2,1,0:T(8,128)(2,1)}, u32[]{:S(2)}, u32[]{:S(2)}) %all-to-all-start.2) | async-done | bytes 1048608 | tf_op jit(solution)/shard_map/all_to_all | solution.py:325
  268.3 6.1 %shard_map.176 = bf16[256,2048]{1,0:T(8,128)(2,1)} custom-call(s32[16,1,256]{2,1,0:T(1,128)} %broadcast_in_dim.2.refs_0_, bf16[512,1024]{1,0:T(8,128)(2,1)} %bitcast.5.refs_1_, bf16[256,2048]{1,0:T(8,128)(2,1)} %shard_map.175.refs_2_), custom_call_target="tpu_custom_call", output_to_operand_aliasing={{}: (2, {})} | custom-call | flops 268435456 | bytes 1572864 | tf_op jit(solution)/shard_map/pallas_call | solution.py:130
  274.4 1.9 fusion.6
  276.4 2.5 psum.7
  278.9 4.7 fusion.11
  283.5 5.8 %shard_map.180 = bf16[512,1024]{1,0:T(8,128)(2,1)} custom-call(s32[16,1,256]{2,1,0:T(1,128)} %broadcast_in_dim.2.refs_0_, bf16[256,2048]{1,0:T(8,128)(2,1)} %get-tuple-element.56.refs_1_), custom_call_target="tpu_custom_call" | custom-call | flops 268435456 | bytes 1572864 | tf_op jit(solution)/shard_map/pallas_call | solution.py:105
  289.3 5.8 %all-to-all-start.5 = ((bf16[16,32,1024]{2,1,0:T(8,128)(2,1)}), bf16[16,32,1024]{2,1,0:T(8,128)(2,1)S(1)}, u32[]{:S(2)}, u32[]{:S(2)}) async-start(bf16[16,32,1024]{2,1,0:T(8,128)(2,1)} %bitcast.31), calls=%async_computation.5 | async-start | bytes 2097152 | tf_op jit(solution)/shard_map/all_to_all | solution.py:325
  295.2 5.9 %shard_map.178 = bf16[512,1024]{1,0:T(8,128)(2,1)} custom-call(s32[16,1,256]{2,1,0:T(1,128)} %broadcast_in_dim.2.refs_0_, bf16[256,2048]{1,0:T(8,128)(2,1)} %get-tuple-element.56.refs_1_), custom_call_target="tpu_custom_call" | custom-call | flops 268435456 | bytes 1572864 | tf_op jit(solution)/shard_map/pallas_call | solution.py:105
  301.0 19.0 %all-to-all-done.5 = bf16[16,32,1024]{2,1,0:T(8,128)(2,1)S(1)} async-done(((bf16[16,32,1024]{2,1,0:T(8,128)(2,1)}), bf16[16,32,1024]{2,1,0:T(8,128)(2,1)S(1)}, u32[]{:S(2)}, u32[]{:S(2)}) %all-to-all-start.5) | async-done | bytes 1048608 | tf_op jit(solution)/shard_map/all_to_all | solution.py:325
  320.0 6.0 %all-to-all-start.4 = ((bf16[16,32,1024]{2,1,0:T(8,128)(2,1)}), bf16[16,32,1024]{2,1,0:T(8,128)(2,1)S(1)}, u32[]{:S(2)}, u32[]{:S(2)}) async-start(bf16[16,32,1024]{2,1,0:T(8,128)(2,1)} %bitcast.29), calls=%async_computation.4 | async-start | bytes 2097152 | tf_op jit(solution)/shard_map/all_to_all | solution.py:325
  326.0 16.7 %shard_map.177 = (bf16[256,2048]{1,0:T(8,128)(2,1)}, f32[256,2048]{1,0:T(8,128)}, f32[256,2048]{1,0:T(8,128)}, bf16[256,2048]{1,0:T(8,128)(2,1)}, bf16[256,2048]{1,0:T(8,128)(2,1)}) custom-call(bf16[256,2048]{1,0:T(8,128)(2,1)} %q_ref.3, bf16[256,2048]{1,0:T(8,128)(2,1)} %maximum_select_fusion.kp_ref, bf16[256,2048]{1,0:T(8,128)(2,1)} %k_ref.3, ...), custom_call_target="tpu_custom_call" | custom-call | flops 2684354560 | bytes 14680064 | tf_op jit(solution)/shard_map/pallas_call | solution.py:283
  342.7 15.5 %shard_map.181 = bf16[512,3072]{1,0:T(8,128)(2,1)} custom-call(bf16[512,3072]{1,0:T(8,128)(2,1)} %bitcast.21, bf16[512,1024]{1,0:T(8,128)(2,1)} %shard_map.174.attn_ref, bf16[512,1024]{1,0:T(8,128)(2,1)} %bitcast.33), custom_call_target="tpu_custom_call" | custom-call | flops 805306368 | bytes 8388608 | tf_op jit(solution)/shard_map/pallas_call | solution.py:220
  359.1 6.9 %all-to-all-start.7 = ((bf16[16,32,3072]{2,1,0:T(8,128)(2,1)}), bf16[16,32,3072]{2,1,0:T(8,128)(2,1)S(1)}, u32[]{:S(2)}, u32[]{:S(2)}) async-start(bf16[16,32,3072]{2,1,0:T(8,128)(2,1)} %bitcast.25), calls=%async_computation.7 | async-start | bytes 6291456 | tf_op jit(solution)/shard_map/all_to_all | solution.py:325
  367.8 1.3 fusion.16
  369.8 1.3 collective-permute-start.11
  371.1 42.5 %collective-permute-done.11 = bf16[128,2048]{1,0:T(8,128)(2,1)S(1)} collective-permute-done((bf16[128,2048]{1,0:T(8,128)(2,1)S(1)}, bf16[128,2048]{1,0:T(8,128)(2,1)S(1)}, u32[]{:S(2)}, u32[]{:S(2)}) %collective-permute-start.11) | collective-permute-done | bytes 524320 | tf_op jit(solution)/shard_map/ppermute | solution.py:26
  414.8 2.1 collective-permute-start.12
  416.9 2.3 collective-permute-start.17
  419.1 2.3 collective-permute-start.15
  421.4 23.7 %collective-permute-done.12 = bf16[128,2048]{1,0:T(8,128)(2,1)S(1)} collective-permute-done((bf16[128,2048]{1,0:T(8,128)(2,1)S(1)}, bf16[128,2048]{1,0:T(8,128)(2,1)S(1)}, u32[]{:S(2)}, u32[]{:S(2)}) %collective-permute-start.12) | collective-permute-done | bytes 524320 | tf_op jit(solution)/shard_map/ppermute | solution.py:26
  445.1 1.3 collective-permute-start.16
  446.3 1.3 collective-permute-start.14
  447.6 1.3 collective-permute-start.13
  448.9 15.5 %shard_map.179 = bf16[512,3072]{1,0:T(8,128)(2,1)} custom-call(bf16[512,3072]{1,0:T(8,128)(2,1)} %bitcast.3.qkv_ref, bf16[512,1024]{1,0:T(8,128)(2,1)} %shard_map.173.attn_ref, bf16[512,1024]{1,0:T(8,128)(2,1)} %bitcast.32), custom_call_target="tpu_custom_call" | custom-call | flops 805306368 | bytes 8388608 | tf_op jit(solution)/shard_map/pallas_call | solution.py:220
  464.5 11.3 %collective-permute-done.16 = bf16[128,2048]{1,0:T(8,128)(2,1)} collective-permute-done((bf16[128,2048]{1,0:T(8,128)(2,1)S(1)}, bf16[128,2048]{1,0:T(8,128)(2,1)}, u32[]{:S(2)}, u32[]{:S(2)}) %collective-permute-start.16) | collective-permute-done | bytes 524320 | tf_op jit(solution)/shard_map/ppermute | solution.py:26
  475.8 2.4 maximum_select_fusion.3
  478.2 2.6 maximum_select_fusion.2
  480.8 1.8 copy-done.2
  482.5 11.2 %all-to-all-start.6 = ((bf16[16,32,3072]{2,1,0:T(8,128)(2,1)}), bf16[16,32,3072]{2,1,0:T(8,128)(2,1)}, u32[]{:S(2)}, u32[]{:S(2)}) async-start(bf16[16,32,3072]{2,1,0:T(8,128)(2,1)} %bitcast.26), calls=%async_computation.6 | async-start | bytes 6291456 | tf_op jit(solution)/shard_map/all_to_all | solution.py:325
  493.8 4.8 add_convert_fusion
  498.6 6.9 %shard_map.182 = (bf16[256,2048]{1,0:T(8,128)(2,1)}, bf16[256,2048]{1,0:T(8,128)(2,1)}, bf16[256,2048]{1,0:T(8,128)(2,1)}) custom-call(s32[16,1,256]{2,1,0:T(1,128)} %broadcast_in_dim.2.refs_0_, bf16[512,3072]{1,0:T(8,128)(2,1)} %bitcast.22), custom_call_target="tpu_custom_call" | custom-call | flops 805306368 | bytes 4718592 | tf_op jit(solution)/shard_map/pallas_call | solution.py:130
  505.6 59.6 %all-to-all-done.6 = bf16[16,32,3072]{2,1,0:T(8,128)(2,1)} async-done(((bf16[16,32,3072]{2,1,0:T(8,128)(2,1)}), bf16[16,32,3072]{2,1,0:T(8,128)(2,1)}, u32[]{:S(2)}, u32[]{:S(2)}) %all-to-all-start.6) | async-done | bytes 3145760 | tf_op jit(solution)/shard_map/all_to_all | solution.py:325
  565.2 6.9 %shard_map.183 = (bf16[256,2048]{1,0:T(8,128)(2,1)}, bf16[256,2048]{1,0:T(8,128)(2,1)}, bf16[256,2048]{1,0:T(8,128)(2,1)}) custom-call(s32[16,1,256]{2,1,0:T(1,128)} %broadcast_in_dim.2.refs_0_, bf16[512,3072]{1,0:T(8,128)(2,1)} %bitcast.17.refs_1_, ...), custom_call_target="tpu_custom_call", output_to_operand_aliasing={{0}: (2, {}), {1}: (3, {}), {2}: (4, {})} | custom-call | flops 805306368 | bytes 4718592 | tf_op jit(solution)/shard_map/pallas_call | solution.py:130
  (48 shorter events, 6.6 us)
Async XLA Ops:
  11.5 108.8 %all-to-all-start = ((bf16[16,32,3072]{2,1,0:T(8,128)(2,1)}), bf16[16,32,3072]{2,1,0:T(8,128)(2,1)S(1)}, u32[]{:S(2)}, u32[]{:S(2)}) async-start(bf16[16,32,3072]{2,1,0:T(8,128)(2,1)} %bitcast.23), calls=%async_computation | async-start | bytes 6291456 | tf_op jit(solution)/shard_map/all_to_all | solution.py:325
  20.6 19.2 %collective-permute-start.2 = (bf16[128,2048]{1,0:T(8,128)(2,1)}, bf16[128,2048]{1,0:T(8,128)(2,1)}, u32[]{:S(2)}, u32[]{:S(2)}) collective-permute-start(bf16[128,2048]{1,0:T(8,128)(2,1)} %slice.33), channel_id=1, source_target_pairs={{6,4},{14,12},{22,20},{30,28},{7,5},{15,13},{23,21},{31,29}} | collective-permute-start | bytes 1572872 | tf_op jit(solution)/shard_map/ppermute | solution.py:26
  26.1 46.3 %collective-permute-start = (bf16[128,2048]{1,0:T(8,128)(2,1)}, bf16[128,2048]{1,0:T(8,128)(2,1)}, u32[]{:S(2)}, u32[]{:S(2)}) collective-permute-start(bf16[128,2048]{1,0:T(8,128)(2,1)} %get-tuple-element.62), channel_id=1, source_target_pairs={{6,0},{14,8},{22,16},{30,24},{7,1},{15,9},{23,17},{31,25}} | collective-permute-start | bytes 1572872 | tf_op jit(solution)/shard_map/ppermute | solution.py:26
  28.2 44.2 %collective-permute-start.1 = (bf16[128,2048]{1,0:T(8,128)(2,1)}, bf16[128,2048]{1,0:T(8,128)(2,1)}, u32[]{:S(2)}, u32[]{:S(2)}) collective-permute-start(bf16[128,2048]{1,0:T(8,128)(2,1)} %get-tuple-element.63), channel_id=1, source_target_pairs={{6,2},{14,10},{22,18},{30,26},{7,3},{15,11},{23,19},{31,27}} | collective-permute-start | bytes 1572872 | tf_op jit(solution)/shard_map/ppermute | solution.py:26
  30.3 84.2 %collective-permute-start.5 = (bf16[256,2048]{1,0:T(8,128)(2,1)}, bf16[256,2048]{1,0:T(8,128)(2,1)}, u32[]{:S(2)}, u32[]{:S(2)}) collective-permute-start(bf16[256,2048]{1,0:T(8,128)(2,1)} %k_ref.3), channel_id=1, source_target_pairs={{0,2},{2,4},{4,6},{8,10},{10,12},{12,14},{16,18},{18,20},{20,22},{... | collective-permute-start | bytes 3145736 | tf_op jit(solution)/shard_map/ppermute | solution.py:26
  74.0 24.4 %collective-permute-start.3 = (bf16[128,2048]{1,0:T(8,128)(2,1)S(1)}, bf16[128,2048]{1,0:T(8,128)(2,1)}, u32[]{:S(2)}, u32[]{:S(2)}) collective-permute-start(bf16[128,2048]{1,0:T(8,128)(2,1)S(1)} %add_add_fusion.1), channel_id=1, source_target_pairs={{0,8},{2,10},{4,12},{6,14},{8,16},{10,18},{12,20},{14,22},{16,24},... | collective-permute-start | bytes 1572872 | tf_op jit(solution)/shard_map/ppermute | solution.py:26
  78.7 38.7 %collective-permute-start.8 = (bf16[256,2048]{1,0:T(8,128)(2,1)}, bf16[256,2048]{1,0:T(8,128)(2,1)}, u32[]{:S(2)}, u32[]{:S(2)}) collective-permute-start(bf16[256,2048]{1,0:T(8,128)(2,1)} %v_ref.3), channel_id=1, source_target_pairs={{0,2},{2,4},{4,6},{8,10},{10,12},{12,14},{16,18},{18,20},{20,22},{... | collective-permute-start | bytes 3145736 | tf_op jit(solution)/shard_map/ppermute | solution.py:26
  98.4 16.1 %collective-permute-start.4 = (bf16[128,2048]{1,0:T(8,128)(2,1)}, bf16[128,2048]{1,0:T(8,128)(2,1)}, u32[]{:S(2)}, u32[]{:S(2)}) collective-permute-start(bf16[128,2048]{1,0:T(8,128)(2,1)} %collective-permute-done.3), channel_id=1, source_target_pairs={{2,0},{10,8},{18,16},{26,24},{3,1},{11,9},{19,17},{27,25}} | collective-permute-start | bytes 1572872 | tf_op jit(solution)/shard_map/ppermute | solution.py:26
  99.8 17.5 %collective-permute-start.7 = (bf16[128,2048]{1,0:T(8,128)(2,1)}, bf16[128,2048]{1,0:T(8,128)(2,1)}, u32[]{:S(2)}, u32[]{:S(2)}) collective-permute-start(bf16[128,2048]{1,0:T(8,128)(2,1)} %collective-permute-done.3), channel_id=1, source_target_pairs={{6,0},{14,8},{22,16},{30,24},{7,1},{15,9},{23,17},{31,25}} | collective-permute-start | bytes 1572872 | tf_op jit(solution)/shard_map/ppermute | solution.py:26
  105.6 11.8 %collective-permute-start.6 = (bf16[128,2048]{1,0:T(8,128)(2,1)}, bf16[128,2048]{1,0:T(8,128)(2,1)}, u32[]{:S(2)}, u32[]{:S(2)}) collective-permute-start(bf16[128,2048]{1,0:T(8,128)(2,1)} %collective-permute-done.3), channel_id=1, source_target_pairs={{4,0},{12,8},{20,16},{28,24},{5,1},{13,9},{21,17},{29,25}} | collective-permute-start | bytes 1572872 | tf_op jit(solution)/shard_map/ppermute | solution.py:26
  120.4 1.7 copy-start
  122.1 88.3 %all-to-all-start.1 = ((bf16[16,32,3072]{2,1,0:T(8,128)(2,1)}), bf16[16,32,3072]{2,1,0:T(8,128)(2,1)}, u32[]{:S(2)}, u32[]{:S(2)}) async-start(bf16[16,32,3072]{2,1,0:T(8,128)(2,1)} %bitcast.24), calls=%async_computation.1 | async-start | bytes 6291456 | tf_op jit(solution)/shard_map/all_to_all | solution.py:325
  210.3 28.8 %all-to-all-start.3 = ((bf16[16,32,1024]{2,1,0:T(8,128)(2,1)}), bf16[16,32,1024]{2,1,0:T(8,128)(2,1)S(1)}, u32[]{:S(2)}, u32[]{:S(2)}) async-start(bf16[16,32,1024]{2,1,0:T(8,128)(2,1)} %bitcast.28), calls=%async_computation.3 | async-start | bytes 2097152 | tf_op jit(solution)/shard_map/all_to_all | solution.py:325
  215.5 29.6 %copy-start.9 = (f32[2048]{0:T(1024)S(1)}, f32[2048]{0:T(1024)}, u32[]{:S(2)}) copy-start(f32[2048]{0:T(1024)} %param.18) | copy-start | bytes 24580
  228.5 16.5 %copy-start.3 = (bf16[256,2048]{1,0:T(8,128)(2,1)S(1)}, bf16[256,2048]{1,0:T(8,128)(2,1)}, u32[]{:S(2)}) copy-start(bf16[256,2048]{1,0:T(8,128)(2,1)} %shard_map.172.attn_ref) | copy-start | bytes 3145732
  228.5 16.5 %copy-start.5 = (bf16[256,2048]{1,0:T(8,128)(2,1)S(1)}, bf16[256,2048]{1,0:T(8,128)(2,1)}, u32[]{:S(2)}) copy-start(bf16[256,2048]{1,0:T(8,128)(2,1)} %param.20) | copy-start | bytes 3145732
  239.2 6.4 %copy-start.6 = (bf16[16,32,1024]{2,1,0:T(8,128)(2,1)}, bf16[16,32,1024]{2,1,0:T(8,128)(2,1)S(1)}, u32[]{:S(2)}) copy-start(bf16[16,32,1024]{2,1,0:T(8,128)(2,1)S(1)} %all-to-all-done.3) | copy-start | bytes 3145732
  239.2 29.1 %all-to-all-start.2 = ((bf16[16,32,1024]{2,1,0:T(8,128)(2,1)}), bf16[16,32,1024]{2,1,0:T(8,128)(2,1)}, u32[]{:S(2)}, u32[]{:S(2)}) async-start(bf16[16,32,1024]{2,1,0:T(8,128)(2,1)} %bitcast.27), calls=%async_computation.2 | async-start | bytes 2097152 | tf_op jit(solution)/shard_map/all_to_all | solution.py:325
  251.7 22.7 %copy-start.4 = (bf16[256,2048]{1,0:T(8,128)(2,1)S(1)}, bf16[256,2048]{1,0:T(8,128)(2,1)}, u32[]{:S(2)}) copy-start(bf16[256,2048]{1,0:T(8,128)(2,1)} %param.21) | copy-start | bytes 3145732
  251.7 22.7 %copy-start.10 = (f32[2048]{0:T(1024)S(1)}, f32[2048]{0:T(1024)}, u32[]{:S(2)}) copy-start(f32[2048]{0:T(1024)} %param.19) | copy-start | bytes 24580
  274.4 4.4 copy-start.1
  289.3 30.6 %all-to-all-start.5 = ((bf16[16,32,1024]{2,1,0:T(8,128)(2,1)}), bf16[16,32,1024]{2,1,0:T(8,128)(2,1)S(1)}, u32[]{:S(2)}, u32[]{:S(2)}) async-start(bf16[16,32,1024]{2,1,0:T(8,128)(2,1)} %bitcast.31), calls=%async_computation.5 | async-start | bytes 2097152 | tf_op jit(solution)/shard_map/all_to_all | solution.py:325
  320.0 22.7 %copy-start.8 = (bf16[16,32,1024]{2,1,0:T(8,128)(2,1)}, bf16[16,32,1024]{2,1,0:T(8,128)(2,1)S(1)}, u32[]{:S(2)}) copy-start(bf16[16,32,1024]{2,1,0:T(8,128)(2,1)S(1)} %all-to-all-done.5) | copy-start | bytes 3145732
  320.0 38.2 %all-to-all-start.4 = ((bf16[16,32,1024]{2,1,0:T(8,128)(2,1)}), bf16[16,32,1024]{2,1,0:T(8,128)(2,1)S(1)}, u32[]{:S(2)}, u32[]{:S(2)}) async-start(bf16[16,32,1024]{2,1,0:T(8,128)(2,1)} %bitcast.29), calls=%async_computation.4 | async-start | bytes 2097152 | tf_op jit(solution)/shard_map/all_to_all | solution.py:325
  358.2 1.0 copy-start.7
  359.1 121.6 %all-to-all-start.7 = ((bf16[16,32,3072]{2,1,0:T(8,128)(2,1)}), bf16[16,32,3072]{2,1,0:T(8,128)(2,1)S(1)}, u32[]{:S(2)}, u32[]{:S(2)}) async-start(bf16[16,32,3072]{2,1,0:T(8,128)(2,1)} %bitcast.25), calls=%async_computation.7 | async-start | bytes 6291456 | tf_op jit(solution)/shard_map/all_to_all | solution.py:325
  367.1 4.0 collective-permute-start.9
  369.1 2.0 collective-permute-start.10
  369.8 43.8 %collective-permute-start.11 = (bf16[128,2048]{1,0:T(8,128)(2,1)S(1)}, bf16[128,2048]{1,0:T(8,128)(2,1)S(1)}, u32[]{:S(2)}, u32[]{:S(2)}) collective-permute-start(bf16[128,2048]{1,0:T(8,128)(2,1)S(1)} %get-tuple-element.61), channel_id=1, source_target_pairs={{0,6},{8,14},{16,22},{24,30},{1,7},{9,15},{17,23},{25,31}} | collective-permute-start | bytes 1572872 | tf_op jit(solution)/shard_map/ppermute | solution.py:26
  414.8 30.3 %collective-permute-start.12 = (bf16[128,2048]{1,0:T(8,128)(2,1)S(1)}, bf16[128,2048]{1,0:T(8,128)(2,1)S(1)}, u32[]{:S(2)}, u32[]{:S(2)}) collective-permute-start(bf16[128,2048]{1,0:T(8,128)(2,1)S(1)} %add_add_fusion), channel_id=1, source_target_pairs={{8,0},{10,2},{12,4},{14,6},{16,8},{18,10},{20,12},{22,14},{24,16},... | collective-permute-start | bytes 1572872 | tf_op jit(solution)/shard_map/ppermute | solution.py:26
  416.9 47.6 %collective-permute-start.17 = (bf16[256,2048]{1,0:T(8,128)(2,1)}, bf16[256,2048]{1,0:T(8,128)(2,1)}, u32[]{:S(2)}, u32[]{:S(2)}) collective-permute-start(bf16[256,2048]{1,0:T(8,128)(2,1)} %get-tuple-element.40), channel_id=1, source_target_pairs={{2,0},{4,2},{6,4},{10,8},{12,10},{14,12},{18,16},{20,18},{22,20},{... | collective-permute-start | bytes 3145736 | tf_op jit(solution)/shard_map/ppermute | solution.py:26
  419.1 59.0 %collective-permute-start.15 = (bf16[256,2048]{1,0:T(8,128)(2,1)}, bf16[256,2048]{1,0:T(8,128)(2,1)}, u32[]{:S(2)}, u32[]{:S(2)}) collective-permute-start(bf16[256,2048]{1,0:T(8,128)(2,1)} %get-tuple-element.39), channel_id=1, source_target_pairs={{2,0},{4,2},{6,4},{10,8},{12,10},{14,12},{18,16},{20,18},{22,20},{... | collective-permute-start | bytes 3145736 | tf_op jit(solution)/shard_map/ppermute | solution.py:26
  445.1 30.7 %collective-permute-start.16 = (bf16[128,2048]{1,0:T(8,128)(2,1)S(1)}, bf16[128,2048]{1,0:T(8,128)(2,1)}, u32[]{:S(2)}, u32[]{:S(2)}) collective-permute-start(bf16[128,2048]{1,0:T(8,128)(2,1)S(1)} %collective-permute-done.12), channel_id=1, source_target_pairs={{4,6},{12,14},{20,22},{28,30},{5,7},{13,15},{21,23},{29,31}} | collective-permute-start | bytes 1572872 | tf_op jit(solution)/shard_map/ppermute | solution.py:26
  446.3 31.8 %collective-permute-start.14 = (bf16[128,2048]{1,0:T(8,128)(2,1)S(1)}, bf16[128,2048]{1,0:T(8,128)(2,1)}, u32[]{:S(2)}, u32[]{:S(2)}) collective-permute-start(bf16[128,2048]{1,0:T(8,128)(2,1)S(1)} %collective-permute-done.12), channel_id=1, source_target_pairs={{2,6},{10,14},{18,22},{26,30},{3,7},{11,15},{19,23},{27,31}} | collective-permute-start | bytes 1572872 | tf_op jit(solution)/shard_map/ppermute | solution.py:26
  447.6 30.5 %collective-permute-start.13 = (bf16[128,2048]{1,0:T(8,128)(2,1)S(1)}, bf16[128,2048]{1,0:T(8,128)(2,1)}, u32[]{:S(2)}, u32[]{:S(2)}) collective-permute-start(bf16[128,2048]{1,0:T(8,128)(2,1)S(1)} %collective-permute-done.12), channel_id=1, source_target_pairs={{0,6},{8,14},{16,22},{24,30},{1,7},{9,15},{17,23},{25,31}} | collective-permute-start | bytes 1572872 | tf_op jit(solution)/shard_map/ppermute | solution.py:26
  480.8 1.8 copy-start.2
  482.5 82.6 %all-to-all-start.6 = ((bf16[16,32,3072]{2,1,0:T(8,128)(2,1)}), bf16[16,32,3072]{2,1,0:T(8,128)(2,1)}, u32[]{:S(2)}, u32[]{:S(2)}) async-start(bf16[16,32,3072]{2,1,0:T(8,128)(2,1)} %bitcast.26), calls=%async_computation.6 | async-start | bytes 6291456 | tf_op jit(solution)/shard_map/all_to_all | solution.py:325

commit v4 on v3

--- a/solution.py
+++ b/solution.py
@@ -26,7 +26,7 @@
     return lax.ppermute(block, "seq", [(a, b) for a, b in routes if 0 <= min(a, b) and max(a, b) < size])
 
 
-def next_door(pair, step):
+def next_door(pair, step, meet):
     size = lax.axis_size("seq")
     if size % GROUP or size == GROUP:
         return tuple(permuted(x, [(i, i + step) for i in range(size)]) for x in pair)
@@ -42,6 +42,7 @@
     for p in range(GROUP):
         if p != leave:
             spread = spread + permuted(pieces[p], [(b + leave, b + p) for b in bases])
+    near, spread = meet(near, spread)
     crossed = permuted(spread, [(i, i + step * GROUP) for i in range(size)])
     landed = [
         crossed if p == enter else permuted(crossed, [(b + p, b + enter) for b in bases])
@@ -339,14 +340,19 @@
         dispatch(slot_at, [clu_query, clu_key, clu_value], first, per, pool_size, True)
         for first in starts
     ]
-    before = next_door((win_key, win_value), 1)
-    sent_first[-1], before = lax.optimization_barrier((sent_first[-1], before))
+
+    def meet_second_exchange(near, spread):
+        sent_first[-1], near, spread = lax.optimization_barrier((sent_first[-1], near, spread))
+        return near, spread
+
+    before = next_door((win_key, win_value), 1, meet_second_exchange)
     held = [exchange(part) for part in sent_first]
+
+    attn_held = [owner_call(owner_fwd_kernel, rows, factor, [qkv], 1) for qkv in held]
+    attn_held[0], before = lax.optimization_barrier((attn_held[0], before))
+    attn_back = [exchange(part) for part in attn_held]
     attn_win = window_fwd(factor, win_query, win_key, win_value, before)
-    held[0], attn_win = lax.optimization_barrier((held[0], attn_win))
-
-    attn_held = [owner_call(owner_fwd_kernel, rows, factor, [qkv], 1) for qkv in held]
-    attn_back = [exchange(part) for part in attn_held]
+    attn_back[0], attn_win = lax.optimization_barrier((attn_back[0], attn_win))
     attn_clu = ()
     for first, part in zip(starts, attn_back):
         attn_clu = collect(slot_at, part, first, per, 1, attn_clu)
@@ -378,14 +384,19 @@
         factor, win_query, win_key, win_value, before, attn_win, dout_win
     )
     grad_held[0], rim_key, rim_val = lax.optimization_barrier((grad_held[0], rim_key, rim_val))
-    after_key, after_val = next_door((rim_key, rim_val), -1)
     clu_grads = ()
     sent = [
         owner_call(owner_bwd_kernel, rows, factor, [qkv, part, grad], 3)
         for qkv, part, grad in zip(held, attn_held, grad_held)
     ]
-    sent[-1], after_key, after_val = lax.optimization_barrier((sent[-1], after_key, after_val))
+
+    def meet_last_exchange(near, spread):
+        sent[-1], near, spread = lax.optimization_barrier((sent[-1], near, spread))
+        return near, spread
+
+    after_key, after_val = next_door((rim_key, rim_val), -1, meet_last_exchange)
     home = [exchange(part) for part in sent]
+    home[0], after_key, after_val = lax.optimization_barrier((home[0], after_key, after_val))
     win_dk = ((key_own + after_key) * factor).astype(BF16)
     win_dv = (val_own + after_val).astype(BF16)
     for first, part in zip(starts, home):

time: 578 us -> 618 us (1.069)
  waiting for transfers between devices: 287 us -> 309 us
  starting transfers between devices: 101 us -> 122 us
    ppermute x18, waiting for transfers between devices: 137 us -> 276 us  [permuted(): lax.ppermute(block, 'seq', [(a, b) for a, b in routes if 0 <= min(a, b) a...]
    all_to_all x8, waiting for transfers between devices: 150 us -> 33.4 us  [exchange(): lax.all_to_all(shaped, 'seq', split_axis=0, concat_axis=0, tiled=True)]
    all_to_all x8, starting transfers between devices: 64.9 us -> 82.6 us  [exchange(): lax.all_to_all(shaped, 'seq', split_axis=0, concat_axis=0, tiled=True)]
  transfers between devices with their start and end apart: 26 -> 26, of which waited for: 11 -> 12; matrix products, arithmetic and copies ran while one was open for 4% -> 4% of each run, Pallas kernels for 20% -> 19%
where the time goes in v4:
time: 618 us; the launch traced here: 613 us
  waiting for transfers between devices  309 us (50%)
  Pallas kernels  140 us (23%)
  starting transfers between devices  122 us (20%)
  other arithmetic  25.4 us (4%)
  local copies, waits for them, and re-layouts  12.5 us (2%)
    ppermute x18, waiting for transfers between devices, permuted(): lax.ppermute(block, 'seq', [(a, b) for a, b in routes if 0 <= min(a, b) a...  276 us
    all_to_all x8, starting transfers between devices, exchange(): lax.all_to_all(shaped, 'seq', split_axis=0, concat_axis=0, tiled=True)  82.6 us
    pallas_call x4, Pallas kernels, owner_call(): call(functools.partial(kernel, rows, factor), (count,), [pl.BlockSpec((po...  57.1 us
    ppermute x18, starting transfers between devices, permuted(): lax.ppermute(block, 'seq', [(a, b) for a, b in routes if 0 <= min(a, b) a...  39.5 us
    all_to_all x8, waiting for transfers between devices, exchange(): lax.all_to_all(shaped, 'seq', split_axis=0, concat_axis=0, tiled=True)  33.4 us
    pallas_call x4, Pallas kernels, dispatch(): call(functools.partial(dispatch_kernel, mark), (count,), [pl.BlockSpec((1...  26.4 us
    pallas_call x4, Pallas kernels, collect(): call(functools.partial(collect_kernel, n_out), (count,), [pl.BlockSpec((1...  26.1 us
    pallas_call x1, Pallas kernels, window_bwd(): call(functools.partial(window_bwd_kernel, factor), (wide // DH,), [here]...  16.7 us
  transfers between devices with their start and end apart: 26, of which 12 were waited for; matrix products, arithmetic and copies ran while one was open for 4% of the time, Pallas kernels for 19%

profile of v4, /device:TPU:14, one launch (start us, length us, event | category | flops | bytes accessed | tf_op | source)
XLA Modules:
  0.0 612.6 jit_solution(8571658362244221276)
XLA Ops:
  0.7 2.1 convert_reduce_fusion
  4.1 7.4 %shard_map.170 = bf16[512,3072]{1,0:T(8,128)(2,1)} custom-call(s32[16,1,256]{2,1,0:T(1,128)} %broadcast_in_dim.2.refs_0_, bf16[256,2048]{1,0:T(8,128)(2,1)} %refs_1_.3, bf16[256,2048]{1,0:T(8,128)(2,1)} %refs_2_.3, bf16[256,2048]{1,0:T(8,128)(2,1)} %refs_3_.3), custom_call_target="tpu_custom_call" | custom-call | flops 805306368 | bytes 4718592 | tf_op jit(solution)/shard_map/pallas_call | solution.py:106
  11.5 7.1 %all-to-all-start = ((bf16[16,32,3072]{2,1,0:T(8,128)(2,1)}), bf16[16,32,3072]{2,1,0:T(8,128)(2,1)S(1)}, u32[]{:S(2)}, u32[]{:S(2)}) async-start(bf16[16,32,3072]{2,1,0:T(8,128)(2,1)} %bitcast.23), calls=%async_computation | async-start | bytes 6291456 | tf_op jit(solution)/shard_map/all_to_all | solution.py:326
  18.7 1.3 collective-permute-start.1
  20.0 1.9 slice.33
  21.8 5.4 collective-permute-start.4
  27.2 1.3 collective-permute-start
  28.5 2.3 fusion.17
  30.8 4.5 collective-permute-start.2
  35.3 2.1 collective-permute-start.3
  37.4 7.3 %shard_map.172 = bf16[512,3072]{1,0:T(8,128)(2,1)} custom-call(s32[16,1,256]{2,1,0:T(1,128)} %broadcast_in_dim.2.refs_0_, bf16[256,2048]{1,0:T(8,128)(2,1)} %refs_1_.3, bf16[256,2048]{1,0:T(8,128)(2,1)} %refs_2_.3, bf16[256,2048]{1,0:T(8,128)(2,1)} %refs_3_.3), custom_call_target="tpu_custom_call" | custom-call | flops 805306368 | bytes 4718592 | tf_op jit(solution)/shard_map/pallas_call | solution.py:106
  44.7 27.9 %collective-permute-done.2 = bf16[128,2048]{1,0:T(8,128)(2,1)} collective-permute-done((bf16[128,2048]{1,0:T(8,128)(2,1)}, bf16[128,2048]{1,0:T(8,128)(2,1)}, u32[]{:S(2)}, u32[]{:S(2)}) %collective-permute-start.2) | collective-permute-done | bytes 524320 | tf_op jit(solution)/shard_map/ppermute | solution.py:26
  72.6 2.4 add_add_fusion.1
  75.0 23.6 %collective-permute-done = bf16[256,2048]{1,0:T(8,128)(2,1)} collective-permute-done((bf16[256,2048]{1,0:T(8,128)(2,1)}, bf16[256,2048]{1,0:T(8,128)(2,1)}, u32[]{:S(2)}, u32[]{:S(2)}) %collective-permute-start) | collective-permute-done | bytes 1048608 | tf_op jit(solution)/shard_map/ppermute | solution.py:26
  98.6 1.7 copy-done
  100.3 15.0 %all-to-all-start.2 = ((bf16[16,32,3072]{2,1,0:T(8,128)(2,1)}), bf16[16,32,3072]{2,1,0:T(8,128)(2,1)}, u32[]{:S(2)}, u32[]{:S(2)}) async-start(bf16[16,32,3072]{2,1,0:T(8,128)(2,1)} %bitcast.24), calls=%async_computation.2 | async-start | bytes 6291456 | tf_op jit(solution)/shard_map/all_to_all | solution.py:326
  115.3 3.4 collective-permute-start.5
  118.7 74.6 %collective-permute-done.5 = bf16[128,2048]{1,0:T(8,128)(2,1)S(1)} collective-permute-done((bf16[128,2048]{1,0:T(8,128)(2,1)}, bf16[128,2048]{1,0:T(8,128)(2,1)S(1)}, u32[]{:S(2)}, u32[]{:S(2)}) %collective-permute-start.5) | collective-permute-done | bytes 524320 | tf_op jit(solution)/shard_map/ppermute | solution.py:26
  194.0 2.8 collective-permute-start.8
  197.4 2.6 maximum_select_fusion.kp_ref
  200.0 5.6 collective-permute-done.8
  205.7 2.6 maximum_select_fusion.1.vp_ref
  208.3 13.1 %shard_map.171.attn_ref = bf16[512,1024]{1,0:T(8,128)(2,1)} custom-call(bf16[512,3072]{1,0:T(8,128)(2,1)} %bitcast.20), custom_call_target="tpu_custom_call" | custom-call | flops 805306368 | bytes 4194304 | tf_op jit(solution)/shard_map/pallas_call | solution.py:221
  221.3 18.1 %all-to-all-start.1 = ((bf16[16,32,1024]{2,1,0:T(8,128)(2,1)}), bf16[16,32,1024]{2,1,0:T(8,128)(2,1)S(1)}, u32[]{:S(2)}, u32[]{:S(2)}) async-start(bf16[16,32,1024]{2,1,0:T(8,128)(2,1)} %bitcast.28), calls=%async_computation.1 | async-start | bytes 2097152 | tf_op jit(solution)/shard_map/all_to_all | solution.py:326
  239.4 13.1 %shard_map.174.attn_ref = bf16[512,1024]{1,0:T(8,128)(2,1)} custom-call(bf16[512,3072]{1,0:T(8,128)(2,1)} %bitcast.5.qkv_ref), custom_call_target="tpu_custom_call" | custom-call | flops 805306368 | bytes 4194304 | tf_op jit(solution)/shard_map/pallas_call | solution.py:221
  252.5 11.6 %all-to-all-done.1 = bf16[16,32,1024]{2,1,0:T(8,128)(2,1)S(1)} async-done(((bf16[16,32,1024]{2,1,0:T(8,128)(2,1)}), bf16[16,32,1024]{2,1,0:T(8,128)(2,1)S(1)}, u32[]{:S(2)}, u32[]{:S(2)}) %all-to-all-start.1) | async-done | bytes 1048608 | tf_op jit(solution)/shard_map/all_to_all | solution.py:326
  264.1 5.9 all-to-all-start.3
  269.9 14.1 %shard_map.173.attn_ref = bf16[256,2048]{1,0:T(8,128)(2,1)} custom-call(bf16[256,2048]{1,0:T(8,128)(2,1)} %q_ref.3, bf16[256,2048]{1,0:T(8,128)(2,1)} %maximum_select_fusion.kp_ref, bf16[256,2048]{1,0:T(8,128)(2,1)} %k_ref.3, bf16[256,2048]{1,0:T(8,128)(2,1)} %maximum_select_fusion.1.vp_ref, bf16[256,2048]{1,0:T(8,128)(2,1)} %v_ref.3), custom_call_target="tpu_custom_call" | custom-call | flops 1073741824 | bytes 6291456 | tf_op jit(solution)/shard_map/pallas_call | solution.py:270
  284.1 6.1 %shard_map.175.refs_2_ = bf16[256,2048]{1,0:T(8,128)(2,1)} custom-call(s32[16,1,256]{2,1,0:T(1,128)} %broadcast_in_dim.2.refs_0_, bf16[512,1024]{1,0:T(8,128)(2,1)} %bitcast.31), custom_call_target="tpu_custom_call" | custom-call | flops 268435456 | bytes 1572864 | tf_op jit(solution)/shard_map/pallas_call | solution.py:131
  290.2 2.9 all-to-all-done.3
  294.1 6.1 %shard_map.176 = bf16[256,2048]{1,0:T(8,128)(2,1)} custom-call(s32[16,1,256]{2,1,0:T(1,128)} %broadcast_in_dim.2.refs_0_, bf16[512,1024]{1,0:T(8,128)(2,1)} %bitcast.29, bf16[256,2048]{1,0:T(8,128)(2,1)} %shard_map.175.refs_2_), custom_call_target="tpu_custom_call", output_to_operand_aliasing={{}: (2, {})} | custom-call | flops 268435456 | bytes 1572864 | tf_op jit(solution)/shard_map/pallas_call | solution.py:131
  300.3 2.7 fusion
  303.0 2.5 psum.7
  305.5 4.7 fusion.11
  310.2 5.8 shard_map.178
  316.0 5.9 all-to-all-start.4
  321.9 5.9 shard_map.180
  327.8 18.9 %all-to-all-done.4 = bf16[16,32,1024]{2,1,0:T(8,128)(2,1)S(1)} async-done(((bf16[16,32,1024]{2,1,0:T(8,128)(2,1)}), bf16[16,32,1024]{2,1,0:T(8,128)(2,1)S(1)}, u32[]{:S(2)}, u32[]{:S(2)}) %all-to-all-start.4) | async-done | bytes 1048608 | tf_op jit(solution)/shard_map/all_to_all | solution.py:326
  346.7 6.0 all-to-all-start.6
  352.7 16.7 %shard_map.177 = (bf16[256,2048]{1,0:T(8,128)(2,1)}, f32[256,2048]{1,0:T(8,128)}, f32[256,2048]{1,0:T(8,128)}, bf16[256,2048]{1,0:T(8,128)(2,1)}, bf16[256,2048]{1,0:T(8,128)(2,1)}) custom-call(bf16[256,2048]{1,0:T(8,128)(2,1)} %q_ref.3, bf16[256,2048]{1,0:T(8,128)(2,1)} %maximum_select_fusion.kp_ref, bf16[256,2048]{1,0:T(8,128)(2,1)} %k_ref.3, ...), custom_call_target="tpu_custom_call" | custom-call | flops 2684354560 | bytes 14680064 | tf_op jit(solution)/shard_map/pallas_call | solution.py:284
  369.4 15.5 %shard_map.179 = bf16[512,3072]{1,0:T(8,128)(2,1)} custom-call(bf16[512,3072]{1,0:T(8,128)(2,1)} %bitcast.21, bf16[512,1024]{1,0:T(8,128)(2,1)} %shard_map.171.attn_ref, bf16[512,1024]{1,0:T(8,128)(2,1)} %bitcast.34), custom_call_target="tpu_custom_call" | custom-call | flops 805306368 | bytes 8388608 | tf_op jit(solution)/shard_map/pallas_call | solution.py:221
  385.8 6.9 %all-to-all-start.5 = ((bf16[16,32,3072]{2,1,0:T(8,128)(2,1)}), bf16[16,32,3072]{2,1,0:T(8,128)(2,1)S(1)}, u32[]{:S(2)}, u32[]{:S(2)}) async-start(bf16[16,32,3072]{2,1,0:T(8,128)(2,1)} %bitcast.26), calls=%async_computation.5 | async-start | bytes 6291456 | tf_op jit(solution)/shard_map/all_to_all | solution.py:326
  392.8 3.6 collective-permute-start.10
  396.4 3.4 collective-permute-start.9
  399.8 2.3 fusion.16
  402.1 1.5 collective-permute-start.11
  403.5 1.5 collective-permute-start.12
  406.3 15.5 %shard_map.181 = bf16[512,3072]{1,0:T(8,128)(2,1)} custom-call(bf16[512,3072]{1,0:T(8,128)(2,1)} %bitcast.5.qkv_ref, bf16[512,1024]{1,0:T(8,128)(2,1)} %shard_map.174.attn_ref, bf16[512,1024]{1,0:T(8,128)(2,1)} %bitcast.33), custom_call_target="tpu_custom_call" | custom-call | flops 805306368 | bytes 8388608 | tf_op jit(solution)/shard_map/pallas_call | solution.py:221
  421.8 21.0 %collective-permute-done.13 = bf16[128,2048]{1,0:T(8,128)(2,1)} collective-permute-done((bf16[128,2048]{1,0:T(8,128)(2,1)}, bf16[128,2048]{1,0:T(8,128)(2,1)}, u32[]{:S(2)}, u32[]{:S(2)}) %collective-permute-start.13) | collective-permute-done | bytes 524320 | tf_op jit(solution)/shard_map/ppermute | solution.py:26
  442.7 2.4 add_add_fusion
  445.2 24.6 %collective-permute-done.9 = bf16[256,2048]{1,0:T(8,128)(2,1)} collective-permute-done((bf16[256,2048]{1,0:T(8,128)(2,1)}, bf16[256,2048]{1,0:T(8,128)(2,1)}, u32[]{:S(2)}, u32[]{:S(2)}) %collective-permute-start.9) | collective-permute-done | bytes 1048608 | tf_op jit(solution)/shard_map/ppermute | solution.py:26
  469.8 1.7 copy-done.2
  471.5 17.6 %all-to-all-start.7 = ((bf16[16,32,3072]{2,1,0:T(8,128)(2,1)}), bf16[16,32,3072]{2,1,0:T(8,128)(2,1)}, u32[]{:S(2)}, u32[]{:S(2)}) async-start(bf16[16,32,3072]{2,1,0:T(8,128)(2,1)} %bitcast.25), calls=%async_computation.7 | async-start | bytes 6291456 | tf_op jit(solution)/shard_map/all_to_all | solution.py:326
  489.1 2.5 collective-permute-start.14
  491.5 75.2 %collective-permute-done.14 = bf16[128,2048]{1,0:T(8,128)(2,1)S(1)} collective-permute-done((bf16[128,2048]{1,0:T(8,128)(2,1)}, bf16[128,2048]{1,0:T(8,128)(2,1)S(1)}, u32[]{:S(2)}, u32[]{:S(2)}) %collective-permute-start.14) | collective-permute-done | bytes 524320 | tf_op jit(solution)/shard_map/ppermute | solution.py:26
  566.7 1.3 collective-permute-start.17
  568.0 1.3 collective-permute-start.16
  569.3 1.3 collective-permute-start.15
  570.6 10.9 %collective-permute-done.17 = bf16[128,2048]{1,0:T(8,128)(2,1)S(1)} collective-permute-done((bf16[128,2048]{1,0:T(8,128)(2,1)S(1)}, bf16[128,2048]{1,0:T(8,128)(2,1)S(1)}, u32[]{:S(2)}, u32[]{:S(2)}) %collective-permute-start.17) | collective-permute-done | bytes 524320 | tf_op jit(solution)/shard_map/ppermute | solution.py:26
  581.9 12.1 %collective-permute-done.16 = bf16[128,2048]{1,0:T(8,128)(2,1)S(1)} collective-permute-done((bf16[128,2048]{1,0:T(8,128)(2,1)S(1)}, bf16[128,2048]{1,0:T(8,128)(2,1)S(1)}, u32[]{:S(2)}, u32[]{:S(2)}) %collective-permute-start.16) | collective-permute-done | bytes 524320 | tf_op jit(solution)/shard_map/ppermute | solution.py:26
  594.5 6.9 %shard_map.182 = (bf16[256,2048]{1,0:T(8,128)(2,1)}, bf16[256,2048]{1,0:T(8,128)(2,1)}, bf16[256,2048]{1,0:T(8,128)(2,1)}) custom-call(s32[16,1,256]{2,1,0:T(1,128)} %broadcast_in_dim.2.refs_0_, bf16[512,3072]{1,0:T(8,128)(2,1)} %bitcast.22), custom_call_target="tpu_custom_call" | custom-call | flops 805306368 | bytes 4718592 | tf_op jit(solution)/shard_map/pallas_call | solution.py:131
  601.4 3.0 add_convert_fusion
  604.4 1.3 multiply_convert_fusion
  605.7 6.9 %shard_map.183 = (bf16[256,2048]{1,0:T(8,128)(2,1)}, bf16[256,2048]{1,0:T(8,128)(2,1)}, bf16[256,2048]{1,0:T(8,128)(2,1)}) custom-call(s32[16,1,256]{2,1,0:T(1,128)} %broadcast_in_dim.2.refs_0_, bf16[512,3072]{1,0:T(8,128)(2,1)} %bitcast.19.refs_1_, ...), custom_call_target="tpu_custom_call", output_to_operand_aliasing={{0}: (2, {}), {1}: (3, {}), {2}: (4, {})} | custom-call | flops 805306368 | bytes 4718592 | tf_op jit(solution)/shard_map/pallas_call | solution.py:131
  (52 shorter events, 6.9 us)
Async XLA Ops:
  11.5 87.1 %all-to-all-start = ((bf16[16,32,3072]{2,1,0:T(8,128)(2,1)}), bf16[16,32,3072]{2,1,0:T(8,128)(2,1)S(1)}, u32[]{:S(2)}, u32[]{:S(2)}) async-start(bf16[16,32,3072]{2,1,0:T(8,128)(2,1)} %bitcast.23), calls=%async_computation | async-start | bytes 6291456 | tf_op jit(solution)/shard_map/all_to_all | solution.py:326
  18.7 79.9 %collective-permute-start.1 = (bf16[256,2048]{1,0:T(8,128)(2,1)}, bf16[256,2048]{1,0:T(8,128)(2,1)}, u32[]{:S(2)}, u32[]{:S(2)}) collective-permute-start(bf16[256,2048]{1,0:T(8,128)(2,1)} %v_ref.3), channel_id=1, source_target_pairs={{0,2},{2,4},{4,6},{8,10},{10,12},{12,14},{16,18},{18,20},{20,22},{... | collective-permute-start | bytes 3145736 | tf_op jit(solution)/shard_map/ppermute | solution.py:26
  21.8 22.9 %collective-permute-start.4 = (bf16[128,2048]{1,0:T(8,128)(2,1)}, bf16[128,2048]{1,0:T(8,128)(2,1)}, u32[]{:S(2)}, u32[]{:S(2)}) collective-permute-start(bf16[128,2048]{1,0:T(8,128)(2,1)} %slice.33), channel_id=1, source_target_pairs={{6,4},{14,12},{22,20},{30,28},{7,5},{15,13},{23,21},{31,29}} | collective-permute-start | bytes 1572872 | tf_op jit(solution)/shard_map/ppermute | solution.py:26
  27.2 71.4 %collective-permute-start = (bf16[256,2048]{1,0:T(8,128)(2,1)}, bf16[256,2048]{1,0:T(8,128)(2,1)}, u32[]{:S(2)}, u32[]{:S(2)}) collective-permute-start(bf16[256,2048]{1,0:T(8,128)(2,1)} %k_ref.3), channel_id=1, source_target_pairs={{0,2},{2,4},{4,6},{8,10},{10,12},{12,14},{16,18},{18,20},{20,22},{... | collective-permute-start | bytes 3145736 | tf_op jit(solution)/shard_map/ppermute | solution.py:26
  30.8 41.9 %collective-permute-start.2 = (bf16[128,2048]{1,0:T(8,128)(2,1)}, bf16[128,2048]{1,0:T(8,128)(2,1)}, u32[]{:S(2)}, u32[]{:S(2)}) collective-permute-start(bf16[128,2048]{1,0:T(8,128)(2,1)} %get-tuple-element.78), channel_id=1, source_target_pairs={{6,0},{14,8},{22,16},{30,24},{7,1},{15,9},{23,17},{31,25}} | collective-permute-start | bytes 1572872 | tf_op jit(solution)/shard_map/ppermute | solution.py:26
  35.3 37.4 %collective-permute-start.3 = (bf16[128,2048]{1,0:T(8,128)(2,1)}, bf16[128,2048]{1,0:T(8,128)(2,1)}, u32[]{:S(2)}, u32[]{:S(2)}) collective-permute-start(bf16[128,2048]{1,0:T(8,128)(2,1)} %get-tuple-element.79), channel_id=1, source_target_pairs={{6,2},{14,10},{22,18},{30,26},{7,3},{15,11},{23,19},{31,27}} | collective-permute-start | bytes 1572872 | tf_op jit(solution)/shard_map/ppermute | solution.py:26
  98.6 1.7 copy-start
  100.3 121.0 %all-to-all-start.2 = ((bf16[16,32,3072]{2,1,0:T(8,128)(2,1)}), bf16[16,32,3072]{2,1,0:T(8,128)(2,1)}, u32[]{:S(2)}, u32[]{:S(2)}) async-start(bf16[16,32,3072]{2,1,0:T(8,128)(2,1)} %bitcast.24), calls=%async_computation.2 | async-start | bytes 6291456 | tf_op jit(solution)/shard_map/all_to_all | solution.py:326
  115.3 78.0 %collective-permute-start.5 = (bf16[128,2048]{1,0:T(8,128)(2,1)}, bf16[128,2048]{1,0:T(8,128)(2,1)S(1)}, u32[]{:S(2)}, u32[]{:S(2)}) collective-permute-start(bf16[128,2048]{1,0:T(8,128)(2,1)} %add_add_fusion.1), channel_id=1, source_target_pairs={{0,8},{2,10},{4,12},{6,14},{8,16},{10,18},{12,20},{14,22},{16,24},... | collective-permute-start | bytes 1572872 | tf_op jit(solution)/shard_map/ppermute | solution.py:26
  193.3 4.2 collective-permute-start.6
  194.0 11.7 %collective-permute-start.8 = (bf16[128,2048]{1,0:T(8,128)(2,1)S(1)}, bf16[128,2048]{1,0:T(8,128)(2,1)S(1)}, u32[]{:S(2)}, u32[]{:S(2)}) collective-permute-start(bf16[128,2048]{1,0:T(8,128)(2,1)S(1)} %collective-permute-done.5), channel_id=1, source_target_pairs={{6,0},{14,8},{22,16},{30,24},{7,1},{15,9},{23,17},{31,25}} | collective-permute-start | bytes 1572872 | tf_op jit(solution)/shard_map/ppermute | solution.py:26
  196.7 9.0 %collective-permute-start.7 = (bf16[128,2048]{1,0:T(8,128)(2,1)S(1)}, bf16[128,2048]{1,0:T(8,128)(2,1)S(1)}, u32[]{:S(2)}, u32[]{:S(2)}) collective-permute-start(bf16[128,2048]{1,0:T(8,128)(2,1)S(1)} %collective-permute-done.5), channel_id=1, source_target_pairs={{4,0},{12,8},{20,16},{28,24},{5,1},{13,9},{21,17},{29,25}} | collective-permute-start | bytes 1572872 | tf_op jit(solution)/shard_map/ppermute | solution.py:26
  221.3 42.8 %all-to-all-start.1 = ((bf16[16,32,1024]{2,1,0:T(8,128)(2,1)}), bf16[16,32,1024]{2,1,0:T(8,128)(2,1)S(1)}, u32[]{:S(2)}, u32[]{:S(2)}) async-start(bf16[16,32,1024]{2,1,0:T(8,128)(2,1)} %bitcast.28), calls=%async_computation.1 | async-start | bytes 2097152 | tf_op jit(solution)/shard_map/all_to_all | solution.py:326
  264.1 20.0 %copy-start.6 = (bf16[16,32,1024]{2,1,0:T(8,128)(2,1)}, bf16[16,32,1024]{2,1,0:T(8,128)(2,1)S(1)}, u32[]{:S(2)}) copy-start(bf16[16,32,1024]{2,1,0:T(8,128)(2,1)S(1)} %all-to-all-done.1) | copy-start | bytes 3145732
  264.1 29.1 %all-to-all-start.3 = ((bf16[16,32,1024]{2,1,0:T(8,128)(2,1)}), bf16[16,32,1024]{2,1,0:T(8,128)(2,1)S(1)}, u32[]{:S(2)}, u32[]{:S(2)}) async-start(bf16[16,32,1024]{2,1,0:T(8,128)(2,1)} %bitcast.27), calls=%async_computation.3 | async-start | bytes 2097152 | tf_op jit(solution)/shard_map/all_to_all | solution.py:326
  290.2 10.0 %copy-start.3 = (bf16[256,2048]{1,0:T(8,128)(2,1)S(1)}, bf16[256,2048]{1,0:T(8,128)(2,1)}, u32[]{:S(2)}) copy-start(bf16[256,2048]{1,0:T(8,128)(2,1)} %shard_map.173.attn_ref) | copy-start | bytes 3145732
  290.2 10.0 %copy-start.4 = (bf16[256,2048]{1,0:T(8,128)(2,1)S(1)}, bf16[256,2048]{1,0:T(8,128)(2,1)}, u32[]{:S(2)}) copy-start(bf16[256,2048]{1,0:T(8,128)(2,1)} %param.21) | copy-start | bytes 3145732
  290.2 10.0 %copy-start.11 = (f32[2048]{0:T(1024)S(1)}, f32[2048]{0:T(1024)}, u32[]{:S(2)}) copy-start(f32[2048]{0:T(1024)} %param.18) | copy-start | bytes 24580
  290.2 10.0 %copy-start.12 = (f32[2048]{0:T(1024)S(1)}, f32[2048]{0:T(1024)}, u32[]{:S(2)}) copy-start(f32[2048]{0:T(1024)} %param.19) | copy-start | bytes 24580
  293.1 1.0 copy-start.5
  300.3 5.2 copy-start.1
  316.0 30.7 %all-to-all-start.4 = ((bf16[16,32,1024]{2,1,0:T(8,128)(2,1)}), bf16[16,32,1024]{2,1,0:T(8,128)(2,1)S(1)}, u32[]{:S(2)}, u32[]{:S(2)}) async-start(bf16[16,32,1024]{2,1,0:T(8,128)(2,1)} %bitcast.32), calls=%async_computation.4 | async-start | bytes 2097152 | tf_op jit(solution)/shard_map/all_to_all | solution.py:326
  346.7 22.7 %copy-start.8 = (bf16[16,32,1024]{2,1,0:T(8,128)(2,1)}, bf16[16,32,1024]{2,1,0:T(8,128)(2,1)S(1)}, u32[]{:S(2)}) copy-start(bf16[16,32,1024]{2,1,0:T(8,128)(2,1)S(1)} %all-to-all-done.4) | copy-start | bytes 3145732
  346.7 38.2 %all-to-all-start.6 = ((bf16[16,32,1024]{2,1,0:T(8,128)(2,1)}), bf16[16,32,1024]{2,1,0:T(8,128)(2,1)S(1)}, u32[]{:S(2)}, u32[]{:S(2)}) async-start(bf16[16,32,1024]{2,1,0:T(8,128)(2,1)} %bitcast.30), calls=%async_computation.6 | async-start | bytes 2097152 | tf_op jit(solution)/shard_map/all_to_all | solution.py:326
  384.9 1.0 copy-start.7
  385.8 83.9 %all-to-all-start.5 = ((bf16[16,32,3072]{2,1,0:T(8,128)(2,1)}), bf16[16,32,3072]{2,1,0:T(8,128)(2,1)S(1)}, u32[]{:S(2)}, u32[]{:S(2)}) async-start(bf16[16,32,3072]{2,1,0:T(8,128)(2,1)} %bitcast.26), calls=%async_computation.5 | async-start | bytes 6291456 | tf_op jit(solution)/shard_map/all_to_all | solution.py:326
  392.8 9.3 %copy-start.10 = (bf16[256,2048]{1,0:T(8,128)(2,1)S(1)}, bf16[256,2048]{1,0:T(8,128)(2,1)}, u32[]{:S(2)}) copy-start(bf16[256,2048]{1,0:T(8,128)(2,1)} %get-tuple-element.52) | copy-start | bytes 3145732
  392.8 52.4 %collective-permute-start.10 = (bf16[256,2048]{1,0:T(8,128)(2,1)}, bf16[256,2048]{1,0:T(8,128)(2,1)}, u32[]{:S(2)}, u32[]{:S(2)}) collective-permute-start(bf16[256,2048]{1,0:T(8,128)(2,1)} %get-tuple-element.53), channel_id=1, source_target_pairs={{2,0},{4,2},{6,4},{10,8},{12,10},{14,12},{18,16},{20,18},{22,20},{... | collective-permute-start | bytes 3145736 | tf_op jit(solution)/shard_map/ppermute | solution.py:26
  396.4 73.4 %collective-permute-start.9 = (bf16[256,2048]{1,0:T(8,128)(2,1)}, bf16[256,2048]{1,0:T(8,128)(2,1)}, u32[]{:S(2)}, u32[]{:S(2)}) collective-permute-start(bf16[256,2048]{1,0:T(8,128)(2,1)} %get-tuple-element.52), channel_id=1, source_target_pairs={{2,0},{4,2},{6,4},{10,8},{12,10},{14,12},{18,16},{20,18},{22,20},{... | collective-permute-start | bytes 3145736 | tf_op jit(solution)/shard_map/ppermute | solution.py:26
  402.1 19.7 %collective-permute-start.11 = (bf16[128,2048]{1,0:T(8,128)(2,1)S(1)}, bf16[128,2048]{1,0:T(8,128)(2,1)}, u32[]{:S(2)}, u32[]{:S(2)}) collective-permute-start(bf16[128,2048]{1,0:T(8,128)(2,1)S(1)} %slice.37), channel_id=1, source_target_pairs={{0,2},{8,10},{16,18},{24,26},{1,3},{9,11},{17,19},{25,27}} | collective-permute-start | bytes 1572872 | tf_op jit(solution)/shard_map/ppermute | solution.py:26
  403.5 18.3 %collective-permute-start.12 = (bf16[128,2048]{1,0:T(8,128)(2,1)}, bf16[128,2048]{1,0:T(8,128)(2,1)}, u32[]{:S(2)}, u32[]{:S(2)}) collective-permute-start(bf16[128,2048]{1,0:T(8,128)(2,1)} %get-tuple-element.76), channel_id=1, source_target_pairs={{0,4},{8,12},{16,20},{24,28},{1,5},{9,13},{17,21},{25,29}} | collective-permute-start | bytes 1572872 | tf_op jit(solution)/shard_map/ppermute | solution.py:26
  405.0 37.7 %collective-permute-start.13 = (bf16[128,2048]{1,0:T(8,128)(2,1)}, bf16[128,2048]{1,0:T(8,128)(2,1)}, u32[]{:S(2)}, u32[]{:S(2)}) collective-permute-start(bf16[128,2048]{1,0:T(8,128)(2,1)} %get-tuple-element.77), channel_id=1, source_target_pairs={{0,6},{8,14},{16,22},{24,30},{1,7},{9,15},{17,23},{25,31}} | collective-permute-start | bytes 1572872 | tf_op jit(solution)/shard_map/ppermute | solution.py:26
  469.8 1.7 copy-start.2
  471.5 134.2 %all-to-all-start.7 = ((bf16[16,32,3072]{2,1,0:T(8,128)(2,1)}), bf16[16,32,3072]{2,1,0:T(8,128)(2,1)}, u32[]{:S(2)}, u32[]{:S(2)}) async-start(bf16[16,32,3072]{2,1,0:T(8,128)(2,1)} %bitcast.25), calls=%async_computation.7 | async-start | bytes 6291456 | tf_op jit(solution)/shard_map/all_to_all | solution.py:326
  489.1 77.7 %collective-permute-start.14 = (bf16[128,2048]{1,0:T(8,128)(2,1)}, bf16[128,2048]{1,0:T(8,128)(2,1)S(1)}, u32[]{:S(2)}, u32[]{:S(2)}) collective-permute-start(bf16[128,2048]{1,0:T(8,128)(2,1)} %add_add_fusion), channel_id=1, source_target_pairs={{8,0},{10,2},{12,4},{14,6},{16,8},{18,10},{20,12},{22,14},{24,16},... | collective-permute-start | bytes 1572872 | tf_op jit(solution)/shard_map/ppermute | solution.py:26
  566.7 14.8 %collective-permute-start.17 = (bf16[128,2048]{1,0:T(8,128)(2,1)S(1)}, bf16[128,2048]{1,0:T(8,128)(2,1)S(1)}, u32[]{:S(2)}, u32[]{:S(2)}) collective-permute-start(bf16[128,2048]{1,0:T(8,128)(2,1)S(1)} %collective-permute-done.14), channel_id=1, source_target_pairs={{4,6},{12,14},{20,22},{28,30},{5,7},{13,15},{21,23},{29,31}} | collective-permute-start | bytes 1572872 | tf_op jit(solution)/shard_map/ppermute | solution.py:26
  568.0 26.0 %collective-permute-start.16 = (bf16[128,2048]{1,0:T(8,128)(2,1)S(1)}, bf16[128,2048]{1,0:T(8,128)(2,1)S(1)}, u32[]{:S(2)}, u32[]{:S(2)}) collective-permute-start(bf16[128,2048]{1,0:T(8,128)(2,1)S(1)} %collective-permute-done.14), channel_id=1, source_target_pairs={{2,6},{10,14},{18,22},{26,30},{3,7},{11,15},{19,23},{27,31}} | collective-permute-start | bytes 1572872 | tf_op jit(solution)/shard_map/ppermute | solution.py:26
  569.3 24.7 %collective-permute-start.15 = (bf16[128,2048]{1,0:T(8,128)(2,1)S(1)}, bf16[128,2048]{1,0:T(8,128)(2,1)S(1)}, u32[]{:S(2)}, u32[]{:S(2)}) collective-permute-start(bf16[128,2048]{1,0:T(8,128)(2,1)S(1)} %collective-permute-done.14), channel_id=1, source_target_pairs={{0,6},{8,14},{16,22},{24,30},{1,7},{9,15},{17,23},{25,31}} | collective-permute-start | bytes 1572872 | tf_op jit(solution)/shard_map/ppermute | solution.py:26
  601.4 3.0 copy-start.9
